TPU v7x, 32 devices: a whole 2x2x4 slice. The times are simulated.
32 devices in a mesh: rep: 8 (over z, core), shard: 4 (over y, x).
Axes of the slice: x: 2, y: 2, z: 4, core: 2. Of those that a mesh axis runs over, the one named last changes fastest.
Arguments:
- tokens: bfloat16 [16384, 1600], P(('rep', 'shard')), may hold values from -6 to 6
- cotangent: bfloat16 [16384, 1600], P(('rep', 'shard')), may hold values from -6 to 6
- doc_start: int32 [16384], P(('rep', 'shard')), may hold values from 0 to 16383, as said below
- query_weight: bfloat16 [1600, 1600], P('shard'), may hold values from -0.15625 to 0.15625
- key_weight: bfloat16 [1600, 320], P('shard'), may hold values from -0.15625 to 0.15625
- value_weight: bfloat16 [1600, 320], P('shard'), may hold values from -0.15625 to 0.15625
- inner_weight: bfloat16 [1600, 6400], P('shard'), may hold values from -0.15625 to 0.15625
- select_weight: bfloat16 [1600, 32], P('shard'), may hold values from -0.15625 to 0.15625
- step_weight: bfloat16 [1600, 50], P('shard'), may hold values from -0.15625 to 0.15625
- mamba_out: bfloat16 [3200, 1600], P('shard'), may hold values from -0.109375 to 0.109375
- mixer_out: bfloat16 [1600, 1600], P('shard'), may hold values from -0.15625 to 0.15625
- gate_weight: bfloat16 [1600, 5504], P(None, 'shard'), may hold values from -0.15625 to 0.15625
- up_weight: bfloat16 [1600, 5504], P(None, 'shard'), may hold values from -0.15625 to 0.15625
- down_weight: bfloat16 [5504, 1600], P('shard'), may hold values from -0.078125 to 0.078125
- attention_gain: float32 [1600], replicated, may hold values from 0.4 to 1.6
- attention_scale: float32 [1600], replicated, may hold values from 0.4 to 1.6
- mamba_scale: float32 [1600], replicated, may hold values from 0.4 to 1.6
- feed_gain: float32 [1600], replicated, may hold values from 0.4 to 1.6
- decay_rate: float32 [50], replicated, may hold values from 4.8828126e-05 to 0.0390625
Outputs:
- output: bfloat16 [16384, 1600], P(('rep', 'shard'))
- token_gradient: bfloat16 [16384, 1600], P(('rep', 'shard'))
- query_gradient: float32 [1600, 1600], P('shard')
- key_gradient: float32 [1600, 320], P('shard')
- value_gradient: float32 [1600, 320], P('shard')
- inner_gradient: float32 [1600, 6400], P('shard')
- select_gradient: float32 [1600, 32], P('shard')
- step_gradient: float32 [1600, 50], P('shard')
- mamba_out_gradient: float32 [3200, 1600], P('shard')
- mixer_out_gradient: float32 [1600, 1600], P('shard')
- gate_gradient: float32 [1600, 5504], P(None, 'shard')
- up_gradient: float32 [1600, 5504], P(None, 'shard')
- down_gradient: float32 [5504, 1600], P('shard')
- attention_gain_gradient: float32 [1600], replicated
- attention_scale_gradient: float32 [1600], replicated
- mamba_scale_gradient: float32 [1600], replicated
- feed_gain_gradient: float32 [1600], replicated
- decay_rate_gradient: float32 [50], replicated
Inputs may be any that keep to these rules, and one draw needn't show every extreme that they name: `doc_start`: each aligned run of 2048 tokens holds exactly three documents, each a run of equal values naming its first position; the first two hold 204 to 511 tokens each.
All inputs are finite; a program needn't handle non-finite values.
Results may differ from a plain program's by a relative error of at most 0.025.
The roundings to bfloat16 on the way count: a program that leaves them out, or rounds other values in their place, can miss the bound.
Values may be sent and summed in bfloat16 or wider, within the bound.
No kernel may reach another device: no remote copies, remote signals or barrier semaphores. Data moves between devices by JAX's collectives and lax.ppermute only.
A program may use at most 704 MiB of HBM per device.

v0:
```python
import jax
import jax.numpy as jnp
from jax import lax
from jax.sharding import PartitionSpec as P

HEADS = 25
KV_HEADS = 5
HEAD_DIM = 64
INNER = 3200
STATE = 16
WINDOW = 1024
MAMBA_DIM = 64
MAMBA_HEADS = 50


EPSILON = 1e-05
HIGHEST = lax.Precision.HIGHEST


def shifted(block, axis, distance):
    devices = range(lax.axis_size(axis))
    route = [(i - distance, i) for i in devices if i - distance in devices]
    return lax.ppermute(block, axis, route)


def entering(array, axis, combine, identity):
    length, here = (lax.axis_size(axis), lax.axis_index(axis))
    everything = jax.tree.map(lambda part: lax.all_gather(part, axis), array)
    start = jax.tree.map(
        lambda part, zero: jnp.broadcast_to(jnp.asarray(zero, part.dtype), part.shape),
        array,
        identity,
    )

    def hop(k, before):
        reached = k < here
        new = combine(before, jax.tree.map(lambda part: part[k], everything))
        return jax.tree.map(lambda a, b: jnp.where(reached, a, b), new, before)

    return lax.fori_loop(0, length, hop, start)


def entering_2(array, axis, join, neutral):
    count = lax.axis_size(axis)
    place = lax.axis_index(axis)
    ahead = count - 1 - place
    gathered = jax.tree.map(
        lambda a, kind: lax.all_gather(a.astype(kind), axis), array, (jnp.bfloat16, jnp.bfloat16)
    )
    state = jax.tree.map(lambda a, e: jnp.zeros_like(a) + jnp.asarray(e, a.dtype), array, neutral)

    def one(hop, state):
        source = count - 1 - hop
        return join(
            state,
            jax.tree.map(
                lambda a, own: lax.dynamic_index_in_dim(a, source, 0, False).astype(own.dtype),
                gathered,
                array,
            ),
        )

    return lax.fori_loop(0, ahead, one, state)


def project(left, right):
    return jnp.dot(left, right, preferred_element_type=jnp.float32)


def left_product(left, right):
    return lax.dot_general(
        left, right, (((0,), (0,)), ((), ())), preferred_element_type=jnp.float32
    )


def right_product(left, right):
    return lax.dot_general(
        left, right, (((1,), (1,)), ((), ())), preferred_element_type=jnp.float32
    )


def inverse_rms(values):
    return lax.rsqrt(jnp.mean(values * values, axis=-1, keepdims=True) + EPSILON)


def rms_back(incoming, normed, factor):
    return factor * (incoming - normed * jnp.mean(incoming * normed, axis=-1, keepdims=True))


def silu_slope(values):
    sigma = jax.nn.sigmoid(values)
    return sigma * (1.0 + values * (1.0 - sigma))


def compose(earlier, later):
    return (earlier[0] * later[0], later[0][:, None, None] * earlier[1] + later[1])


def body(
    tokens,
    cotangent,
    doc_start,
    query_weight,
    key_weight,
    value_weight,
    inner_weight,
    select_weight,
    step_weight,
    mamba_out,
    mixer_out,
    gate_weight,
    up_weight,
    down_weight,
    attention_gain,
    attention_scale,
    mamba_scale,
    feed_gain,
    decay_rate,
):
    count = tokens.shape[0]
    begin = lax.axis_index(("rep", "shard")) * count
    place = begin + jnp.arange(count, dtype=jnp.int32)
    blocks = (WINDOW + count - 1) // count
    groups = HEADS // KV_HEADS
    factor = HEAD_DIM ** (-0.5)
    (
        query_full,
        key_full,
        value_full,
        inner_full,
        select_full,
        step_full,
        mamba_full,
        mixer_full,
        gate_full,
        up_full,
        down_full,
    ) = (
        lax.all_gather(query_weight, "shard", axis=0, tiled=True),
        lax.all_gather(key_weight, "shard", axis=0, tiled=True),
        lax.all_gather(value_weight, "shard", axis=0, tiled=True),
        lax.all_gather(inner_weight, "shard", axis=0, tiled=True),
        lax.all_gather(select_weight, "shard", axis=0, tiled=True),
        lax.all_gather(step_weight, "shard", axis=0, tiled=True),
        lax.all_gather(mamba_out, "shard", axis=0, tiled=True),
        lax.all_gather(mixer_out, "shard", axis=0, tiled=True),
        lax.all_gather(gate_weight, "shard", axis=1, tiled=True),
        lax.all_gather(up_weight, "shard", axis=1, tiled=True),
        lax.all_gather(down_weight, "shard", axis=0, tiled=True),
    )
    inputs = tokens.astype(jnp.float32)
    scale_one = inverse_rms(inputs)
    unit_one = inputs * scale_one
    normed = (unit_one * attention_gain).astype(jnp.bfloat16)
    query = project(normed, query_full).astype(jnp.bfloat16)
    keys = project(normed, key_full).astype(jnp.bfloat16)
    values = project(normed, value_full).astype(jnp.bfloat16)
    moving = jnp.stack([keys, values])
    pairs = [moving]
    for hop in range(blocks):
        moving = shifted(moving, "shard", 1)
        pairs.insert(0, moving)
    window_pairs = jnp.concatenate(pairs, 1)
    span = (blocks + 1) * count
    all_keys = window_pairs[0].reshape(span, KV_HEADS, HEAD_DIM)
    all_values = window_pairs[1].reshape(span, KV_HEADS, HEAD_DIM)
    key_place = begin - blocks * count + jnp.arange(span, dtype=jnp.int32)
    allowed = (
        (key_place[None, :] <= place[:, None])
        & (key_place[None, :] > place[:, None] - WINDOW)
        & (key_place[None, :] >= doc_start[:, None])
    )
    query_heads = query.reshape(count, KV_HEADS, groups, HEAD_DIM)
    raw = jnp.einsum("tkgd,skd->kgts", query_heads, all_keys, preferred_element_type=jnp.float32)
    scores = jnp.where(allowed, raw * factor, -1e30)
    peak = jnp.max(scores, axis=-1, keepdims=True)
    logsum = peak + jnp.log(jnp.sum(jnp.exp(scores - peak), axis=-1, keepdims=True))
    weights_low = jnp.exp(scores - logsum).astype(jnp.bfloat16)
    attended = jnp.einsum(
        "kgts,skd->tkgd", weights_low, all_values, preferred_element_type=jnp.float32
    ).reshape(count, HEADS * HEAD_DIM)
    inner = project(normed, inner_full)
    signal = inner[:, :INNER]
    switch = inner[:, INNER:]
    select = project(normed, select_full)
    writer = select[:, :STATE].astype(jnp.bfloat16)
    reader = select[:, STATE:].astype(jnp.bfloat16)
    step_raw = project(normed, step_full)
    step = jax.nn.softplus(step_raw)
    heads_in = signal.reshape(count, MAMBA_HEADS, MAMBA_DIM)
    drive = (heads_in * step[:, :, None]).astype(jnp.bfloat16)
    rate = -step * decay_rate[None, :]
    cumul = jnp.cumsum(rate, axis=0)
    valid = (place[None, :] <= place[:, None]) & (place[None, :] >= doc_start[:, None])
    spread = cumul.T[:, :, None] - cumul.T[:, None, :]
    decay = jnp.where(valid[None], jnp.exp(jnp.where(valid[None], spread, 0.0)), 0.0)
    gram = right_product(reader, writer)
    mixing = (gram[None] * decay).astype(jnp.bfloat16)
    intra = jnp.einsum("hts,shd->thd", mixing, drive, preferred_element_type=jnp.float32)
    enter = jnp.exp(cumul) * (doc_start < begin)[:, None]
    tail = jnp.exp(cumul[-1][None, :] - cumul) * (place >= doc_start[-1])[:, None]
    carry = jnp.exp(cumul[-1]) * (doc_start[-1] < begin)
    reader_wide = reader.astype(jnp.float32)
    writer_wide = writer.astype(jnp.float32)
    drive_wide = drive.astype(jnp.float32)
    local = jnp.einsum("sh,shd,sn->hdn", tail, drive_wide, writer_wide, precision=HIGHEST)
    prefix = entering(
        (carry, local), "shard", compose, (jnp.ones_like(carry), jnp.zeros_like(local))
    )
    state_in = prefix[1]
    through = jnp.einsum("tn,hdn->thd", reader_wide, state_in, precision=HIGHEST)
    mixed_flat = (intra + enter[:, :, None] * through).reshape(count, INNER)
    gated = (mixed_flat * jax.nn.silu(switch)).astype(jnp.bfloat16)
    mamba_y = project(gated, mamba_full)
    scale_att = inverse_rms(attended)
    unit_att = attended * scale_att
    scale_mam = inverse_rms(mamba_y)
    unit_mam = mamba_y * scale_mam
    blend = (0.5 * (attention_scale * unit_att + mamba_scale * unit_mam)).astype(jnp.bfloat16)
    middle = inputs + project(blend, mixer_full)
    scale_two = inverse_rms(middle)
    unit_two = middle * scale_two
    feed_in = (unit_two * feed_gain).astype(jnp.bfloat16)
    gate = project(feed_in, gate_full)
    up = project(feed_in, up_full)
    active = (jax.nn.silu(gate) * up).astype(jnp.bfloat16)
    partial_value = project(active, down_full)
    output = (middle + partial_value).astype(jnp.bfloat16)
    upstream = cotangent.astype(jnp.float32)
    down_part = left_product(active, cotangent)
    d_active = right_product(cotangent, down_full)
    d_gate = (d_active * up * silu_slope(gate)).astype(jnp.bfloat16)
    d_up = (d_active * jax.nn.silu(gate)).astype(jnp.bfloat16)
    gate_part = left_product(feed_in, d_gate)
    up_part = left_product(feed_in, d_up)
    feed_back = right_product(d_gate, gate_full) + right_product(d_up, up_full)
    gate_owned, up_owned, down_owned = (
        lax.psum_scatter(
            gate_part.astype(jnp.bfloat16), "shard", scatter_dimension=1, tiled=True
        ).astype(jnp.float32),
        lax.psum_scatter(
            up_part.astype(jnp.bfloat16), "shard", scatter_dimension=1, tiled=True
        ).astype(jnp.float32),
        lax.psum_scatter(
            down_part.astype(jnp.bfloat16), "shard", scatter_dimension=0, tiled=True
        ).astype(jnp.float32),
    )
    feed_gain_part = jnp.sum(feed_back * unit_two, axis=0)
    d_middle = upstream + rms_back(feed_back * feed_gain, unit_two, scale_two)
    d_branch = d_middle.astype(jnp.bfloat16)
    d_blend = right_product(d_branch, mixer_full)
    attention_scale_part = jnp.sum(0.5 * d_blend * unit_att, axis=0)
    mamba_scale_part = jnp.sum(0.5 * d_blend * unit_mam, axis=0)
    d_attended = rms_back(0.5 * d_blend * attention_scale, unit_att, scale_att).astype(jnp.bfloat16)
    d_mamba = rms_back(0.5 * d_blend * mamba_scale, unit_mam, scale_mam).astype(jnp.bfloat16)
    d_gated = right_product(d_mamba, mamba_full)
    d_mixed = (
        (d_gated * jax.nn.silu(switch)).astype(jnp.bfloat16).reshape(count, MAMBA_HEADS, MAMBA_DIM)
    )
    d_switch = (d_gated * mixed_flat * silu_slope(switch)).astype(jnp.bfloat16)
    d_mix = (
        jnp.einsum("thd,shd->hts", d_mixed, drive, preferred_element_type=jnp.float32)
        .astype(jnp.bfloat16)
        .astype(jnp.float32)
    )
    d_drive = jnp.einsum("hts,thd->shd", mixing, d_mixed, preferred_element_type=jnp.float32)
    d_gram = jnp.sum(d_mix * decay, axis=0).astype(jnp.bfloat16)
    d_decay = d_mix * gram[None]
    d_mixed_wide = d_mixed.astype(jnp.float32)
    d_enter = jnp.sum(d_mixed_wide * through, axis=-1)
    d_through = d_mixed_wide * enter[:, :, None]
    d_reader_state = jnp.einsum("thd,hdn->tn", d_through, state_in, precision=HIGHEST)
    state_grad = jnp.einsum("thd,tn->hdn", d_through, reader_wide, precision=HIGHEST)
    later = entering_2(
        (carry, state_grad), "shard", compose, (jnp.ones_like(carry), jnp.zeros_like(state_grad))
    )
    d_out = later[1]
    d_carry = jnp.sum(d_out * state_in, axis=(1, 2))
    d_tail = jnp.einsum("hdn,shd,sn->sh", d_out, drive_wide, writer_wide, precision=HIGHEST)
    d_drive = d_drive + tail[:, :, None] * jnp.einsum(
        "hdn,sn->shd", d_out, writer_wide, precision=HIGHEST
    )
    d_writer_state = jnp.einsum("sh,shd,hdn->sn", tail, drive_wide, d_out, precision=HIGHEST)
    d_spread = d_decay * decay
    d_cumul = (jnp.sum(d_spread, axis=2) - jnp.sum(d_spread, axis=1)).T
    tail_term = d_tail * tail
    d_cumul = d_cumul + d_enter * enter - tail_term
    d_cumul = d_cumul.at[-1].add(jnp.sum(tail_term, axis=0) + d_carry * carry)
    d_rate = jnp.flip(jnp.cumsum(jnp.flip(d_cumul, 0), axis=0), 0)
    decay_rate_part = -jnp.sum(d_rate * step, axis=0)
    d_drive_low = d_drive.astype(jnp.bfloat16).astype(jnp.float32)
    d_step = -d_rate * decay_rate[None, :] + jnp.sum(d_drive_low * heads_in, axis=-1)
    d_signal = (d_drive_low * step[:, :, None]).reshape(count, INNER).astype(jnp.bfloat16)
    d_step_raw = (d_step * jax.nn.sigmoid(step_raw)).astype(jnp.bfloat16)
    d_reader = (project(d_gram, writer) + d_reader_state).astype(jnp.bfloat16)
    d_writer = (left_product(d_gram, reader) + d_writer_state).astype(jnp.bfloat16)
    d_select = jnp.concatenate([d_writer, d_reader], axis=1)
    d_inner = jnp.concatenate([d_signal, d_switch], axis=1)
    d_heads = d_attended.reshape(count, KV_HEADS, groups, HEAD_DIM)
    raw_again = jnp.einsum(
        "tkgd,skd->kgts", query_heads, all_keys, preferred_element_type=jnp.float32
    )
    probs = jnp.exp(jnp.where(allowed, raw_again * factor, -1e30) - logsum)
    probs_low = probs.astype(jnp.bfloat16)
    d_probs = jnp.einsum("tkgd,skd->kgts", d_heads, all_values, preferred_element_type=jnp.float32)
    d_scores = (probs * (d_probs - jnp.sum(probs * d_probs, axis=-1, keepdims=True))).astype(
        jnp.bfloat16
    )
    d_query = (
        (
            jnp.einsum("kgts,skd->tkgd", d_scores, all_keys, preferred_element_type=jnp.float32)
            * factor
        )
        .astype(jnp.bfloat16)
        .reshape(count, HEADS * HEAD_DIM)
    )
    d_keys_all = (
        jnp.einsum("kgts,tkgd->skd", d_scores, query_heads, preferred_element_type=jnp.float32)
        * factor
    )
    d_values_all = jnp.einsum(
        "kgts,tkgd->skd", probs_low, d_heads, preferred_element_type=jnp.float32
    )
    halo_grads = jnp.stack([d_keys_all, d_values_all]).reshape(
        2, blocks + 1, count, KV_HEADS * HEAD_DIM
    )
    incoming = jnp.zeros((2, count, KV_HEADS * HEAD_DIM), jnp.float32)
    for hop in range(blocks):
        incoming = shifted(
            (incoming + halo_grads[:, hop]).astype(jnp.bfloat16), "shard", -1
        ).astype(jnp.float32)
    own_grads = (halo_grads[:, blocks] + incoming).astype(jnp.bfloat16)
    d_keys = own_grads[0]
    d_values = own_grads[1]
    d_normed = (
        right_product(d_query, query_full)
        + right_product(d_keys, key_full)
        + right_product(d_values, value_full)
    )
    d_normed = (
        d_normed
        + right_product(d_inner, inner_full)
        + right_product(d_select, select_full)
        + right_product(d_step_raw, step_full)
    )
    attention_gain_part = jnp.sum(d_normed * unit_one, axis=0)
    token_gradient = (d_middle + rms_back(d_normed * attention_gain, unit_one, scale_one)).astype(
        jnp.bfloat16
    )
    query_part = left_product(normed, d_query)
    key_part = left_product(normed, d_keys)
    value_part = left_product(normed, d_values)
    inner_part = left_product(normed, d_inner)
    select_part = left_product(normed, d_select)
    step_part = left_product(normed, d_step_raw)
    mamba_part = left_product(gated, d_mamba)
    mixer_part = left_product(blend, d_branch)
    (
        query_owned,
        key_owned,
        value_owned,
        inner_owned,
        select_owned,
        step_owned,
        mamba_owned,
        mixer_owned,
    ) = (
        lax.psum_scatter(
            query_part.astype(jnp.bfloat16), "shard", scatter_dimension=0, tiled=True
        ).astype(jnp.float32),
        lax.psum_scatter(
            key_part.astype(jnp.bfloat16), "shard", scatter_dimension=0, tiled=True
        ).astype(jnp.float32),
        lax.psum_scatter(
            value_part.astype(jnp.bfloat16), "shard", scatter_dimension=0, tiled=True
        ).astype(jnp.float32),
        lax.psum_scatter(
            inner_part.astype(jnp.bfloat16), "shard", scatter_dimension=0, tiled=True
        ).astype(jnp.float32),
        lax.psum_scatter(
            select_part.astype(jnp.bfloat16), "shard", scatter_dimension=0, tiled=True
        ).astype(jnp.float32),
        lax.psum_scatter(
            step_part.astype(jnp.bfloat16), "shard", scatter_dimension=0, tiled=True
        ).astype(jnp.float32),
        lax.psum_scatter(
            mamba_part.astype(jnp.bfloat16), "shard", scatter_dimension=0, tiled=True
        ).astype(jnp.float32),
        lax.psum_scatter(
            mixer_part.astype(jnp.bfloat16), "shard", scatter_dimension=0, tiled=True
        ).astype(jnp.float32),
    )
    summed = (
        lax.psum(query_owned.astype(jnp.bfloat16), "rep").astype(jnp.float32),
        lax.psum(key_owned.astype(jnp.bfloat16), "rep").astype(jnp.float32),
        lax.psum(value_owned.astype(jnp.bfloat16), "rep").astype(jnp.float32),
        lax.psum(inner_owned.astype(jnp.bfloat16), "rep").astype(jnp.float32),
        lax.psum(select_owned.astype(jnp.bfloat16), "rep").astype(jnp.float32),
        lax.psum(step_owned.astype(jnp.bfloat16), "rep").astype(jnp.float32),
        lax.psum(mamba_owned.astype(jnp.bfloat16), "rep").astype(jnp.float32),
        lax.psum(mixer_owned.astype(jnp.bfloat16), "rep").astype(jnp.float32),
        lax.psum(gate_owned.astype(jnp.bfloat16), "rep").astype(jnp.float32),
        lax.psum(up_owned.astype(jnp.bfloat16), "rep").astype(jnp.float32),
        lax.psum(down_owned.astype(jnp.bfloat16), "rep").astype(jnp.float32),
    )
    small = lax.psum(
        (
            attention_gain_part,
            attention_scale_part,
            mamba_scale_part,
            feed_gain_part,
            decay_rate_part,
        ),
        ("rep", "shard"),
    )
    return (
        output,
        token_gradient,
        summed[0],
        summed[1],
        summed[2],
        summed[3],
        summed[4],
        summed[5],
        summed[6],
        summed[7],
        summed[8],
        summed[9],
        summed[10],
        small[0],
        small[1],
        small[2],
        small[3],
        small[4],
    )


def solution(mesh):
    placed = (
        P(("rep", "shard"), None),
        P(("rep", "shard"), None),
        P(("rep", "shard")),
        P("shard", None),
        P("shard", None),
        P("shard", None),
        P("shard", None),
        P("shard", None),
        P("shard", None),
        P("shard", None),
        P("shard", None),
        P(None, "shard"),
        P(None, "shard"),
        P("shard", None),
        P(),
        P(),
        P(),
        P(),
        P(),
    )
    return jax.shard_map(
        body,
        mesh=mesh,
        in_specs=placed,
        out_specs=(
            P(("rep", "shard"), None),
            P(("rep", "shard"), None),
            P("shard", None),
            P("shard", None),
            P("shard", None),
            P("shard", None),
            P("shard", None),
            P("shard", None),
            P("shard", None),
            P("shard", None),
            P(None, "shard"),
            P(None, "shard"),
            P("shard", None),
            P(),
            P(),
            P(),
            P(),
            P(),
        ),
        check_vma=False,
    )
```

profile of v0, /device:TPU:1, one launch (start us, length us, event | category | flops | bytes accessed | tf_op | source)
XLA Modules:
  0.0 3338.2 jit_solution(2773541168964952200)
XLA Ops:
  11.2 18.4 all_gather.53
  29.7 19.7 all_gather.54
  59.2 31.4 all-gather.3
  90.8 8.1 all-gather.2
  109.8 19.3 all-gather.8
  129.7 8.1 all-gather.4
  141.6 6.5 convolution_convert_fusion.8
  148.1 29.0 fusion.9
  177.1 28.1 exponential_reduce_fusion
  205.2 31.2 fusion.35
  236.5 42.7 %all-gather.29.cloned.1.call-done = bf16[4,1376,1600]{1,2,0:T(8,128)(2,1)} async-done(((bf16[1,1376,1600]{1,2,0:T(8,128)(2,1)}), bf16[4,1376,1600]{1,2,0:T(8,128)(2,1)}) %all-gather.29.cloned.1.call-update) | async-done | bytes 17612816 | tf_op jit(solution)/shard_map/all_gather | solution.py:149
  279.3 24.3 copy.111
  303.6 146.5 %all-gather.27.cloned.1.call-done = bf16[4,1376,1600]{1,2,0:T(8,128)(2,1)} async-done(((bf16[1,1376,1600]{1,2,0:T(8,128)(2,1)}), bf16[4,1376,1600]{1,2,0:T(8,128)(2,1)}) %all-gather.27.cloned.1.call-update) | async-done | bytes 17612816 | tf_op jit(solution)/shard_map/all_gather | solution.py:148
  450.1 24.4 copy.110
  474.5 146.3 %all-gather.25.cloned.1.call-done = bf16[4,1376,1600]{1,2,0:T(8,128)(2,1)} async-done(((bf16[1,1376,1600]{1,2,0:T(8,128)(2,1)}), bf16[4,1376,1600]{1,2,0:T(8,128)(2,1)}) %all-gather.25.cloned.1.call-update) | async-done | bytes 17612816 | tf_op jit(solution)/shard_map/all_gather | solution.py:147
  620.8 24.5 copy.109
  645.3 166.4 %all-gather.19.cloned.1.call-done = bf16[1600,6400]{1,0:T(8,128)(2,1)} async-done(((bf16[400,6400]{1,0:T(8,128)(2,1)}), bf16[1600,6400]{1,0:T(8,128)(2,1)}) %all-gather.19.cloned.1.call-update) | async-done | bytes 20480016 | tf_op jit(solution)/shard_map/all_gather | solution.py:142
  811.7 15.7 fusion.100
  835.3 8.1 copy.103
  850.1 24.0 all-gather
  874.1 10.6 while.30
  888.7 16.5 bitcast_add_fusion.2
  905.3 8.1 copy.108
  919.2 8.2 all-gather.21.cloned.1.call-done
  927.4 9.5 multiply_reduce_fusion.7
  941.0 50.2 %all-gather.23.cloned.1.call-done = bf16[1600,1600]{1,0:T(8,128)(2,1)} async-done(((bf16[400,1600]{1,0:T(8,128)(2,1)}), bf16[1600,1600]{1,0:T(8,128)(2,1)}) %all-gather.23.cloned.1.call-update) | async-done | bytes 5120016 | tf_op jit(solution)/shard_map/all_gather | solution.py:146
  999.2 17.6 fusion.102
  1016.9 17.3 fusion.101
  1034.2 25.7 multiply_convert_fusion.3
  1059.9 16.5 fusion.103
  1076.4 19.8 multiply_reduce_fusion
  1100.6 7.9 multiply_reduce_fusion.1
  1110.8 15.8 multiply_convert_fusion.6
  1144.6 10.2 all-gather.1
  1169.7 32.8 fusion.7
  1207.3 15.1 convolution_convert_fusion.2
  1222.4 12.4 convolution_convert_fusion.3
  1249.5 20.5 fusion.16
  1272.7 15.1 convolution_convert_fusion.1
  1290.7 32.3 convolution_bitcast_fusion
  1327.6 55.4 %fusion.1 = (f32[5,5,512]{2,1,0:T(8,128)}, f32[5,1536,512,5]{2,1,3,0:T(8,128)}) fusion(f32[5,1536,512,5]{2,1,3,0:T(8,128)} %get-tuple-element.310, f32[5,5,512]{2,1,0:T(8,128)S(1)} %copy-done.66, pred[512,1536]{0,1:T(8,128)(4,1)S(1)} %copy-done.1, bf16[1536,5,64,1]{0,2,3,1:T(8,128)(2,1)S(1)} %bitcast.329, bf16[512,5,5,64]{0,3,2,1:T(8,128)(2,1)S(1)} %bitcast.315), kind=kOutput, calls=%fused_computation.7 | convolution fusion | flops 2614873600 | bytes 160796672 | tf_op jit(solution)/shard_map/tkgd,skd->kgts/dot_general | solution.py:305
  1383.0 67.1 %fusion.3 = bf16[5,5,512,1536]{2,3,1,0:T(8,128)(2,1)} fusion(f32[5,1536,512,5]{2,1,3,0:T(8,128)} %get-tuple-element.318, f32[5,1536,512,5]{2,1,3,0:T(8,128)} %get-tuple-element.310, f32[5,5,512]{2,1,0:T(8,128)} %get-tuple-element.317, f32[5,5,512]{2,1,0:T(8,128)S(1)} %copy-done.66, pred[512,1536]{0,1:T(8,128)(4,1)S(1)} %copy-done.1), kind=kLoop, calls=%fused_computation.9 | loop fusion | flops 117964800 | bytes 197496832 | tf_op jit(solution)/shard_map/convert_element_type | solution.py:306
  1450.2 18.6 fusion.40
  1479.3 28.0 collective-permute-done.2
  1508.9 30.1 collective-permute-done.3
  1543.5 8.5 convolution_convert_fusion.6
  1553.2 17.8 multiply_convert_fusion.11
  1578.5 11.5 convolution_convert_fusion.5
  1595.7 17.3 convolution_convert_fusion
  1615.6 604.5 %all-reduce.22.cloned.1.call-done = (bf16[1600,5504]{1,0:T(8,128)(2,1)}, bf16[1600,5504]{1,0:T(8,128)(2,1)}, bf16[5504,1600]{0,1:T(8,128)(2,1)}, bf16[1600,32]{0,1:T(8,128)(2,1)}, bf16[1600,50]{0,1:T(8,128)(2,1)}) async-done(((bf16[1600,5504]{1,0:T(8,128)(2,1)}, bf16[1600,5504]{1,0:T(8,128)(2,1)}, bf16[5504,1600]{0,1:T(8,128)(2,1)}, bf16[1600,32]{0,1:T(8,128)(2,1)}, bf16[1600,50]{0,1:T(8,128)(2,1)}), ...) | async-done | bytes 53100816
  2223.2 6.9 constant_dynamic-slice_fusion.2
  2230.0 7.1 constant_dynamic-slice_fusion.3
  2237.2 7.0 constant_dynamic-slice_fusion.4
  2244.2 9.8 reduce-scatter.28.cloned.1.call-done
  2254.0 32.6 reduce-scatter.26.cloned.1.call-done
  2286.6 67.8 %reduce-scatter.32.cloned.1.call-done = bf16[400,1600]{1,0:T(8,128)(2,1)} async-done(((bf16[1600,1600]{1,0:T(8,128)(2,1)}), bf16[400,1600]{1,0:T(8,128)(2,1)}) %reduce-scatter.32.cloned.1.call-update) | async-done | bytes 1280016
  2354.4 67.6 %reduce-scatter.24.cloned.1.call-done = bf16[400,1600]{1,0:T(8,128)(2,1)} async-done(((bf16[1600,1600]{1,0:T(8,128)(2,1)}), bf16[400,1600]{1,0:T(8,128)(2,1)}) %reduce-scatter.24.cloned.1.call-update) | async-done | bytes 1280016
  2422.0 110.0 %reduce-scatter.22.cloned.1.call-done = bf16[800,1600]{1,0:T(8,128)(2,1)} async-done(((bf16[3200,1600]{1,0:T(8,128)(2,1)}), bf16[800,1600]{1,0:T(8,128)(2,1)}) %reduce-scatter.22.cloned.1.call-update) | async-done | bytes 2560016 | tf_op jit(solution)/shard_map/reduce_scatter | solution.py:386
  2532.0 220.0 %reduce-scatter.30.cloned.1.call-done = bf16[400,6400]{1,0:T(8,128)(2,1)} async-done(((bf16[1600,6400]{1,0:T(8,128)(2,1)}), bf16[400,6400]{1,0:T(8,128)(2,1)}) %reduce-scatter.30.cloned.1.call-update) | async-done | bytes 5120016
  2755.3 7.5 fusion.105
  2762.8 16.2 fusion.38
  2785.4 18.5 fusion.25
  2809.1 43.4 %all-reduce.10 = (f32[1600]{0:T(1024)}, f32[1600]{0:T(1024)}, f32[1600]{0:T(1024)}, f32[1600]{0:T(1024)}, f32[50]{0:T(128)}) all-reduce(f32[1600]{0:T(1024)S(1)} %get-tuple-element.237, f32[1600]{0:T(1024)S(1)} %copy-done.102, f32[1600]{0:T(1024)S(1)} %copy-done.101, ...), channel_id=1, replica_groups=mesh['rep'=8,'shard'=4] {'rep','shard'}, use_global_device_ids=true, to_apply=%region_49.50 | all-reduce | flops 6450 | bytes 51600 | tf_op jit(solution)/shard_map/psum | solution.py:406
  2860.3 441.5 %all-reduce.20.cloned.1.call-done = (bf16[400,1600]{1,0:T(8,128)(2,1)}, bf16[400,320]{1,0:T(8,128)(2,1)}, bf16[400,320]{1,0:T(8,128)(2,1)}, bf16[400,6400]{1,0:T...) async-done(((bf16[400,1600]{1,0:T(8,128)(2,1)}, ...) | async-done | bytes 23961616 | tf_op jit(solution)/shard_map/psum | solution.py:394
  (419 shorter events, 237.4 us)
Async XLA Ops:
  7.2 134.4 %all-gather.17.cloned.1.call-start = ((), (), s32[]{:S(2)}) async-start(), calls=%async_computation.6 | async-start | bytes 6656000 | tf_op jit(solution)/shard_map/all_gather | solution.py:139
  7.9 271.3 %all-gather.29.cloned.1.call-start = ((), (), s32[]{:S(2)}) async-start(), calls=%async_computation.13 | async-start | bytes 22528000 | tf_op jit(solution)/shard_map/all_gather | solution.py:149
  8.7 441.4 %all-gather.27.cloned.1.call-start = ((), (), s32[]{:S(2)}) async-start(), calls=%async_computation.12 | async-start | bytes 22528000 | tf_op jit(solution)/shard_map/all_gather | solution.py:148
  9.4 611.4 %all-gather.25.cloned.1.call-start = ((), (), s32[]{:S(2)}) async-start(), calls=%async_computation.11 | async-start | bytes 22528000 | tf_op jit(solution)/shard_map/all_gather | solution.py:147
  10.0 801.7 %all-gather.19.cloned.1.call-start = ((), (), s32[]{:S(2)}) async-start(), calls=%async_computation.7 | async-start | bytes 25600000 | tf_op jit(solution)/shard_map/all_gather | solution.py:142
  10.6 19.1 copy-start.71
  10.6 38.8 %copy-start.11 = (bf16[512,1600]{0,1:T(8,128)(2,1)S(1)}, bf16[512,1600]{0,1:T(8,128)(2,1)}, u32[]{:S(2)}) copy-start(bf16[512,1600]{0,1:T(8,128)(2,1)} %param.25) | copy-start | bytes 4915204
  10.6 39.2 %copy-start.82 = (f32[1600]{0:T(1024)S(1)}, f32[1600]{0:T(1024)}, u32[]{:S(2)}) copy-start(f32[1600]{0:T(1024)} %param.39) | copy-start | bytes 19204
  10.6 916.8 %all-gather.21.cloned.1.call-start = ((), (), s32[]{:S(2)}) async-start(), calls=%async_computation.8 | async-start | bytes 13312000 | tf_op jit(solution)/shard_map/all_gather | solution.py:145
  11.2 980.0 %all-gather.23.cloned.1.call-start = ((), (), s32[]{:S(2)}) async-start(), calls=%async_computation.9 | async-start | bytes 6656000 | tf_op jit(solution)/shard_map/all_gather | solution.py:146
  29.7 21.4 copy-start.30
  50.2 51.1 %copy-start.3 = (bf16[512,1600]{0,1:T(8,128)(2,1)}, bf16[512,1600]{0,1:T(8,128)(2,1)S(1)}, u32[]{:S(2)}) copy-start(bf16[512,1600]{0,1:T(8,128)(2,1)S(1)} %fusion.27) | copy-start | bytes 4915204
  51.1 39.7 %copy-start.84 = (bf16[400,50]{0,1:T(8,128)(2,1)S(1)}, bf16[400,50]{0,1:T(8,128)(2,1)}, u32[]{:S(2)}) copy-start(bf16[400,50]{0,1:T(8,128)(2,1)} %param.33) | copy-start | bytes 120004
  51.9 49.4 %copy-start.104 = (f32[50]{0:T(128)S(1)}, f32[50]{0:T(128)}, u32[]{:S(2)}) copy-start(f32[50]{0:T(128)} %param.43) | copy-start | bytes 604
  52.8 54.9 %collective-permute-start = (bf16[2,512,320]{1,2,0:T(8,128)(2,1)}, bf16[2,512,320]{1,2,0:T(8,128)(2,1)}, u32[]{:S(2)}, u32[]{:S(2)}) collective-permute-start(bf16[2,512,320]{1,2,0:T(8,128)(2,1)} %pad_maximum_fusion.5), channel_id=1, source_target_pairs={{0,1},{1,2},{2,3},{4,5},{5,6},{6,7},{8,9},{9,10},{10,11},{12,13},{... | collective-permute-start | bytes 1966088 | tf_op jit(solution)/shard_map/ppermute | solution.py:23
  57.8 2162.2 %all-reduce.22.cloned.1.call-start = ((), (), s32[]{:S(2)}) async-start(), calls=%async_computation.21 | async-start | bytes 106262528
  100.7 784.1 %copy-start.62 = (bf16[512,32]{0,1:T(8,128)(2,1)}, bf16[512,32]{0,1:T(8,128)(2,1)S(1)}, u32[]{:S(2)}) copy-start(bf16[512,32]{0,1:T(8,128)(2,1)S(1)} %convolution_convert_fusion.15) | copy-start | bytes 98308
  101.8 37.2 %copy-start.56 = (f32[512,50]{0,1:T(8,128)}, f32[512,50]{0,1:T(8,128)S(1)}, u32[]{:S(2)}) copy-start(f32[512,50]{0,1:T(8,128)S(1)} %get-tuple-element.306) | copy-start | bytes 307204
  103.5 785.2 %copy-start.49 = (f32[7,8,4,128]{3,1,2,0:T(8,128)}, f32[7,8,4,128]{3,1,2,0:T(8,128)S(1)}, u32[]{:S(2)}) copy-start(f32[7,8,4,128]{3,1,2,0:T(8,128)S(1)} %copy.159) | copy-start | bytes 344068
  105.7 24.0 copy-start.96
  105.7 24.0 copy-start.97
  107.7 31.2 collective-permute-start.1
  138.9 66.3 %copy-start = (pred[512,1536]{0,1:T(8,128)(4,1)}, pred[512,1536]{0,1:T(8,128)(4,1)S(1)}, u32[]{:S(2)}) copy-start(pred[512,1536]{0,1:T(8,128)(4,1)S(1)} %compare_and_fusion) | copy-start | bytes 2359300
  148.1 29.0 copy-start.2
  177.1 28.1 copy-start.64
  177.1 28.1 copy-start.31
  205.2 31.3 copy-start.65
  236.5 700.4 %copy-start.98 = (f32[512]{0:T(512)}, f32[512]{0:T(512)S(1)}, u32[]{:S(2)}) copy-start(f32[512]{0:T(512)S(1)} %add_rsqrt_fusion.2) | copy-start | bytes 6148
  474.5 337.2 %copy-start.4 = (bf16[512,1600]{0,1:T(8,128)(2,1)S(1)}, bf16[512,1600]{0,1:T(8,128)(2,1)}, u32[]{:S(2)}) copy-start(bf16[512,1600]{0,1:T(8,128)(2,1)} %copy-done.3) | copy-start | bytes 4915204
  847.4 41.3 %copy-start.8 = (bf16[512,50,64]{0,2,1:T(8,128)(2,1)}, bf16[512,50,64]{0,2,1:T(8,128)(2,1)S(1)}, u32[]{:S(2)}) copy-start(bf16[512,50,64]{0,2,1:T(8,128)(2,1)S(1)} %multiply_convert_fusion.9) | copy-start | bytes 9830404
  888.7 16.6 copy-start.10
  919.1 17.7 copy-start.33
  919.1 19.5 copy-start.88
  919.1 19.5 copy-start.90
  938.6 52.6 %copy-start.12 = (bf16[512,1600]{0,1:T(8,128)(2,1)S(1)}, bf16[512,1600]{0,1:T(8,128)(2,1)}, u32[]{:S(2)}) copy-start(bf16[512,1600]{0,1:T(8,128)(2,1)} %param.25) | copy-start | bytes 4915204
  941.0 56.2 %copy-start.44 = (bf16[512,1600]{0,1:T(8,128)(2,1)}, bf16[512,1600]{0,1:T(8,128)(2,1)S(1)}, u32[]{:S(2)}) copy-start(bf16[512,1600]{0,1:T(8,128)(2,1)S(1)} %get-tuple-element.284) | copy-start | bytes 4915204
  999.2 17.7 copy-start.42
  1016.9 17.3 copy-start.40
  1059.9 16.5 copy-start.16
  1202.6 19.8 slice-start.8
  1236.8 51.0 %copy-start.74 = (bf16[512,16]{0,1:T(8,128)(2,1)}, bf16[512,16]{0,1:T(8,128)(2,1)S(1)}, u32[]{:S(2)}) copy-start(bf16[512,16]{0,1:T(8,128)(2,1)S(1)} %fusion.51) | copy-start | bytes 49156
  1249.5 20.6 copy-start.57
  1249.5 20.6 copy-start.69
  1249.5 20.6 copy-start.105
  1249.5 21.9 copy-start.5
  1249.5 23.2 copy-start.41
  1289.0 965.0 %reduce-scatter.28.cloned.1.call-start = ((), (), s32[]{:S(2)}) async-start(), calls=%async_computation.16 | async-start | bytes 1536000
  1475.7 31.6 collective-permute-start.2
  1479.3 59.9 %copy-start.6 = (bf16[512,1600]{0,1:T(8,128)(2,1)S(1)}, bf16[512,1600]{0,1:T(8,128)(2,1)}, u32[]{:S(2)}) copy-start(bf16[512,1600]{0,1:T(8,128)(2,1)} %copy-done.3) | copy-start | bytes 4915204
  1507.6 31.4 collective-permute-start.3
  1541.3 745.3 %reduce-scatter.26.cloned.1.call-start = ((), (), s32[]{:S(2)}) async-start(), calls=%async_computation.15 | async-start | bytes 1536000
  1543.5 810.9 %reduce-scatter.32.cloned.1.call-start = ((), (), s32[]{:S(2)}) async-start(), calls=%async_computation.18 | async-start | bytes 6656000
  1552.0 870.0 %reduce-scatter.24.cloned.1.call-start = ((), (), s32[]{:S(2)}) async-start(), calls=%async_computation.14 | async-start | bytes 6656000
  1577.1 955.0 %reduce-scatter.22.cloned.1.call-start = ((), (), s32[]{:S(2)}) async-start(), calls=%async_computation.10 | async-start | bytes 13312000 | tf_op jit(solution)/shard_map/reduce_scatter | solution.py:386
  1590.0 1162.0 %reduce-scatter.30.cloned.1.call-start = ((), (), s32[]{:S(2)}) async-start(), calls=%async_computation.17 | async-start | bytes 25600000
  1613.1 1244.4 %all-reduce.18.cloned.1.call-start = ((), (), s32[]{:S(2)}) async-start(), calls=%async_computation.19 | async-start | bytes 180224 | tf_op jit(solution)/shard_map/psum | solution.py:398
  2237.2 1064.7 %all-reduce.20.cloned.1.call-start = ((), (), s32[]{:S(2)}) async-start(), calls=%async_computation.20 | async-start | bytes 49152000 | tf_op jit(solution)/shard_map/psum | solution.py:394
  2785.4 18.6 copy-start.13
  2785.4 18.6 copy-start.19
  2785.4 18.6 copy-start.61
  2785.4 18.6 copy-start.75
  2785.4 18.6 copy-start.77
  2785.4 18.6 copy-start.83
  2785.4 18.6 copy-start.94
  (75 other events, 410.6 us)
Sparse Core Ops, SparseCore 0:
  9.9 88.3 all-gather.16
  100.1 179.0 all-gather.28
  281.1 168.9 all-gather.26
  451.8 168.9 all-gather.24
  622.5 189.1 all-gather.18
  813.4 113.9 all-gather.20
  929.2 61.9 all-gather.22
  1289.2 930.8 all-reduce.21
  2224.0 29.9 reduce-scatter.27
  2257.4 29.1 reduce-scatter.25
  2290.5 63.8 reduce-scatter.31
  2358.1 63.8 reduce-scatter.23
  2425.4 106.5 reduce-scatter.21
  2535.3 216.7 reduce-scatter.29
  2754.9 52.5 all-reduce.17
  2812.7 489.0 all-reduce.19
where the time goes:
time: 3350 us; the launch traced here: 3340 us
  waiting for transfers between devices  2180 us (65%)
  matrix products  593 us (18%)
  other arithmetic  187 us (6%)
  blocking collectives  183 us (5%)
  local copies, waits for them, and re-layouts  171 us (5%)
    unnamed x22, waiting for transfers between devices  1010 us
    psum x1, waiting for transfers between devices, body(): lax.psum(query_owned.astype(jnp.bfloat16), 'rep').astype(jnp.float32)  442 us
    all_gather x1, waiting for transfers between devices, body(): lax.all_gather(inner_weight, 'shard', axis=0, tiled=True)  166 us
    all_gather x1, waiting for transfers between devices, body(): lax.all_gather(up_weight, 'shard', axis=1, tiled=True)  147 us
    all_gather x1, waiting for transfers between devices, body(): lax.all_gather(gate_weight, 'shard', axis=1, tiled=True)  146 us
    dot_general x12, matrix products, right_product(): lax.dot_general(left, right, (((1,), (1,)), ((), ())), preferred_element_...  127 us
    reduce_scatter x1, waiting for transfers between devices, body(): lax.psum_scatter(mamba_part.astype(jnp.bfloat16), 'shard', scatter_dimens...  110 us
    dot_general x12, matrix products, left_product(): lax.dot_general(left, right, (((0,), (0,)), ((), ())), preferred_element_...  93.2 us
  transfers between devices with their start and end apart: 20, of which 16 were waited for; matrix products, arithmetic and copies ran while one was open for 19% of the time, Pallas kernels for 0%

commit v1 on v0

v1 whole, which is shorter than its diff:
```python
import jax
import jax.numpy as jnp
from jax import lax
from jax.sharding import PartitionSpec as P

HEADS = 25
KV_HEADS = 5
HEAD_DIM = 64
INNER = 3200
STATE = 16
WINDOW = 1024
MAMBA_DIM = 64
MAMBA_HEADS = 50


EPSILON = 1e-05
HIGHEST = lax.Precision.HIGHEST


def moved(block, axis, distance):
    devices = range(lax.axis_size(axis))
    route = [(i - distance, i) for i in devices if i - distance in devices]
    return lax.ppermute(block, axis, route)


def swapped(block):
    return lax.ppermute(block, "core", [(0, 1), (1, 0)])


def pick(first, second, core):
    return jnp.where(core == 0, first, second)


def state_from(local, carry, sign):
    length = lax.axis_size("shard")
    total = moved(local, "shard", sign)
    product = None
    for distance in range(2, length):
        between = moved(carry, "shard", sign * (distance - 1))
        product = between if product is None else product * between
        total = total + product[:, None, None] * moved(local, "shard", sign * distance)
    return total


def sum_over_chips(part):
    if lax.axis_size("zz") != 4:
        return lax.psum(part, "zz")
    place = lax.axis_index("zz")
    wide = part.astype(jnp.float32)
    inward = lax.ppermute(part, "zz", [(0, 1), (3, 2)]).astype(jnp.float32)
    side = (wide + inward).astype(jnp.bfloat16)
    across = lax.ppermute(side, "zz", [(1, 2), (2, 1)]).astype(jnp.float32)
    full = (side.astype(jnp.float32) + across).astype(jnp.bfloat16)
    back = lax.ppermute(full, "zz", [(1, 0), (2, 3)])
    return jnp.where((place == 0) | (place == 3), back, full)


def gathered(weight, core):
    rows = weight.shape[0] // 2
    half = lax.dynamic_slice_in_dim(weight, core * rows, rows, 0)
    return lax.all_gather(half, ("shard", "core"), axis=0, tiled=True)


def core_half(part, core):
    rows = part.shape[0] // 2
    mine = lax.dynamic_slice_in_dim(part, core * rows, rows, 0)
    other = lax.dynamic_slice_in_dim(part, (1 - core) * rows, rows, 0)
    return (mine.astype(jnp.float32) + swapped(other).astype(jnp.float32)).astype(jnp.bfloat16)


def both_halves(mine, core, axis):
    other = swapped(mine)
    return jnp.concatenate([pick(mine, other, core), pick(other, mine, core)], axis).astype(jnp.float32)


def both_cores(full, core):
    columns = full.shape[1] // 2
    first, second = full[:, :columns], full[:, columns:]
    return jnp.concatenate([pick(first, second, core), swapped(pick(second, first, core))], 0)


def scattered(part, axis=0):
    return lax.psum_scatter(part.astype(jnp.bfloat16), "shard", scatter_dimension=axis, tiled=True)


def project(left, right):
    return jnp.dot(left, right, preferred_element_type=jnp.float32)


def left_product(left, right):
    return lax.dot_general(
        left, right, (((0,), (0,)), ((), ())), preferred_element_type=jnp.float32
    )


def right_product(left, right):
    return lax.dot_general(
        left, right, (((1,), (1,)), ((), ())), preferred_element_type=jnp.float32
    )


def inverse_rms(values):
    return lax.rsqrt(jnp.mean(values * values, axis=-1, keepdims=True) + EPSILON)


def rms_back(incoming, normed, factor):
    return factor * (incoming - normed * jnp.mean(incoming * normed, axis=-1, keepdims=True))


def silu_slope(values):
    sigma = jax.nn.sigmoid(values)
    return sigma * (1.0 + values * (1.0 - sigma))


def body(
    tokens,
    cotangent,
    doc_start,
    query_weight,
    key_weight,
    value_weight,
    inner_weight,
    select_weight,
    step_weight,
    mamba_out,
    mixer_out,
    gate_weight,
    up_weight,
    down_weight,
    attention_gain,
    attention_scale,
    mamba_scale,
    feed_gain,
    decay_rate,
):
    count = tokens.shape[0]
    core = lax.axis_index("core")
    begin = lax.axis_index(("zz", "core", "shard")) * count
    place = begin + jnp.arange(count, dtype=jnp.int32)
    blocks = (WINDOW + count - 1) // count
    groups = HEADS // KV_HEADS
    factor = HEAD_DIM ** (-0.5)
    widths = [query_weight.shape[1], key_weight.shape[1], value_weight.shape[1], 2 * STATE, MAMBA_HEADS]
    used = sum(widths)
    spare = -used % 256
    mixed_weight = jnp.pad(
        jnp.concatenate([query_weight, key_weight, value_weight, select_weight, step_weight], 1),
        ((0, 0), (0, spare)),
    )
    mixed_full = gathered(mixed_weight, core)
    inner_full = gathered(inner_weight, core)
    mamba_full = gathered(mamba_out, core)
    mixer_full = gathered(mixer_out, core)
    cotangent_all = lax.all_gather(cotangent, "shard", axis=0, tiled=True)
    inputs = tokens.astype(jnp.float32)
    scale_one = inverse_rms(inputs)
    unit_one = inputs * scale_one
    normed = (unit_one * attention_gain).astype(jnp.bfloat16)
    normed_both = jnp.concatenate([normed, swapped(normed)], 0)
    first = project(normed, mixed_full)
    cuts = [sum(widths[:i]) for i in range(6)]
    query = first[:, : cuts[1]].astype(jnp.bfloat16)
    pair = first[:, cuts[1] : cuts[3]].astype(jnp.bfloat16)
    select = first[:, cuts[3] : cuts[4]]
    step_raw = first[:, cuts[4] : cuts[5]]
    window_pairs = jnp.concatenate([moved(pair, "shard", d) for d in range(blocks, 0, -1)] + [pair], 0)
    span = (blocks + 1) * count
    all_keys = window_pairs[:, : widths[1]]
    all_values = window_pairs[:, widths[1] :]
    all_keys = all_keys.reshape(span, KV_HEADS, HEAD_DIM)
    all_values = all_values.reshape(span, KV_HEADS, HEAD_DIM)
    key_place = begin - blocks * count + jnp.arange(span, dtype=jnp.int32)
    allowed = (
        (key_place[None, :] <= place[:, None])
        & (key_place[None, :] > place[:, None] - WINDOW)
        & (key_place[None, :] >= doc_start[:, None])
    )
    query_heads = query.reshape(count, KV_HEADS, groups, HEAD_DIM)
    raw = jnp.einsum("tkgd,skd->kgts", query_heads, all_keys, preferred_element_type=jnp.float32)
    scores = jnp.where(allowed, raw * factor, -1e30)
    peak = jnp.max(scores, axis=-1, keepdims=True)
    logsum = peak + jnp.log(jnp.sum(jnp.exp(scores - peak), axis=-1, keepdims=True))
    weights_low = jnp.exp(scores - logsum).astype(jnp.bfloat16)
    attended = jnp.einsum(
        "kgts,skd->tkgd", weights_low, all_values, preferred_element_type=jnp.float32
    ).reshape(count, HEADS * HEAD_DIM)
    inner = project(normed, inner_full)
    signal = inner[:, :INNER]
    switch = inner[:, INNER:]
    writer = select[:, :STATE].astype(jnp.bfloat16)
    reader = select[:, STATE:].astype(jnp.bfloat16)
    step = jax.nn.softplus(step_raw)
    heads_in = signal.reshape(count, MAMBA_HEADS, MAMBA_DIM)
    drive = (heads_in * step[:, :, None]).astype(jnp.bfloat16)
    rate = -step * decay_rate[None, :]
    cumul = jnp.cumsum(rate, axis=0)
    valid = (place[None, :] <= place[:, None]) & (place[None, :] >= doc_start[:, None])
    spread = cumul.T[:, :, None] - cumul.T[:, None, :]
    decay = jnp.where(valid[None], jnp.exp(jnp.where(valid[None], spread, 0.0)), 0.0)
    gram = right_product(reader, writer)
    mixing = (gram[None] * decay).astype(jnp.bfloat16)
    intra = jnp.einsum("hts,shd->thd", mixing, drive, preferred_element_type=jnp.float32)
    enter = jnp.exp(cumul) * (doc_start < begin)[:, None]
    tail = jnp.exp(cumul[-1][None, :] - cumul) * (place >= doc_start[-1])[:, None]
    carry = jnp.exp(cumul[-1]) * (doc_start[-1] < begin)
    reader_wide = reader.astype(jnp.float32)
    writer_wide = writer.astype(jnp.float32)
    drive_wide = drive.astype(jnp.float32)
    local = jnp.einsum("sh,shd,sn->hdn", tail, drive_wide, writer_wide, precision=HIGHEST)
    state_in = state_from(local, carry, 1)
    through = jnp.einsum("tn,hdn->thd", reader_wide, state_in, precision=HIGHEST)
    mixed_flat = (intra + enter[:, :, None] * through).reshape(count, INNER)
    gated = (mixed_flat * jax.nn.silu(switch)).astype(jnp.bfloat16)
    mamba_y = project(gated, mamba_full)
    scale_att = inverse_rms(attended)
    unit_att = attended * scale_att
    scale_mam = inverse_rms(mamba_y)
    unit_mam = mamba_y * scale_mam
    blend = (0.5 * (attention_scale * unit_att + mamba_scale * unit_mam)).astype(jnp.bfloat16)
    middle = inputs + project(blend, mixer_full)
    scale_two = inverse_rms(middle)
    unit_two = middle * scale_two
    feed_in = (unit_two * feed_gain).astype(jnp.bfloat16)
    feed_all = lax.all_gather(feed_in, "shard", axis=0, tiled=True)
    gate = project(feed_all, gate_weight)
    up = project(feed_all, up_weight)
    active = (jax.nn.silu(gate) * up).astype(jnp.bfloat16)
    output = (middle + scattered(project(active, down_weight)).astype(jnp.float32)).astype(jnp.bfloat16)
    upstream = cotangent.astype(jnp.float32)
    d_active = right_product(cotangent_all, down_weight)
    d_gate = (d_active * up * silu_slope(gate)).astype(jnp.bfloat16)
    d_up = (d_active * jax.nn.silu(gate)).astype(jnp.bfloat16)
    feed_back = scattered(right_product(d_gate, gate_weight) + right_product(d_up, up_weight)).astype(
        jnp.float32
    )
    gate_part = left_product(feed_all, d_gate).astype(jnp.bfloat16)
    up_part = left_product(feed_all, d_up).astype(jnp.bfloat16)
    down_part = left_product(active, cotangent_all).astype(jnp.bfloat16)
    gate_sum = sum_over_chips(core_half(gate_part, core))
    up_sum = sum_over_chips(core_half(up_part, core))
    down_sum = sum_over_chips(core_half(down_part, core))
    feed_gain_part = jnp.sum(feed_back * unit_two, axis=0)
    d_middle = upstream + rms_back(feed_back * feed_gain, unit_two, scale_two)
    d_branch = d_middle.astype(jnp.bfloat16)
    d_blend = right_product(d_branch, mixer_full)
    attention_scale_part = jnp.sum(0.5 * d_blend * unit_att, axis=0)
    mamba_scale_part = jnp.sum(0.5 * d_blend * unit_mam, axis=0)
    d_attended = rms_back(0.5 * d_blend * attention_scale, unit_att, scale_att).astype(jnp.bfloat16)
    d_mamba = rms_back(0.5 * d_blend * mamba_scale, unit_mam, scale_mam).astype(jnp.bfloat16)
    d_gated = right_product(d_mamba, mamba_full)
    d_mixed = (
        (d_gated * jax.nn.silu(switch)).astype(jnp.bfloat16).reshape(count, MAMBA_HEADS, MAMBA_DIM)
    )
    d_switch = (d_gated * mixed_flat * silu_slope(switch)).astype(jnp.bfloat16)
    d_mix = (
        jnp.einsum("thd,shd->hts", d_mixed, drive, preferred_element_type=jnp.float32)
        .astype(jnp.bfloat16)
        .astype(jnp.float32)
    )
    d_drive = jnp.einsum("hts,thd->shd", mixing, d_mixed, preferred_element_type=jnp.float32)
    d_gram = jnp.sum(d_mix * decay, axis=0).astype(jnp.bfloat16)
    d_decay = d_mix * gram[None]
    d_mixed_wide = d_mixed.astype(jnp.float32)
    d_enter = jnp.sum(d_mixed_wide * through, axis=-1)
    d_through = d_mixed_wide * enter[:, :, None]
    d_reader_state = jnp.einsum("thd,hdn->tn", d_through, state_in, precision=HIGHEST)
    state_grad = jnp.einsum("thd,tn->hdn", d_through, reader_wide, precision=HIGHEST)
    d_out = state_from(state_grad, carry, -1)
    d_carry = jnp.sum(d_out * state_in, axis=(1, 2))
    d_tail = jnp.einsum("hdn,shd,sn->sh", d_out, drive_wide, writer_wide, precision=HIGHEST)
    d_drive = d_drive + tail[:, :, None] * jnp.einsum(
        "hdn,sn->shd", d_out, writer_wide, precision=HIGHEST
    )
    d_writer_state = jnp.einsum("sh,shd,hdn->sn", tail, drive_wide, d_out, precision=HIGHEST)
    d_spread = d_decay * decay
    d_cumul = (jnp.sum(d_spread, axis=2) - jnp.sum(d_spread, axis=1)).T
    tail_term = d_tail * tail
    d_cumul = d_cumul + d_enter * enter - tail_term
    d_cumul = d_cumul.at[-1].add(jnp.sum(tail_term, axis=0) + d_carry * carry)
    d_rate = jnp.flip(jnp.cumsum(jnp.flip(d_cumul, 0), axis=0), 0)
    decay_rate_part = -jnp.sum(d_rate * step, axis=0)
    d_drive_low = d_drive.astype(jnp.bfloat16).astype(jnp.float32)
    d_step = -d_rate * decay_rate[None, :] + jnp.sum(d_drive_low * heads_in, axis=-1)
    d_signal = (d_drive_low * step[:, :, None]).reshape(count, INNER).astype(jnp.bfloat16)
    d_step_raw = (d_step * jax.nn.sigmoid(step_raw)).astype(jnp.bfloat16)
    d_reader = (project(d_gram, writer) + d_reader_state).astype(jnp.bfloat16)
    d_writer = (left_product(d_gram, reader) + d_writer_state).astype(jnp.bfloat16)
    d_select = jnp.concatenate([d_writer, d_reader], axis=1)
    d_inner = jnp.concatenate([d_signal, d_switch], axis=1)
    d_heads = d_attended.reshape(count, KV_HEADS, groups, HEAD_DIM)
    raw_again = jnp.einsum(
        "tkgd,skd->kgts", query_heads, all_keys, preferred_element_type=jnp.float32
    )
    probs = jnp.exp(jnp.where(allowed, raw_again * factor, -1e30) - logsum)
    probs_low = probs.astype(jnp.bfloat16)
    d_probs = jnp.einsum("tkgd,skd->kgts", d_heads, all_values, preferred_element_type=jnp.float32)
    d_scores = (probs * (d_probs - jnp.sum(probs * d_probs, axis=-1, keepdims=True))).astype(
        jnp.bfloat16
    )
    d_query = (
        (
            jnp.einsum("kgts,skd->tkgd", d_scores, all_keys, preferred_element_type=jnp.float32)
            * factor
        )
        .astype(jnp.bfloat16)
        .reshape(count, HEADS * HEAD_DIM)
    )
    d_keys_all = (
        jnp.einsum("kgts,tkgd->skd", d_scores, query_heads, preferred_element_type=jnp.float32)
        * factor
    )
    d_values_all = jnp.einsum(
        "kgts,tkgd->skd", probs_low, d_heads, preferred_element_type=jnp.float32
    )
    halo_grads = jnp.concatenate(
        [d_keys_all.reshape(span, widths[1]), d_values_all.reshape(span, widths[2])], 1
    )
    own_grads = halo_grads[blocks * count :]
    for distance in range(1, blocks + 1):
        away = halo_grads[(blocks - distance) * count : (blocks - distance + 1) * count]
        own_grads = own_grads + moved(away.astype(jnp.bfloat16), "shard", -distance).astype(jnp.float32)
    d_mixed_all = jnp.pad(
        jnp.concatenate([d_query, own_grads.astype(jnp.bfloat16), d_select, d_step_raw], 1),
        ((0, 0), (0, spare)),
    )
    d_normed = right_product(d_inner, inner_full) + right_product(d_mixed_all, mixed_full)
    attention_gain_part = jnp.sum(d_normed * unit_one, axis=0)
    token_gradient = (d_middle + rms_back(d_normed * attention_gain, unit_one, scale_one)).astype(
        jnp.bfloat16
    )
    inner_sum = sum_over_chips(scattered(left_product(normed_both, both_cores(d_inner, core))))
    mixed_sum = sum_over_chips(scattered(left_product(normed_both, both_cores(d_mixed_all, core))))
    gated_both = jnp.concatenate([gated, swapped(gated)], 0)
    mamba_sum = sum_over_chips(scattered(left_product(gated_both, both_cores(d_mamba, core))))
    blend_both = jnp.concatenate([blend, swapped(blend)], 0)
    mixer_sum = sum_over_chips(scattered(left_product(blend_both, both_cores(d_branch, core))))
    mixed_gradient = both_halves(mixed_sum, core, 1)
    query_gradient, key_gradient, value_gradient, select_gradient, step_gradient = (
        mixed_gradient[:, cuts[i] : cuts[i + 1]] for i in range(5)
    )
    summed = (
        query_gradient,
        key_gradient,
        value_gradient,
        both_halves(inner_sum, core, 1),
        select_gradient,
        step_gradient,
        both_halves(mamba_sum, core, 1),
        both_halves(mixer_sum, core, 1),
        both_halves(gate_sum, core, 0),
        both_halves(up_sum, core, 0),
        both_halves(down_sum, core, 0),
    )
    small = lax.psum(
        (
            attention_gain_part,
            attention_scale_part,
            mamba_scale_part,
            feed_gain_part,
            decay_rate_part,
        ),
        ("zz", "core", "shard"),
    )
    return (
        output,
        token_gradient,
        summed[0],
        summed[1],
        summed[2],
        summed[3],
        summed[4],
        summed[5],
        summed[6],
        summed[7],
        summed[8],
        summed[9],
        summed[10],
        small[0],
        small[1],
        small[2],
        small[3],
        small[4],
    )


def solution(mesh):
    rep, shard = mesh.shape["rep"], mesh.shape["shard"]
    mesh = jax.sharding.Mesh(mesh.devices.reshape(rep // 2, 2, shard), ("zz", "core", "shard"))
    placed = (
        P(("zz", "core", "shard"), None),
        P(("zz", "core", "shard"), None),
        P(("zz", "core", "shard")),
        P("shard", None),
        P("shard", None),
        P("shard", None),
        P("shard", None),
        P("shard", None),
        P("shard", None),
        P("shard", None),
        P("shard", None),
        P(None, "shard"),
        P(None, "shard"),
        P("shard", None),
        P(),
        P(),
        P(),
        P(),
        P(),
    )
    return jax.shard_map(
        body,
        mesh=mesh,
        in_specs=placed,
        out_specs=(
            P(("zz", "core", "shard"), None),
            P(("zz", "core", "shard"), None),
            P("shard", None),
            P("shard", None),
            P("shard", None),
            P("shard", None),
            P("shard", None),
            P("shard", None),
            P("shard", None),
            P("shard", None),
            P(None, "shard"),
            P(None, "shard"),
            P("shard", None),
            P(),
            P(),
            P(),
            P(),
            P(),
        ),
        check_vma=False,
    )
```

time: 3350 us -> 1740 us (0.52)
  waiting for transfers between devices: 2180 us -> 619 us
  blocking collectives: 183 us -> 74.9 us
  starting transfers between devices: 10.5 us -> 88.6 us
  other arithmetic: 187 us -> 253 us
  local copies, waits for them, and re-layouts: 171 us -> 107 us
    unnamed x22 -> x14, waiting for transfers between devices: 1010 us -> 0.71 us
    psum x2 -> x0, waiting for transfers between devices: 442 us -> none  [the longest x1 442 us: body(): lax.psum(query_owned.astype(jnp.bfloat16), 'rep').astype(jnp.float32)]
    all_gather x7 -> x6, waiting for transfers between devices: 560 us -> 157 us  [the longest x1 72.2 us: body(): feed_all = lax.all_gather(feed_in, 'shard', axis=0, tiled=True)]
    ppermute x4 -> x52, waiting for transfers between devices: 58.1 us -> 399 us  [the longest x7 208 us: sum_over_chips(): inward = lax.ppermute(part, 'zz', [(0, 1), (3, 2)]).astype(jnp.float32)]
    all_gather x8 -> x0, blocking collectives: 139 us -> none  [the longest x2 32.1 us: entering(): everything = jax.tree.map(lambda part: lax.all_gather(part, axis), array)]
    ppermute x4 -> x52, starting transfers between devices: 9.47 us -> 88.1 us  [the longest x14 26.7 us: moved(): return lax.ppermute(block, axis, route)]
    all_gather x5 -> x0, local copies, waits for them, and re-layouts: 73.4 us -> none  [the longest x1 24.5 us: body(): lax.all_gather(gate_weight, 'shard', axis=1, tiled=True)]
    reduce_scatter x1 -> x4, waiting for transfers between devices: 110 us -> 63.2 us  [scattered(): lax.psum_scatter(part.astype(jnp.bfloat16), 'shard', scatter_dimension=ax...]
  transfers between devices with their start and end apart: 20 -> 64, of which waited for: 16 -> 22; matrix products, arithmetic and copies ran while one was open for 19% -> 49% of each run, Pallas kernels for 0% -> 0%
where the time goes in v1:
time: 1740 us; the launch traced here: 1730 us
  waiting for transfers between devices  619 us (36%)
  matrix products  571 us (33%)
  other arithmetic  253 us (15%)
  local copies, waits for them, and re-layouts  107 us (6%)
  starting transfers between devices  88.6 us (5%)
  blocking collectives  74.9 us (4%)
    ppermute x7, waiting for transfers between devices, sum_over_chips(): inward = lax.ppermute(part, 'zz', [(0, 1), (3, 2)]).astype(jnp.float32)  208 us
    ppermute x7, waiting for transfers between devices, sum_over_chips(): back = lax.ppermute(full, 'zz', [(1, 0), (2, 3)])  138 us
    dot_general x8, matrix products, right_product(): lax.dot_general(left, right, (((1,), (1,)), ((), ())), preferred_element_...  111 us
    dot_general x8, matrix products, project(): return jnp.dot(left, right, preferred_element_type=jnp.float32)  89.9 us
    dot_general x8, matrix products, left_product(): lax.dot_general(left, right, (((0,), (0,)), ((), ())), preferred_element_...  85.9 us
    psum x1, blocking collectives, body(): lax.psum((attention_gain_part, attention_scale_part, mamba_scale_part, fe...  74.9 us
    all_gather x1, waiting for transfers between devices, body(): feed_all = lax.all_gather(feed_in, 'shard', axis=0, tiled=True)  72.2 us
    reduce_scatter x4, waiting for transfers between devices, scattered(): lax.psum_scatter(part.astype(jnp.bfloat16), 'shard', scatter_dimension=ax...  63.2 us
  transfers between devices with their start and end apart: 64, of which 22 were waited for; matrix products, arithmetic and copies ran while one was open for 49% of the time, Pallas kernels for 0%

profile of v1, /device:TPU:1, one launch (start us, length us, event | category | flops | bytes accessed | tf_op | source)
XLA Modules:
  0.0 1730.9 jit_solution(4389602114339313089)
XLA Ops:
  29.0 43.2 %all-gather.7.cloned.1.call-done = bf16[1600,2560]{1,0:T(8,128)(2,1)} async-done(((bf16[200,2560]{1,0:T(8,128)(2,1)}), bf16[1600,2560]{1,0:T(8,128)(2,1)}) %all-gather.7.cloned.1.call-update) | async-done | bytes 8192016 | tf_op jit(solution)/shard_map/all_gather | solution.py:61
  72.2 7.9 fusion.123
  101.7 13.3 collective-permute-done.3
  115.0 7.7 collective-permute-done.5
  126.2 32.1 %fusion.8 = (f32[5,5,512]{2,1,0:T(8,128)S(1)}, f32[5,1536,512,5]{2,1,3,0:T(8,128)}) fusion(pred[512,1536]{0,1:T(8,128)(4,1)S(1)} %compare_and_fusion, bf16[1536,5,64,1]{0,2,3,1:T(8,128)(2,1)} %bitcast.202, bf16[512,5,5,64]{0,3,2,1:T(8,128)(2,1)S(1)} %bitcast.190), kind=kOutput, calls=%fused_computation.17 | convolution fusion | flops 2575552000 | bytes 82102272 | tf_op jit(solution)/shard_map/tkgd,skd->kgts/dot_general | solution.py:179
  158.3 25.7 %exponential_reduce_fusion = f32[5,5,512]{2,1,0:T(8,128)S(1)} fusion(f32[5,1536,512,5]{2,1,3,0:T(8,128)} %get-tuple-element.208, f32[5,5,512]{2,1,0:T(8,128)S(1)} %get-tuple-element.207, pred[512,1536]{0,1:T(8,128)(4,1)S(1)} %compare_and_fusion), kind=kLoop, calls=%fused_computation.7 | loop fusion | flops 78630400 | bytes 79532032 | tf_op jit(solution)/shard_map/reduce_sum | solution.py:182
  184.1 31.7 %fusion.54 = (f32[512]{0:T(512)S(1)}, f32[5,64,5,512]{3,1,2,0:T(8,128)}) fusion(bf16[1536,5,64,1]{0,2,3,1:T(8,128)(2,1)S(1)} %bitcast.210, f32[5,1536,512,5]{2,1,3,0:T(8,128)} %get-tuple-element.208, f32[5,5,512]{2,1,0:T(8,128)S(1)} %log_add_fusion, pred[512,1536]{0,1:T(8,128)(4,1)S(1)} %compare_and_fusion), kind=kOutput, calls=%fused_computation.112 | convolution fusion | flops 2596863488 | bytes 83742720 | tf_op jit(solution)/shard_map/kgts,skd->tkgd/dot_general | solution.py:184
  215.8 16.7 fusion.124
  241.3 21.3 %copy.205 = f32[512,3200]{0,1:T(8,128)} copy(f32[512,3200]{1,0:T(8,128)} %slice.151) | data formatting | bytes 13107200 | tf_op jit(solution)/shard_map/slice | solution.py:188
  278.9 20.5 %collective-permute-done.4 = f32[50,64,16]{1,2,0:T(8,128)S(1)} collective-permute-done((f32[50,64,16]{1,2,0:T(8,128)S(1)}, f32[50,64,16]{1,2,0:T(8,128)S(1)}, u32[]{:S(2)}, u32[]{:S(2)}) %collective-permute-start.4) | collective-permute-done | bytes 204832 | tf_op jit(solution)/shard_map/ppermute | solution.py:23
  303.4 16.7 bitcast_add_fusion.1
  320.0 8.2 copy.212
  328.3 6.9 multiply_convert_fusion.8
  335.2 10.5 multiply_reduce_fusion.5
  350.2 6.4 multiply_reduce_fusion.4
  360.4 72.2 %all-gather.15.cloned.1.call-done = bf16[2048,1600]{0,1:T(8,128)(2,1)} async-done(((bf16[512,1600]{0,1:T(8,128)(2,1)}), bf16[2048,1600]{0,1:T(8,128)(2,1)}) %all-gather.15.cloned.1.call-update) | async-done | bytes 6553616 | tf_op jit(solution)/shard_map/all_gather | solution.py:224
  432.6 17.0 fusion.125
  449.6 15.7 fusion.126
  465.4 41.2 %all-gather.17.cloned.1.call-done = bf16[2048,1600]{0,1:T(8,128)(2,1)} async-done(((bf16[512,1600]{0,1:T(8,128)(2,1)}), bf16[2048,1600]{0,1:T(8,128)(2,1)}) %all-gather.17.cloned.1.call-update) | async-done | bytes 6553616 | tf_op jit(solution)/shard_map/all_gather | solution.py:154
  506.6 24.0 %multiply_convert_fusion.3 = (bf16[2048,1376]{0,1:T(8,128)(2,1)}, bf16[2048,1376]{0,1:T(8,128)(2,1)}, bf16[2048,1376]{0,1:T(8,128)(2,1)}) fusion(f32[2048,1376]{0,1:T(8,128)} %fusion.125, f32[2048,1376]{0,1:T(8,128)} %fusion.126, bf16[2048,1600]{0,1:T(8,128)(2,1)} %all-gather.17.cloned.1.call-done, bf16[1376,1600]{0,1:T(8,128)(2,1)} %param.34), kind=kOutput, calls=%fused_computation.23 | convolution fusion | flops 9060024320 | bytes 50409472 | tf_op jit(solution)/shard_map/dot_general | solution.py:97
  530.5 14.0 fusion.127
  544.6 16.0 add_convert_fusion
  570.0 63.1 %reduce-scatter.13.cloned.1.call-done = bf16[512,1600]{0,1:T(8,128)(2,1)} async-done(((bf16[2048,1600]{0,1:T(8,128)(2,1)}), bf16[512,1600]{0,1:T(8,128)(2,1)}) %reduce-scatter.13.cloned.1.call-update) | async-done | bytes 1638416 | tf_op jit(solution)/shard_map/reduce_scatter | solution.py:83
  641.6 8.4 multiply_reduce_fusion
  652.4 14.8 multiply_convert_fusion.7
  667.2 5.8 copy.213
  673.0 7.1 fusion.13
  684.0 17.6 %fusion.9 = f32[50,64,512]{2,1,0:T(8,128)} fusion(bf16[512,50,64]{0,2,1:T(8,128)(2,1)S(1)} %bitcast.193, f32[50,512]{1,0:T(8,128)S(1)} %bitcast.218, f32[512,512]{1,0:T(8,128)S(1)} %copy-done.59, pred[512,512]{1,0:T(8,128)(4,1)S(1)} %copy-done.73), kind=kOutput, calls=%fused_computation.18 | convolution fusion | flops 1743257600 | bytes 11243520 | tf_op jit(solution)/shard_map/hts,thd->shd/dot_general | solution.py:260
  706.7 33.0 %fusion.6 = (f32[50,512]{1,0:T(8,128)}, f32[50,512]{1,0:T(8,128)}, bf16[512,512]{1,0:T(8,128)(2,1)}) fusion(f32[50,512]{1,0:T(8,128)S(1)} %bitcast.219, f32[512,512]{1,0:T(8,128)S(1)} %copy-done.60, pred[512,512]{1,0:T(8,128)(4,1)S(1)} %copy-done.73, bf16[512,50,64]{0,2,1:T(8,128)(2,1)S(1)} %bitcast.195, bf16[512,50,64]{0,2,1:T(8,128)(2,1)S(1)} %copy-done.11), kind=kOutput, calls=%fused_computation.15 | convolution fusion | flops 1821587456 | bytes 8695808 | tf_op jit(solution)/shard_map/thd,shd->hts/dot_general | solution.py:256
  739.7 56.8 %fusion = (f32[5,5,512]{2,1,0:T(8,128)S(1)}, f32[5,1536,512,5]{2,1,3,0:T(8,128)}) fusion(f32[5,1536,512,5]{2,1,3,0:T(8,128)} %get-tuple-element.208, f32[5,5,512]{2,1,0:T(8,128)S(1)} %copy-done.67, pred[512,1536]{0,1:T(8,128)(4,1)S(1)} %copy-done.3, bf16[1536,5,64,1]{0,2,3,1:T(8,128)(2,1)} %bitcast.209, bf16[512,5,5,64]{0,3,2,1:T(8,128)(2,1)S(1)} %bitcast.207), kind=kOutput, calls=%fused_computation.2 | convolution fusion | flops 2614873600 | bytes 160796672 | tf_op jit(solution)/shard_map/tkgd,skd->kgts/dot_general | solution.py:296
  796.5 30.0 %fusion.85 = f32[5,64,1536,1]{2,1,3,0:T(8,128)} fusion(bf16[512,5,5,64]{0,3,2,1:T(8,128)(2,1)S(1)} %bitcast.208, f32[5,1536,512,5]{2,1,3,0:T(8,128)} %get-tuple-element.208, f32[5,5,512]{2,1,0:T(8,128)S(1)} %copy-done.67, pred[512,1536]{0,1:T(8,128)(4,1)S(1)} %copy-done.3), kind=kOutput, calls=%fused_computation.202 | convolution fusion | flops 2595225600 | bytes 83085312 | tf_op jit(solution)/shard_map/kgts,tkgd->skd/dot_general | solution.py:312
  826.5 61.9 %fusion.2 = bf16[5,5,512,1536]{2,3,1,0:T(8,128)(2,1)} fusion(f32[5,1536,512,5]{2,1,3,0:T(8,128)} %get-tuple-element.215, f32[5,1536,512,5]{2,1,3,0:T(8,128)} %get-tuple-element.208, f32[5,5,512]{2,1,0:T(8,128)S(1)} %get-tuple-element.214, f32[5,5,512]{2,1,0:T(8,128)S(1)} %copy-done.67, pred[512,1536]{0,1:T(8,128)(4,1)S(1)} %copy-done.3), kind=kLoop, calls=%fused_computation.4 | loop fusion | flops 117964800 | bytes 197496832 | tf_op jit(solution)/shard_map/convert_element_type | solution.py:297
  888.4 18.1 %fusion.57 = f32[5,64,1536]{2,1,0:T(8,128)S(1)} fusion(bf16[512,5,5,64]{0,3,2,1:T(8,128)(2,1)} %bitcast.191, bf16[5,5,512,1536]{2,3,1,0:T(8,128)(2,1)} %fusion.2), kind=kOutput, calls=%fused_computation.133 | convolution fusion | flops 2517073920 | bytes 42926080 | tf_op jit(solution)/shard_map/kgts,tkgd->skd/dot_general | solution.py:309
  906.5 17.6 %multiply_convert_fusion.10 = bf16[5,64,5,512]{3,1,2,0:T(8,128)(2,1)} fusion(bf16[1536,5,64,1]{0,2,3,1:T(8,128)(2,1)} %bitcast.203, bf16[5,5,512,1536]{2,3,1,0:T(8,128)(2,1)} %fusion.2), kind=kOutput, calls=%fused_computation.115 | convolution fusion | flops 2518220800 | bytes 41943040 | tf_op jit(solution)/shard_map/kgts,skd->tkgd/dot_general | solution.py:302
  943.6 7.6 convolution_convert_fusion.8
  959.9 8.7 fusion.15
  978.7 6.0 copy.216
  984.7 8.7 convolution_convert_fusion.2
  993.5 8.4 broadcast_select_fusion.1
  1005.1 5.5 collective-permute-done.20
  1010.5 14.8 convolution_convert_fusion.1
  1025.9 15.0 convolution_convert_fusion.6
  1041.3 14.8 convolution_convert_fusion.4
  1059.2 14.2 convolution_convert_fusion.5
  1081.1 9.8 convolution_convert_fusion.7
  1099.2 29.5 %collective-permute-done.48 = bf16[688,1600]{1,0:T(8,128)(2,1)} collective-permute-done((bf16[688,1600]{1,0:T(8,128)(2,1)S(1)}, bf16[688,1600]{1,0:T(8,128)(2,1)}, u32[]{:S(2)}, u32[]{:S(2)}) %collective-permute-start.48) | collective-permute-done | bytes 2201632 | tf_op jit(solution)/shard_map/ppermute | solution.py:50
  1131.7 45.3 %collective-permute-done.43 = bf16[800,1376]{1,0:T(8,128)(2,1)S(1)} collective-permute-done((bf16[800,1376]{1,0:T(8,128)(2,1)S(1)}, bf16[800,1376]{1,0:T(8,128)(2,1)S(1)}, u32[]{:S(2)}, u32[]{:S(2)}) %collective-permute-start.43) | collective-permute-done | bytes 2201632 | tf_op jit(solution)/shard_map/ppermute | solution.py:50
  1181.0 44.2 %collective-permute-done.38 = bf16[800,1376]{1,0:T(8,128)(2,1)S(1)} collective-permute-done((bf16[800,1376]{1,0:T(8,128)(2,1)S(1)}, bf16[800,1376]{1,0:T(8,128)(2,1)S(1)}, u32[]{:S(2)}, u32[]{:S(2)}) %collective-permute-start.38) | collective-permute-done | bytes 2201632 | tf_op jit(solution)/shard_map/ppermute | solution.py:50
  1243.0 40.2 %collective-permute-done.50 = bf16[688,1600]{1,0:T(8,128)(2,1)} collective-permute-done((bf16[688,1600]{1,0:T(8,128)(2,1)S(1)}, bf16[688,1600]{1,0:T(8,128)(2,1)}, u32[]{:S(2)}, u32[]{:S(2)}) %collective-permute-start.50) | collective-permute-done | bytes 2201632 | tf_op jit(solution)/shard_map/ppermute | solution.py:54
  1288.9 14.6 convolution_convert_fusion.3
  1303.5 28.0 %collective-permute-done.45 = bf16[800,1376]{1,0:T(8,128)(2,1)} collective-permute-done((bf16[800,1376]{1,0:T(8,128)(2,1)}, bf16[800,1376]{1,0:T(8,128)(2,1)}, u32[]{:S(2)}, u32[]{:S(2)}) %collective-permute-start.45) | collective-permute-done | bytes 2201632 | tf_op jit(solution)/shard_map/ppermute | solution.py:54
  1338.3 41.5 %collective-permute-done.40 = bf16[800,1376]{1,0:T(8,128)(2,1)} collective-permute-done((bf16[800,1376]{1,0:T(8,128)(2,1)}, bf16[800,1376]{1,0:T(8,128)(2,1)}, u32[]{:S(2)}, u32[]{:S(2)}) %collective-permute-start.40) | collective-permute-done | bytes 2201632 | tf_op jit(solution)/shard_map/ppermute | solution.py:54
  1391.4 10.3 copy.230
  1414.0 5.9 maximum_convert_fusion.2
  1421.0 8.9 collective-permute-done.33
  1430.9 6.3 collective-permute-start.16
  1439.2 10.1 fusion.61
  1451.0 6.5 collective-permute-done.16
  1460.8 51.5 %collective-permute-done.21 = bf16[400,3200]{1,0:T(8,128)(2,1)S(1)} collective-permute-done((bf16[400,3200]{1,0:T(8,128)(2,1)}, bf16[400,3200]{1,0:T(8,128)(2,1)S(1)}, u32[]{:S(2)}, u32[]{:S(2)}) %collective-permute-start.21) | collective-permute-done | bytes 2560032 | tf_op jit(solution)/shard_map/ppermute | solution.py:50
  1516.7 21.6 %fusion.49 = (f32[1600]{0:T(1024)S(1)}, f32[512]{0:T(512)S(1)}, f32[512,1600]{0,1:T(8,128)}) fusion(bf16[512,1600]{0,1:T(8,128)(2,1)S(1)} %copy-done.16, f32[512]{0:T(512)S(1)} %copy-done.92, f32[1600]{0:T(1024)S(1)} %copy-done.83, f32[512,1600]{0,1:T(8,128)} %fusion.61, bf16[1600,6400]{1,0:T(8,128)(2,1)} %all-gather.9.cloned.1.call-done, ...), kind=kOutput, calls=%fused_computation.104 | convolution fusion | flops 10505418752 | bytes 35242496 | tf_op jit(solution)/shard_map/dot_general | solution.py:97
  1555.8 21.8 %collective-permute-done.27 = bf16[800,800]{1,0:T(8,128)(2,1)S(1)} collective-permute-done((bf16[800,800]{1,0:T(8,128)(2,1)}, bf16[800,800]{1,0:T(8,128)(2,1)S(1)}, u32[]{:S(2)}, u32[]{:S(2)}) %collective-permute-start.27) | collective-permute-done | bytes 1280032 | tf_op jit(solution)/shard_map/ppermute | solution.py:50
  1581.1 6.4 fusion.48
  1587.6 74.9 %all-reduce.4 = (f32[1600]{0:T(1024)}, f32[1600]{0:T(1024)}, f32[1600]{0:T(1024)}, f32[1600]{0:T(1024)}, f32[50]{0:T(128)}) all-reduce(f32[1600]{0:T(1024)S(1)} %get-tuple-element.147, f32[1600]{0:T(1024)S(1)} %copy-done.94, f32[1600]{0:T(1024)S(1)} %copy-done.93, ...), channel_id=1, replica_groups=mesh['zz'=4,'core'=2,'shard'=4] {'zz','core','shard'}, use_global_device_ids=true, to_apply=%region_29.30 | all-reduce | flops 6450 | bytes 51600 | tf_op jit(solution)/shard_map/psum | solution.py:354
  1675.4 28.3 %collective-permute-done.29 = bf16[800,800]{1,0:T(8,128)(2,1)S(1)} collective-permute-done((bf16[800,800]{1,0:T(8,128)(2,1)S(1)}, bf16[800,800]{1,0:T(8,128)(2,1)S(1)}, u32[]{:S(2)}, u32[]{:S(2)}) %collective-permute-start.29) | collective-permute-done | bytes 1280032 | tf_op jit(solution)/shard_map/ppermute | solution.py:54
  (474 shorter events, 301.7 us)
Async XLA Ops:
  7.2 65.0 %all-gather.7.cloned.1.call-start = ((), (), s32[]{:S(2)}) async-start(), calls=%async_computation.6 | async-start | bytes 9216000 | tf_op jit(solution)/shard_map/all_gather | solution.py:61
  16.0 199.8 %all-gather.9.cloned.1.call-start = ((), (), s32[]{:S(2)}) async-start(), calls=%async_computation.7 | async-start | bytes 23040000 | tf_op jit(solution)/shard_map/all_gather | solution.py:61
  19.5 315.7 %all-gather.11.cloned.1.call-start = ((), (), s32[]{:S(2)}) async-start(), calls=%async_computation.8 | async-start | bytes 11980800 | tf_op jit(solution)/shard_map/all_gather | solution.py:61
  20.7 329.5 %all-gather.13.cloned.1.call-start = ((), (), s32[]{:S(2)}) async-start(), calls=%async_computation.9 | async-start | bytes 5990400 | tf_op jit(solution)/shard_map/all_gather | solution.py:61
  22.9 409.8 %all-gather.15.cloned.1.call-start = ((), (), s32[]{:S(2)}) async-start(), calls=%async_computation.10 | async-start | bytes 8192000 | tf_op jit(solution)/shard_map/all_gather | solution.py:224
  80.2 43.0 %collective-permute-start = (bf16[512,640]{0,1:T(8,128)(2,1)S(1)}, bf16[512,640]{0,1:T(8,128)(2,1)}, u32[]{:S(2)}, u32[]{:S(2)}) collective-permute-start(bf16[512,640]{0,1:T(8,128)(2,1)S(1)} %slice.147), channel_id=1, source_target_pairs={{0,2},{1,3},{4,6},{5,7},{8,10},{9,11},{12,14},{13,15},{16,18},{17,... | collective-permute-start | bytes 1966088 | tf_op jit(solution)/shard_map/ppermute | solution.py:23
  83.9 39.4 %collective-permute-start.1 = (bf16[512,640]{0,1:T(8,128)(2,1)S(1)}, bf16[512,640]{0,1:T(8,128)(2,1)}, u32[]{:S(2)}, u32[]{:S(2)}) collective-permute-start(bf16[512,640]{0,1:T(8,128)(2,1)S(1)} %slice.147), channel_id=1, source_target_pairs={{0,1},{1,2},{2,3},{4,5},{5,6},{6,7},{8,9},{9,10},{10,11},{12,13},{... | collective-permute-start | bytes 1966088 | tf_op jit(solution)/shard_map/ppermute | solution.py:23
  91.6 23.3 %collective-permute-start.3 = (f32[50]{0:T(128)S(1)}, f32[50]{0:T(128)S(1)}, u32[]{:S(2)}, u32[]{:S(2)}) collective-permute-start(f32[50]{0:T(128)S(1)} %exponential_multiply_fusion.2), channel_id=1, source_target_pairs={{0,1},{1,2},{2,3},{4,5},{5,6},{6,7},{8,9},{9,10},{10,11},{12,13},{... | collective-permute-start | bytes 608 | tf_op jit(solution)/shard_map/ppermute | solution.py:23
  92.9 29.7 %collective-permute-start.5 = (f32[50]{0:T(128)S(1)}, f32[50]{0:T(128)}, u32[]{:S(2)}, u32[]{:S(2)}) collective-permute-start(f32[50]{0:T(128)S(1)} %exponential_multiply_fusion.2), channel_id=1, source_target_pairs={{0,2},{1,3},{4,6},{5,7},{8,10},{9,11},{12,14},{13,15},{16,18},{17,... | collective-permute-start | bytes 608 | tf_op jit(solution)/shard_map/ppermute | solution.py:23
  269.5 9.4 collective-permute-start.2
  270.9 28.6 %collective-permute-start.4 = (f32[50,64,16]{1,2,0:T(8,128)S(1)}, f32[50,64,16]{1,2,0:T(8,128)S(1)}, u32[]{:S(2)}, u32[]{:S(2)}) collective-permute-start(f32[50,64,16]{1,2,0:T(8,128)S(1)} %fusion.70), channel_id=1, source_target_pairs={{0,2},{1,3},{4,6},{5,7},{8,10},{9,11},{12,14},{13,15},{16,18},{17,... | collective-permute-start | bytes 614408 | tf_op jit(solution)/shard_map/ppermute | solution.py:23
  275.4 24.0 %collective-permute-start.6 = (f32[50,64,16]{1,2,0:T(8,128)S(1)}, f32[50,64,16]{1,2,0:T(8,128)S(1)}, u32[]{:S(2)}, u32[]{:S(2)}) collective-permute-start(f32[50,64,16]{1,2,0:T(8,128)S(1)} %fusion.70), channel_id=1, source_target_pairs={{0,3},{4,7},{8,11},{12,15},{16,19},{20,23},{24,27},{28,31}} | collective-permute-start | bytes 614408 | tf_op jit(solution)/shard_map/ppermute | solution.py:23
  359.8 146.7 %all-gather.17.cloned.1.call-start = ((), (), s32[]{:S(2)}) async-start(), calls=%async_computation.12 | async-start | bytes 8192000 | tf_op jit(solution)/shard_map/all_gather | solution.py:154
  360.4 272.8 %reduce-scatter.13.cloned.1.call-start = ((), (), s32[]{:S(2)}) async-start(), calls=%async_computation.13 | async-start | bytes 8192000 | tf_op jit(solution)/shard_map/reduce_scatter | solution.py:83
  560.6 852.1 %reduce-scatter.21.cloned.1.call-start = ((), (), s32[]{:S(2)}) async-start(), calls=%async_computation.17 | async-start | bytes 3584000
  560.7 424.0 %collective-permute-start.14 = (bf16[512,1600]{0,1:T(8,128)(2,1)}, bf16[512,1600]{0,1:T(8,128)(2,1)}, u32[]{:S(2)}, u32[]{:S(2)}) collective-permute-start(bf16[512,1600]{0,1:T(8,128)(2,1)} %fusion.43), channel_id=1, source_target_pairs={{0,4},{4,0},{1,5},{5,1},{2,6},{6,2},{3,7},{7,3},{8,12},{12,8},{9,1... | collective-permute-start | bytes 4915208 | tf_op jit(solution)/shard_map/ppermute | solution.py:27
  561.4 4.3 collective-permute-start.8
  562.7 5.2 collective-permute-start.10
  568.4 375.2 %collective-permute-start.31 = (bf16[512,1600]{0,1:T(8,128)(2,1)}, bf16[512,1600]{0,1:T(8,128)(2,1)}, u32[]{:S(2)}, u32[]{:S(2)}) collective-permute-start(bf16[512,1600]{0,1:T(8,128)(2,1)} %get-tuple-element.160), channel_id=1, source_target_pairs={{0,4},{4,0},{1,5},{5,1},{2,6},{6,2},{3,7},{7,3},{8,12},{12,8},{9,1... | collective-permute-start | bytes 4915208 | tf_op jit(solution)/shard_map/ppermute | solution.py:27
  680.1 253.6 %collective-permute-start.11 = (f32[50,64,16]{1,2,0:T(8,128)}, f32[50,64,16]{1,2,0:T(8,128)}, u32[]{:S(2)}, u32[]{:S(2)}) collective-permute-start(f32[50,64,16]{1,2,0:T(8,128)} %fusion.13), channel_id=1, source_target_pairs={{3,0},{7,4},{11,8},{15,12},{19,16},{23,20},{27,24},{31,28}} | collective-permute-start | bytes 614408 | tf_op jit(solution)/shard_map/ppermute | solution.py:23
  681.4 253.7 %collective-permute-start.7 = (f32[50,64,16]{1,2,0:T(8,128)}, f32[50,64,16]{1,2,0:T(8,128)}, u32[]{:S(2)}, u32[]{:S(2)}) collective-permute-start(f32[50,64,16]{1,2,0:T(8,128)} %fusion.13), channel_id=1, source_target_pairs={{1,0},{2,1},{3,2},{5,4},{6,5},{7,6},{9,8},{10,9},{11,10},{13,12},{... | collective-permute-start | bytes 614408 | tf_op jit(solution)/shard_map/ppermute | solution.py:23
  682.7 253.7 %collective-permute-start.9 = (f32[50,64,16]{1,2,0:T(8,128)}, f32[50,64,16]{1,2,0:T(8,128)}, u32[]{:S(2)}, u32[]{:S(2)}) collective-permute-start(f32[50,64,16]{1,2,0:T(8,128)} %fusion.13), channel_id=1, source_target_pairs={{2,0},{3,1},{6,4},{7,5},{10,8},{11,9},{14,12},{15,13},{18,16},{19,... | collective-permute-start | bytes 614408 | tf_op jit(solution)/shard_map/ppermute | solution.py:23
  933.7 35.0 %collective-permute-start.12 = (bf16[512,640]{0,1:T(8,128)(2,1)}, bf16[512,640]{0,1:T(8,128)(2,1)}, u32[]{:S(2)}, u32[]{:S(2)}) collective-permute-start(bf16[512,640]{0,1:T(8,128)(2,1)} %get-tuple-element.189), channel_id=1, source_target_pairs={{1,0},{2,1},{3,2},{5,4},{6,5},{7,6},{9,8},{10,9},{11,10},{13,12},{... | collective-permute-start | bytes 1966088 | tf_op jit(solution)/shard_map/ppermute | solution.py:23
  935.1 33.5 %collective-permute-start.13 = (bf16[512,640]{0,1:T(8,128)(2,1)}, bf16[512,640]{0,1:T(8,128)(2,1)}, u32[]{:S(2)}, u32[]{:S(2)}) collective-permute-start(bf16[512,640]{0,1:T(8,128)(2,1)} %get-tuple-element.190), channel_id=1, source_target_pairs={{2,0},{3,1},{6,4},{7,5},{10,8},{11,9},{14,12},{15,13},{18,16},{19,... | collective-permute-start | bytes 1966088 | tf_op jit(solution)/shard_map/ppermute | solution.py:23
  936.4 7.1 collective-permute-start.32
  951.2 479.7 %reduce-scatter.15.cloned.1.call-start = ((), (), s32[]{:S(2)}) async-start(), calls=%async_computation.14 | async-start | bytes 5120000 | tf_op jit(solution)/shard_map/reduce_scatter | solution.py:83
  978.7 6.0 collective-permute-start.15
  993.4 443.8 %reduce-scatter.19.cloned.1.call-start = ((), (), s32[]{:S(2)}) async-start(), calls=%async_computation.16 | async-start | bytes 12800000
  1003.6 7.0 collective-permute-start.20
  1025.4 516.9 %reduce-scatter.17.cloned.1.call-start = ((), (), s32[]{:S(2)}) async-start(), calls=%async_computation.15 | async-start | bytes 7168000 | tf_op jit(solution)/shard_map/reduce_scatter | solution.py:83
  1025.4 55.7 %collective-permute-start.25 = (bf16[512,3200]{1,0:T(8,128)(2,1)}, bf16[512,3200]{1,0:T(8,128)(2,1)S(1)}, u32[]{:S(2)}, u32[]{:S(2)}) collective-permute-start(bf16[512,3200]{1,0:T(8,128)(2,1)} %multiply_convert_fusion.8), channel_id=1, source_target_pairs={{0,4},{4,0},{1,5},{5,1},{2,6},{6,2},{3,7},{7,3},{8,12},{12,8},{9,1... | collective-permute-start | bytes 9830408 | tf_op jit(solution)/shard_map/ppermute | solution.py:27
  1041.1 35.3 %collective-permute-start.47 = (bf16[688,1600]{1,0:T(8,128)(2,1)S(1)}, bf16[688,1600]{1,0:T(8,128)(2,1)S(1)}, u32[]{:S(2)}, u32[]{:S(2)}) collective-permute-start(bf16[688,1600]{1,0:T(8,128)(2,1)S(1)} %constant_dynamic-slice_fusion), channel_id=1, source_target_pairs={{0,4},{4,0},{1,5},{5,1},{2,6},{6,2},{3,7},{7,3},{8,12},{12,8},{9,1... | collective-permute-start | bytes 6604808 | tf_op jit(solution)/shard_map/ppermute | solution.py:27
  1058.9 32.1 %collective-permute-start.42 = (bf16[800,1376]{1,0:T(8,128)(2,1)}, bf16[800,1376]{1,0:T(8,128)(2,1)}, u32[]{:S(2)}, u32[]{:S(2)}) collective-permute-start(bf16[800,1376]{1,0:T(8,128)(2,1)} %constant_dynamic-slice_fusion.1), channel_id=1, source_target_pairs={{0,4},{4,0},{1,5},{5,1},{2,6},{6,2},{3,7},{7,3},{8,12},{12,8},{9,1... | collective-permute-start | bytes 6604808 | tf_op jit(solution)/shard_map/ppermute | solution.py:27
  1073.6 7.5 collective-permute-start.26
  1076.3 19.2 %collective-permute-start.37 = (bf16[800,1376]{1,0:T(8,128)(2,1)}, bf16[800,1376]{1,0:T(8,128)(2,1)}, u32[]{:S(2)}, u32[]{:S(2)}) collective-permute-start(bf16[800,1376]{1,0:T(8,128)(2,1)} %constant_dynamic-slice_fusion.2), channel_id=1, source_target_pairs={{0,4},{4,0},{1,5},{5,1},{2,6},{6,2},{3,7},{7,3},{8,12},{12,8},{9,1... | collective-permute-start | bytes 6604808 | tf_op jit(solution)/shard_map/ppermute | solution.py:27
  1077.0 51.6 %collective-permute-start.48 = (bf16[688,1600]{1,0:T(8,128)(2,1)S(1)}, bf16[688,1600]{1,0:T(8,128)(2,1)}, u32[]{:S(2)}, u32[]{:S(2)}) collective-permute-start(bf16[688,1600]{1,0:T(8,128)(2,1)S(1)} %add_convert_fusion.5), channel_id=1, source_target_pairs={{0,8},{24,16},{1,9},{25,17},{2,10},{26,18},{3,11},{27,19},{4,12},{... | collective-permute-start | bytes 6604808 | tf_op jit(solution)/shard_map/ppermute | solution.py:50
  1090.9 490.1 %reduce-scatter.11.cloned.1.call-start = ((), (), s32[]{:S(2)}) async-start(), calls=%async_computation.11 | async-start | bytes 8192000 | tf_op jit(solution)/shard_map/reduce_scatter | solution.py:83
  1094.0 82.9 %collective-permute-start.43 = (bf16[800,1376]{1,0:T(8,128)(2,1)S(1)}, bf16[800,1376]{1,0:T(8,128)(2,1)S(1)}, u32[]{:S(2)}, u32[]{:S(2)}) collective-permute-start(bf16[800,1376]{1,0:T(8,128)(2,1)S(1)} %add_convert_fusion.8), channel_id=1, source_target_pairs={{0,8},{24,16},{1,9},{25,17},{2,10},{26,18},{3,11},{27,19},{4,12},{... | collective-permute-start | bytes 6604808 | tf_op jit(solution)/shard_map/ppermute | solution.py:50
  1097.7 127.5 %collective-permute-start.38 = (bf16[800,1376]{1,0:T(8,128)(2,1)S(1)}, bf16[800,1376]{1,0:T(8,128)(2,1)S(1)}, u32[]{:S(2)}, u32[]{:S(2)}) collective-permute-start(bf16[800,1376]{1,0:T(8,128)(2,1)S(1)} %add_convert_fusion.11), channel_id=1, source_target_pairs={{0,8},{24,16},{1,9},{25,17},{2,10},{26,18},{3,11},{27,19},{4,12},{... | collective-permute-start | bytes 6604808 | tf_op jit(solution)/shard_map/ppermute | solution.py:50
  1130.8 98.4 %collective-permute-start.49 = (bf16[688,1600]{1,0:T(8,128)(2,1)S(1)}, bf16[688,1600]{1,0:T(8,128)(2,1)S(1)}, u32[]{:S(2)}, u32[]{:S(2)}) collective-permute-start(bf16[688,1600]{1,0:T(8,128)(2,1)S(1)} %add_convert_fusion.4), channel_id=1, source_target_pairs={{8,16},{16,8},{9,17},{17,9},{10,18},{18,10},{11,19},{19,11},{12,20... | collective-permute-start | bytes 6604808 | tf_op jit(solution)/shard_map/ppermute | solution.py:52
  1178.9 52.3 %collective-permute-start.44 = (bf16[800,1376]{1,0:T(8,128)(2,1)}, bf16[800,1376]{1,0:T(8,128)(2,1)}, u32[]{:S(2)}, u32[]{:S(2)}) collective-permute-start(bf16[800,1376]{1,0:T(8,128)(2,1)} %add_convert_fusion.7), channel_id=1, source_target_pairs={{8,16},{16,8},{9,17},{17,9},{10,18},{18,10},{11,19},{19,11},{12,20... | collective-permute-start | bytes 6604808 | tf_op jit(solution)/shard_map/ppermute | solution.py:52
  1227.2 10.2 collective-permute-start.39
  1229.9 53.3 %collective-permute-start.50 = (bf16[688,1600]{1,0:T(8,128)(2,1)S(1)}, bf16[688,1600]{1,0:T(8,128)(2,1)}, u32[]{:S(2)}, u32[]{:S(2)}) collective-permute-start(bf16[688,1600]{1,0:T(8,128)(2,1)S(1)} %add_convert_fusion.3), channel_id=1, source_target_pairs={{8,0},{16,24},{9,1},{17,25},{10,2},{18,26},{11,3},{19,27},{12,4},{... | collective-permute-start | bytes 6604808 | tf_op jit(solution)/shard_map/ppermute | solution.py:54
  1236.1 95.4 %collective-permute-start.45 = (bf16[800,1376]{1,0:T(8,128)(2,1)}, bf16[800,1376]{1,0:T(8,128)(2,1)}, u32[]{:S(2)}, u32[]{:S(2)}) collective-permute-start(bf16[800,1376]{1,0:T(8,128)(2,1)} %add_convert_fusion.6), channel_id=1, source_target_pairs={{8,0},{16,24},{9,1},{17,25},{10,2},{18,26},{11,3},{19,27},{12,4},{... | collective-permute-start | bytes 6604808 | tf_op jit(solution)/shard_map/ppermute | solution.py:54
  1241.7 138.0 %collective-permute-start.40 = (bf16[800,1376]{1,0:T(8,128)(2,1)}, bf16[800,1376]{1,0:T(8,128)(2,1)}, u32[]{:S(2)}, u32[]{:S(2)}) collective-permute-start(bf16[800,1376]{1,0:T(8,128)(2,1)} %add_convert_fusion.9), channel_id=1, source_target_pairs={{8,0},{16,24},{9,1},{17,25},{10,2},{18,26},{11,3},{19,27},{12,4},{... | collective-permute-start | bytes 6604808 | tf_op jit(solution)/shard_map/ppermute | solution.py:54
  1285.3 99.8 %collective-permute-start.51 = (bf16[688,1600]{1,0:T(8,128)(2,1)S(1)}, bf16[688,1600]{1,0:T(8,128)(2,1)}, u32[]{:S(2)}, u32[]{:S(2)}) collective-permute-start(bf16[688,1600]{1,0:T(8,128)(2,1)S(1)} %broadcast_select_fusion.5), channel_id=1, source_target_pairs={{0,4},{4,0},{1,5},{5,1},{2,6},{6,2},{3,7},{7,3},{8,12},{12,8},{9,1... | collective-permute-start | bytes 6604808 | tf_op jit(solution)/shard_map/ppermute | solution.py:27
  1334.7 67.0 %collective-permute-start.46 = (bf16[800,1376]{1,0:T(8,128)(2,1)}, bf16[800,1376]{1,0:T(8,128)(2,1)}, u32[]{:S(2)}, u32[]{:S(2)}) collective-permute-start(bf16[800,1376]{1,0:T(8,128)(2,1)} %broadcast_select_fusion.8), channel_id=1, source_target_pairs={{0,4},{4,0},{1,5},{5,1},{2,6},{6,2},{3,7},{7,3},{8,12},{12,8},{9,1... | collective-permute-start | bytes 6604808 | tf_op jit(solution)/shard_map/ppermute | solution.py:27
  1383.0 21.4 %collective-permute-start.41 = (bf16[800,1376]{1,0:T(8,128)(2,1)}, bf16[800,1376]{1,0:T(8,128)(2,1)}, u32[]{:S(2)}, u32[]{:S(2)}) collective-permute-start(bf16[800,1376]{1,0:T(8,128)(2,1)} %broadcast_select_fusion.9), channel_id=1, source_target_pairs={{0,4},{4,0},{1,5},{5,1},{2,6},{6,2},{3,7},{7,3},{8,12},{12,8},{9,1... | collective-permute-start | bytes 6604808 | tf_op jit(solution)/shard_map/ppermute | solution.py:27
  1412.7 17.2 collective-permute-start.33
  1430.1 19.2 %collective-permute-start.34 = (bf16[400,800]{1,0:T(8,128)(2,1)S(1)}, bf16[400,800]{1,0:T(8,128)(2,1)S(1)}, u32[]{:S(2)}, u32[]{:S(2)}) collective-permute-start(bf16[400,800]{1,0:T(8,128)(2,1)S(1)} %add_convert_fusion.18), channel_id=1, source_target_pairs={{8,16},{16,8},{9,17},{17,9},{10,18},{18,10},{11,19},{19,11},{12,20... | collective-permute-start | bytes 1920008 | tf_op jit(solution)/shard_map/ppermute | solution.py:52
  1430.9 26.6 %collective-permute-start.16 = (bf16[400,1280]{1,0:T(8,128)(2,1)}, bf16[400,1280]{1,0:T(8,128)(2,1)}, u32[]{:S(2)}, u32[]{:S(2)}) collective-permute-start(bf16[400,1280]{1,0:T(8,128)(2,1)} %reduce-scatter.15.cloned.1.call-done), channel_id=1, source_target_pairs={{0,8},{24,16},{1,9},{25,17},{2,10},{26,18},{3,11},{27,19},{4,12},{... | collective-permute-start | bytes 3072008 | tf_op jit(solution)/shard_map/ppermute | solution.py:50
  1437.2 75.1 %collective-permute-start.21 = (bf16[400,3200]{1,0:T(8,128)(2,1)}, bf16[400,3200]{1,0:T(8,128)(2,1)S(1)}, u32[]{:S(2)}, u32[]{:S(2)}) collective-permute-start(bf16[400,3200]{1,0:T(8,128)(2,1)} %reduce-scatter.19.cloned.1.call-done), channel_id=1, source_target_pairs={{0,8},{24,16},{1,9},{25,17},{2,10},{26,18},{3,11},{27,19},{4,12},{... | collective-permute-start | bytes 7680008 | tf_op jit(solution)/shard_map/ppermute | solution.py:50
  1449.5 88.7 %collective-permute-start.35 = (bf16[400,800]{1,0:T(8,128)(2,1)S(1)}, bf16[400,800]{1,0:T(8,128)(2,1)}, u32[]{:S(2)}, u32[]{:S(2)}) collective-permute-start(bf16[400,800]{1,0:T(8,128)(2,1)S(1)} %add_convert_fusion.17), channel_id=1, source_target_pairs={{8,0},{16,24},{9,1},{17,25},{10,2},{18,26},{11,3},{19,27},{12,4},{... | collective-permute-start | bytes 1920008 | tf_op jit(solution)/shard_map/ppermute | solution.py:54
  1459.1 87.5 %collective-permute-start.17 = (bf16[400,1280]{1,0:T(8,128)(2,1)S(1)}, bf16[400,1280]{1,0:T(8,128)(2,1)}, u32[]{:S(2)}, u32[]{:S(2)}) collective-permute-start(bf16[400,1280]{1,0:T(8,128)(2,1)S(1)} %add_convert_fusion.16), channel_id=1, source_target_pairs={{8,16},{16,8},{9,17},{17,9},{10,18},{18,10},{11,19},{19,11},{12,20... | collective-permute-start | bytes 3072008 | tf_op jit(solution)/shard_map/ppermute | solution.py:52
  1514.5 35.3 %collective-permute-start.22 = (bf16[400,3200]{1,0:T(8,128)(2,1)}, bf16[400,3200]{1,0:T(8,128)(2,1)}, u32[]{:S(2)}, u32[]{:S(2)}) collective-permute-start(bf16[400,3200]{1,0:T(8,128)(2,1)} %add_convert_fusion.2), channel_id=1, source_target_pairs={{8,16},{16,8},{9,17},{17,9},{10,18},{18,10},{11,19},{19,11},{12,20... | collective-permute-start | bytes 7680008 | tf_op jit(solution)/shard_map/ppermute | solution.py:52
  1540.3 122.2 %collective-permute-start.36 = (bf16[400,800]{1,0:T(8,128)(2,1)}, bf16[400,800]{1,0:T(8,128)(2,1)S(1)}, u32[]{:S(2)}, u32[]{:S(2)}) collective-permute-start(bf16[400,800]{1,0:T(8,128)(2,1)} %broadcast_select_fusion.26), channel_id=1, source_target_pairs={{0,4},{4,0},{1,5},{5,1},{2,6},{6,2},{3,7},{7,3},{8,12},{12,8},{9,1... | collective-permute-start | bytes 1920008 | tf_op jit(solution)/shard_map/ppermute | solution.py:27
  1542.2 35.4 %collective-permute-start.27 = (bf16[800,800]{1,0:T(8,128)(2,1)}, bf16[800,800]{1,0:T(8,128)(2,1)S(1)}, u32[]{:S(2)}, u32[]{:S(2)}) collective-permute-start(bf16[800,800]{1,0:T(8,128)(2,1)} %reduce-scatter.17.cloned.1.call-done), channel_id=1, source_target_pairs={{0,8},{24,16},{1,9},{25,17},{2,10},{26,18},{3,11},{27,19},{4,12},{... | collective-permute-start | bytes 3840008 | tf_op jit(solution)/shard_map/ppermute | solution.py:50
  1548.4 115.4 %collective-permute-start.18 = (bf16[400,1280]{1,0:T(8,128)(2,1)S(1)}, bf16[400,1280]{1,0:T(8,128)(2,1)}, u32[]{:S(2)}, u32[]{:S(2)}) collective-permute-start(bf16[400,1280]{1,0:T(8,128)(2,1)S(1)} %add_convert_fusion.15), channel_id=1, source_target_pairs={{8,0},{16,24},{9,1},{17,25},{10,2},{18,26},{11,3},{19,27},{12,4},{... | collective-permute-start | bytes 3072008 | tf_op jit(solution)/shard_map/ppermute | solution.py:54
  1554.4 115.7 %collective-permute-start.23 = (bf16[400,3200]{1,0:T(8,128)(2,1)}, bf16[400,3200]{1,0:T(8,128)(2,1)}, u32[]{:S(2)}, u32[]{:S(2)}) collective-permute-start(bf16[400,3200]{1,0:T(8,128)(2,1)} %add_convert_fusion.1), channel_id=1, source_target_pairs={{8,0},{16,24},{9,1},{17,25},{10,2},{18,26},{11,3},{19,27},{12,4},{... | collective-permute-start | bytes 7680008 | tf_op jit(solution)/shard_map/ppermute | solution.py:54
  1579.1 87.5 %collective-permute-start.28 = (bf16[800,800]{1,0:T(8,128)(2,1)}, bf16[800,800]{1,0:T(8,128)(2,1)}, u32[]{:S(2)}, u32[]{:S(2)}) collective-permute-start(bf16[800,800]{1,0:T(8,128)(2,1)} %add_convert_fusion.14), channel_id=1, source_target_pairs={{8,16},{16,8},{9,17},{17,9},{10,18},{18,10},{11,19},{19,11},{12,20... | collective-permute-start | bytes 3840008 | tf_op jit(solution)/shard_map/ppermute | solution.py:52
  1665.1 40.7 %collective-permute-start.19 = (bf16[400,1280]{1,0:T(8,128)(2,1)S(1)}, bf16[400,1280]{1,0:T(8,128)(2,1)S(1)}, u32[]{:S(2)}, u32[]{:S(2)}) collective-permute-start(bf16[400,1280]{1,0:T(8,128)(2,1)S(1)} %broadcast_select_fusion.19), channel_id=1, source_target_pairs={{0,4},{4,0},{1,5},{5,1},{2,6},{6,2},{3,7},{7,3},{8,12},{12,8},{9,1... | collective-permute-start | bytes 3072008 | tf_op jit(solution)/shard_map/ppermute | solution.py:27
  1668.8 34.9 %collective-permute-start.29 = (bf16[800,800]{1,0:T(8,128)(2,1)S(1)}, bf16[800,800]{1,0:T(8,128)(2,1)S(1)}, u32[]{:S(2)}, u32[]{:S(2)}) collective-permute-start(bf16[800,800]{1,0:T(8,128)(2,1)S(1)} %add_convert_fusion.13), channel_id=1, source_target_pairs={{8,0},{16,24},{9,1},{17,25},{10,2},{18,26},{11,3},{19,27},{12,4},{... | collective-permute-start | bytes 3840008 | tf_op jit(solution)/shard_map/ppermute | solution.py:54
  1673.6 42.6 %collective-permute-start.24 = (bf16[400,3200]{1,0:T(8,128)(2,1)}, bf16[400,3200]{1,0:T(8,128)(2,1)}, u32[]{:S(2)}, u32[]{:S(2)}) collective-permute-start(bf16[400,3200]{1,0:T(8,128)(2,1)} %broadcast_select_fusion.2), channel_id=1, source_target_pairs={{0,4},{4,0},{1,5},{5,1},{2,6},{6,2},{3,7},{7,3},{8,12},{12,8},{9,1... | collective-permute-start | bytes 7680008 | tf_op jit(solution)/shard_map/ppermute | solution.py:27
  1705.0 6.0 collective-permute-start.30
  (105 other events, 2790.3 us)
Sparse Core Ops, SparseCore 0:
  16.1 56.0 all-gather.6
  74.7 130.8 all-gather.8
  208.0 63.9 all-gather.10
  273.7 51.6 all-gather.12
  359.9 72.6 all-gather.14
  434.3 72.1 all-gather.16
  560.7 72.4 reduce-scatter.12
  951.3 51.1 reduce-scatter.20
  1006.0 51.8 reduce-scatter.14
  1061.6 121.0 reduce-scatter.18
  1186.0 65.8 reduce-scatter.16
  1303.6 78.5 reduce-scatter.10

commit v2 on v1

v2 whole, which is shorter than its diff:
```python
import jax
import jax.numpy as jnp
from jax import lax
from jax.experimental import pallas as pl
from jax.experimental.pallas import tpu as pltpu
from jax.sharding import PartitionSpec as P

HEADS = 25
KV_HEADS = 5
HEAD_DIM = 64
INNER = 3200
STATE = 16
WINDOW = 1024
MAMBA_DIM = 64
MAMBA_HEADS = 50
PAIRS = MAMBA_HEADS // 2
TILE = 2 * MAMBA_DIM
PER = 5
GROUPS = HEADS // KV_HEADS
PAIR_WIDTH = 2 * KV_HEADS * HEAD_DIM


EPSILON = 1e-05


def moved(block, axis, distance):
    devices = range(lax.axis_size(axis))
    route = [(i - distance, i) for i in devices if i - distance in devices]
    return lax.ppermute(block, axis, route)


def swapped(block):
    return lax.ppermute(block, "core", [(0, 1), (1, 0)])


def pick(first, second, core):
    return jnp.where(core == 0, first, second)


def state_from(local, carry, sign):
    length = lax.axis_size("shard")
    total = moved(local, "shard", sign)
    product = None
    for distance in range(2, length):
        between = moved(carry, "shard", sign * (distance - 1))
        product = between if product is None else product * between
        total = total + product * moved(local, "shard", sign * distance)
    return total


def after(value, *others):
    return lax.optimization_barrier((value, *others))[0]


def add_low(first, second):
    return (first.astype(jnp.float32) + second.astype(jnp.float32)).astype(jnp.bfloat16)


class ChipSum:
    routes = ([(0, 1), (3, 2)], [(1, 2), (2, 1)], [(1, 0), (2, 3)])

    def __init__(self, part):
        self.line = lax.axis_size("zz") == 4
        self.part = part
        self.step = 0

    def send(self):
        if self.line:
            return lax.ppermute(self.part, "zz", self.routes[self.step])
        return lax.psum(self.part, "zz") if self.step == 2 else self.part

    def take(self, arrived):
        if self.step == 2:
            place = lax.axis_index("zz")
            inner = (place == 1) | (place == 2)
            self.part = jnp.where(inner, self.part, arrived) if self.line else arrived
        elif self.line:
            self.part = add_low(self.part, arrived)
        self.step += 1

    def total(self):
        while self.step < 3:
            self.take(self.send())
        return self.part


def advance(value, sums, later=()):
    kept = lax.optimization_barrier(
        (value, tuple(s.send() for s in sums), tuple(s.part for s in sums), tuple(s.part for s in later))
    )
    for s, part in zip(later, kept[3]):
        s.part = part
    for s, arrived, part in zip(sums, kept[1], kept[2]):
        s.part = part
        s.take(arrived)
    return kept[0]


def gathered(weight, core):
    rows = weight.shape[0] // 2
    half = lax.dynamic_slice_in_dim(weight, core * rows, rows, 0)
    return lax.all_gather(half, ("shard", "core"), axis=0, tiled=True)


def core_half(part, core):
    rows = part.shape[0] // 2
    mine = lax.dynamic_slice_in_dim(part, core * rows, rows, 0)
    other = lax.dynamic_slice_in_dim(part, (1 - core) * rows, rows, 0)
    return (mine.astype(jnp.float32) + swapped(other).astype(jnp.float32)).astype(jnp.bfloat16)


def both_halves(mine, core, axis):
    other = swapped(mine)
    return jnp.concatenate([pick(mine, other, core), pick(other, mine, core)], axis).astype(jnp.float32)


def both_cores(full, core):
    columns = full.shape[1] // 2
    first, second = full[:, :columns], full[:, columns:]
    return jnp.concatenate([pick(first, second, core), swapped(pick(second, first, core))], 0)


def scattered(part, axis=0):
    return lax.psum_scatter(part.astype(jnp.bfloat16), "shard", scatter_dimension=axis, tiled=True)


def project(left, right):
    return jnp.dot(left, right, preferred_element_type=jnp.float32)


def left_product(left, right):
    return lax.dot_general(
        left, right, (((0,), (0,)), ((), ())), preferred_element_type=jnp.float32
    )


def right_product(left, right):
    return lax.dot_general(
        left, right, (((1,), (1,)), ((), ())), preferred_element_type=jnp.float32
    )


def inverse_rms(values):
    return lax.rsqrt(jnp.mean(values * values, axis=-1, keepdims=True) + EPSILON)


def rms_back(incoming, normed, factor):
    return factor * (incoming - normed * jnp.mean(incoming * normed, axis=-1, keepdims=True))


def silu_slope(values):
    sigma = jax.nn.sigmoid(values)
    return sigma * (1.0 + values * (1.0 - sigma))


def sum_over_axis(values, axis):
    size = lax.axis_size(axis)
    distance = 1
    while distance < size:
        values = values + lax.ppermute(values, axis, [(i, i ^ distance) for i in range(size)])
        distance *= 2
    return values


def pair_rows(values):
    return values.T.reshape(PAIRS, 2, values.shape[0])


def head_lanes(values):
    return jnp.repeat(values, MAMBA_DIM)[None]


def contract(left, right, left_axis, right_axis):
    return lax.dot_general(left, right, (((left_axis,), (right_axis,)), ((), ())), preferred_element_type=jnp.float32)

def allowed_bias(low, start, keys, rows):
    key = start + lax.broadcasted_iota(jnp.int32, (keys, rows), 0)
    query = start + lax.broadcasted_iota(jnp.int32, (keys, rows), 1)
    return jnp.where((key >= low) & (key <= query + WINDOW), 0.0, -1e30)

def attend_kernel(low_ref, query_ref, pair_ref, out_ref, logsum_ref, heads, first, second, mixed, bias):
    rows = query_ref.shape[0]
    keys = WINDOW + rows
    start = pl.multiple_of(pl.program_id(0) * rows, rows)
    bias[...] = allowed_bias(low_ref[...], start, keys, rows)
    scale = HEAD_DIM**-0.5
    for head in range(HEADS):
        heads[head] = query_ref[:, head * HEAD_DIM : (head + 1) * HEAD_DIM] * jnp.bfloat16(scale)
    for group in range(KV_HEADS):
        both = pair_ref[pl.ds(start, keys), group * 2 * HEAD_DIM : (group + 1) * 2 * HEAD_DIM]
        first[group] = both[:, :HEAD_DIM]
        second[group] = both.T[HEAD_DIM:]

    def one(head, carry):
        group = head // (HEADS // KV_HEADS)
        scores = contract(first[group], heads[head], 1, 1) + bias[...]
        peak = jnp.max(scores, axis=0, keepdims=True)
        weights = jnp.exp(scores - peak)
        total = jnp.sum(weights, axis=0, keepdims=True)
        out = contract(second[group], weights.astype(jnp.bfloat16), 1, 0)
        mixed[head] = out * (1.0 / total)
        logsum_ref[pl.ds(head, 1)] = (peak + jnp.log(total))[None]
        return carry

    lax.fori_loop(0, HEADS, one, 0, unroll=5)
    for head in range(0, HEADS - 1, 2):
        out_ref[:, head * HEAD_DIM : (head + 2) * HEAD_DIM] = jnp.concatenate([mixed[head], mixed[head + 1]], 0).T
    out_ref[:, (HEADS - 1) * HEAD_DIM :] = mixed[HEADS - 1].T

def attend(low, query, pair):
    count = query.shape[0]
    span = pair.shape[0]
    rows = min(256, count)
    keys = WINDOW + rows
    return pl.pallas_call(
        attend_kernel,
        grid=(count // rows,),
        in_specs=[
            pl.BlockSpec((1, rows), lambda i: (0, i)),
            pl.BlockSpec((rows, HEADS * HEAD_DIM), lambda i: (i, 0)),
            pl.BlockSpec((span, 2 * KV_HEADS * HEAD_DIM), lambda i: (0, 0), pipeline_mode=pl.Buffered(1)),
        ],
        out_specs=[
            pl.BlockSpec((rows, HEADS * HEAD_DIM), lambda i: (i, 0)),
            pl.BlockSpec((HEADS, 1, rows), lambda i: (0, 0, i)),
        ],
        out_shape=[
            jax.ShapeDtypeStruct((count, HEADS * HEAD_DIM), jnp.float32),
            jax.ShapeDtypeStruct((HEADS, 1, count), jnp.float32),
        ],
        scratch_shapes=[
            pltpu.VMEM((HEADS, rows, HEAD_DIM), jnp.bfloat16),
            pltpu.VMEM((KV_HEADS, keys, HEAD_DIM), jnp.bfloat16),
            pltpu.VMEM((KV_HEADS, HEAD_DIM, keys), jnp.bfloat16),
            pltpu.VMEM((HEADS, HEAD_DIM, rows), jnp.float32),
            pltpu.VMEM((keys, rows), jnp.float32),
        ],
        compiler_params=pltpu.CompilerParams(vmem_limit_bytes=56 * 2**20),
        name="attend",
    )(low, query, pair)

def attend_back_kernel(low_ref, query_ref, pair_ref, out_ref, logsum_ref, given_ref, d_query_ref, d_pair_ref,
                       heads, given, deltas, first, first_t, second, bias, d_heads):
    rows = query_ref.shape[0]
    keys = WINDOW + rows
    step = pl.program_id(0)
    start = pl.multiple_of(step * rows, rows)
    bias[...] = allowed_bias(low_ref[...], start, keys, rows)
    scale = HEAD_DIM**-0.5

    @pl.when(step == 0)
    def _():
        d_pair_ref[...] = jnp.zeros_like(d_pair_ref)

    for head in range(HEADS):
        span = slice(head * HEAD_DIM, (head + 1) * HEAD_DIM)
        heads[head] = query_ref[:, span] * jnp.bfloat16(scale)
        given[head] = given_ref[:, span]
        product = given_ref[:, span].astype(jnp.float32) * out_ref[:, span]
        deltas[head] = jnp.sum(product.T, axis=0, keepdims=True)
    for group in range(KV_HEADS):
        both = pair_ref[pl.ds(start, keys), group * 2 * HEAD_DIM : (group + 1) * 2 * HEAD_DIM]
        first[group] = both[:, :HEAD_DIM]
        second[group] = both[:, HEAD_DIM:]
        first_t[group] = both.T[:HEAD_DIM]

    groups = HEADS // KV_HEADS

    for group in range(KV_HEADS):
        def one(index, carry):
            d_first, d_second = carry
            head = group * groups + index
            scores = contract(first[group], heads[head], 1, 1) + bias[...]
            probs = jnp.exp(scores - logsum_ref[head])
            d_probs = contract(second[group], given[head], 1, 1)
            d_scores = (probs * (d_probs - deltas[head])).astype(jnp.bfloat16)
            d_heads[head] = contract(first_t[group], d_scores, 1, 0)
            d_first = d_first + contract(d_scores, heads[head], 1, 0)
            d_second = d_second + contract(probs.astype(jnp.bfloat16), given[head], 1, 0)
            return d_first, d_second

        zero = jnp.zeros((keys, HEAD_DIM), jnp.float32)
        d_first, d_second = lax.fori_loop(0, groups, one, (zero, zero), unroll=True)
        span = slice(group * 2 * HEAD_DIM, (group + 1) * 2 * HEAD_DIM)
        d_pair_ref[pl.ds(start, keys), span] += jnp.concatenate([d_first, d_second], 1)
    for head in range(0, HEADS - 1, 2):
        d_query_ref[:, head * HEAD_DIM : (head + 2) * HEAD_DIM] = (
            (jnp.concatenate([d_heads[head], d_heads[head + 1]], 0) * scale).T.astype(jnp.bfloat16)
        )
    d_query_ref[:, (HEADS - 1) * HEAD_DIM :] = (d_heads[HEADS - 1] * scale).T.astype(jnp.bfloat16)

def attend_back(low, query, pair, out, logsum, given):
    count = query.shape[0]
    span = pair.shape[0]
    rows = min(256, count)
    keys = WINDOW + rows
    wide = HEADS * HEAD_DIM
    row = pl.BlockSpec((rows, wide), lambda i: (i, 0))
    whole = pl.BlockSpec((span, 2 * KV_HEADS * HEAD_DIM), lambda i: (0, 0), pipeline_mode=pl.Buffered(1))
    return pl.pallas_call(
        attend_back_kernel,
        grid=(count // rows,),
        in_specs=[
            pl.BlockSpec((1, rows), lambda i: (0, i)),
            row,
            whole,
            row,
            pl.BlockSpec((HEADS, 1, rows), lambda i: (0, 0, i)),
            row,
        ],
        out_specs=[row, pl.BlockSpec((span, 2 * KV_HEADS * HEAD_DIM), lambda i: (0, 0))],
        out_shape=[
            jax.ShapeDtypeStruct((count, wide), jnp.bfloat16),
            jax.ShapeDtypeStruct((span, 2 * KV_HEADS * HEAD_DIM), jnp.float32),
        ],
        scratch_shapes=[
            pltpu.VMEM((HEADS, rows, HEAD_DIM), jnp.bfloat16),
            pltpu.VMEM((HEADS, rows, HEAD_DIM), jnp.bfloat16),
            pltpu.VMEM((HEADS, 1, rows), jnp.float32),
            pltpu.VMEM((KV_HEADS, keys, HEAD_DIM), jnp.bfloat16),
            pltpu.VMEM((KV_HEADS, HEAD_DIM, keys), jnp.bfloat16),
            pltpu.VMEM((KV_HEADS, keys, HEAD_DIM), jnp.bfloat16),
            pltpu.VMEM((keys, rows), jnp.float32),
            pltpu.VMEM((HEADS, HEAD_DIM, rows), jnp.float32),
        ],
        compiler_params=pltpu.CompilerParams(vmem_limit_bytes=58 * 2**20),
        name="attend_back",
    )(low, query, pair, out, logsum, given)


def contract_split(left, right, right_axis=0):
    high = right.astype(jnp.bfloat16)
    rest = (right - high.astype(jnp.float32)).astype(jnp.bfloat16)
    return contract(left, high, 1, right_axis) + contract(left, rest, 1, right_axis)

def spread_lanes(rows):
    high = rows.astype(jnp.bfloat16).astype(jnp.float32)
    rest = rows - high
    middle = rest.astype(jnp.bfloat16).astype(jnp.float32)
    parts = jnp.concatenate([high, middle, rest - middle], 0).astype(jnp.bfloat16)
    row = lax.broadcasted_iota(jnp.int32, (6, TILE), 0) % 2
    lane = lax.broadcasted_iota(jnp.int32, (6, TILE), 1) // MAMBA_DIM
    return contract(parts, jnp.where(row == lane, 1.0, 0.0).astype(jnp.bfloat16), 0, 0)

def over_pairs(one, unroll):
    def step(pair, carry):
        one(pair, pl.ds(pl.multiple_of(pair * TILE, TILE), TILE))
        return carry

    lax.fori_loop(0, PER, step, 0, unroll=unroll)


def head_rows(values):
    row = lax.broadcasted_iota(jnp.int32, (8, TILE), 0)
    lane = lax.broadcasted_iota(jnp.int32, (8, TILE), 1) // MAMBA_DIM
    ones = jnp.where(row == lane, 1.0, 0.0).astype(jnp.bfloat16)
    return contract_split(ones, values, 1)[:2]

def drive_kernel(signal_ref, step_ref, tail_ref, writer_ref, drive_ref, local_ref):
    def one(pair, lane):
        drive = (signal_ref[:, lane] * spread_lanes(step_ref[pair])).astype(jnp.bfloat16)
        drive_ref[:, lane] = drive
        weighted = drive.astype(jnp.float32) * spread_lanes(tail_ref[pair])
        local_ref[:, lane] = contract_split(writer_ref[...], weighted)

    over_pairs(one, True)

def pair_block(count):
    return pl.BlockSpec((PER, 2, count), lambda p: (p, 0, 0))

def lanes(rows):
    return pl.BlockSpec((rows, PER * TILE), lambda p: (0, p))

def fixed(rows, columns):
    return pl.BlockSpec((rows, columns), lambda p: (0, 0))

def make_drive(signal, step_rows, tail_rows, writer):
    count = signal.shape[0]
    return pl.pallas_call(
        drive_kernel,
        grid=(PAIRS // PER,),
        in_specs=[lanes(count), pair_block(count), pair_block(count), fixed(STATE, count)],
        out_specs=[lanes(count), lanes(STATE)],
        out_shape=[jax.ShapeDtypeStruct((count, INNER), jnp.bfloat16), jax.ShapeDtypeStruct((STATE, INNER), jnp.float32)],
        name="make_drive",
    )(signal, step_rows, tail_rows, writer)

def mix_kernel(drive_ref, cumul_ref, enter_ref, gram_ref, bias_ref, reader_ref, state_ref, out_ref):
    count = drive_ref.shape[0]

    def one(pair, lane):
        cumul = cumul_ref[pair]
        columns = cumul.T
        drive = drive_ref[:, lane]
        through = contract_split(reader_ref[...], state_ref[:, lane])
        carried = through * spread_lanes(enter_ref[pair])
        for first in range(0, count, TILE):
            width = first + TILE
            rows = slice(first, width)
            halves = []
            for head in range(2):
                spread = columns[rows, head : head + 1] - cumul[head : head + 1, :width]
                decay = jnp.exp(spread + bias_ref[rows, :width])
                mixing = (gram_ref[rows, :width] * decay).astype(jnp.bfloat16)
                halves.append(contract(mixing, drive[:width, head * MAMBA_DIM : (head + 1) * MAMBA_DIM], 1, 0))
            out_ref[rows, lane] = jnp.concatenate(halves, 1) + carried[rows]

    over_pairs(one, False)

def mix(drive, cumul_rows, enter_rows, gram, bias, reader, state):
    count = drive.shape[0]
    return pl.pallas_call(
        mix_kernel,
        grid=(PAIRS // PER,),
        in_specs=[lanes(count), pair_block(count), pair_block(count), fixed(count, count), fixed(count, count), fixed(count, STATE), lanes(STATE)],
        out_specs=lanes(count),
        out_shape=jax.ShapeDtypeStruct((count, INNER), jnp.float32),
        compiler_params=pltpu.CompilerParams(vmem_limit_bytes=40 * 2**20),
        name="mix",
    )(drive, cumul_rows, enter_rows, gram, bias, reader, state)

def leave_kernel(d_mixed_ref, enter_ref, reader_ref, out_ref):
    def one(pair, lane):
        weighted = d_mixed_ref[:, lane].astype(jnp.float32) * spread_lanes(enter_ref[pair])
        out_ref[:, lane] = contract_split(reader_ref[...], weighted)

    over_pairs(one, True)

def leave_back(d_mixed, enter_rows, reader):
    count = d_mixed.shape[0]
    return pl.pallas_call(
        leave_kernel,
        grid=(PAIRS // PER,),
        in_specs=[lanes(count), pair_block(count), fixed(STATE, count)],
        out_specs=lanes(STATE),
        out_shape=jax.ShapeDtypeStruct((STATE, INNER), jnp.float32),
        name="leave_back",
    )(d_mixed, enter_rows, reader)

def mix_back_kernel(d_mixed_ref, mixed_ref, drive_ref, signal_ref, step_ref, cumul_ref, enter_ref, tail_ref, gram_ref, bias_ref,
                    writer_ref, state_ref, d_state_ref,
                    d_signal_ref, d_gram_ref, d_reader_ref, d_writer_ref, stats_ref, sums_ref):
    count = drive_ref.shape[0]

    @pl.when(pl.program_id(0) == 0)
    def _():
        d_gram_ref[...] = jnp.zeros_like(d_gram_ref)
        d_reader_ref[...] = jnp.zeros_like(d_reader_ref)
        d_writer_ref[...] = jnp.zeros_like(d_writer_ref)

    def one(pair, lane):
        cumul = cumul_ref[pair]
        columns = cumul.T
        state, d_state = state_ref[:, lane], d_state_ref[:, lane]
        given = d_mixed_ref[:, lane]
        d_mixed = given.astype(jnp.float32)
        drive_low = drive_ref[:, lane]
        drive = drive_low.astype(jnp.float32)
        entered = (d_mixed * spread_lanes(enter_ref[pair])).astype(jnp.bfloat16)
        d_reader_ref[...] += contract(entered, state.astype(jnp.bfloat16), 1, 1)
        written = contract_split(writer_ref[...], d_state)
        tail = spread_lanes(tail_ref[pair])
        d_writer_ref[...] += contract((drive * tail).astype(jnp.bfloat16), d_state.astype(jnp.bfloat16), 1, 1)
        d_from_tail = written * tail
        carried = jnp.sum(d_state * state, axis=0, keepdims=True)
        left = jnp.sum(d_from_tail * drive, axis=0, keepdims=True)
        sums_ref[pair] = jnp.concatenate([carried, left], 0)
        pieces = []
        for first in range(0, count, TILE):
            rows = slice(first, first + TILE)
            after = slice(first, count)
            halves = []
            for head in range(2):
                part = slice(head * MAMBA_DIM, (head + 1) * MAMBA_DIM)
                spread = cumul[head : head + 1, after] - columns[rows, head : head + 1]
                decay = jnp.exp(spread + bias_ref[rows, after])
                mixing = (gram_ref[rows, after] * decay).astype(jnp.bfloat16)
                d_mixing = contract(drive_low[rows, part], given[after, part], 1, 1)
                d_mixing = d_mixing.astype(jnp.bfloat16).astype(jnp.float32)
                d_gram_ref[rows, after] += d_mixing * decay
                halves.append(contract(mixing, given[after, part], 1, 0))
            pieces.append(jnp.concatenate(halves, 1))
        d_drive = jnp.concatenate(pieces, 0) + d_from_tail
        d_drive_low = d_drive.astype(jnp.bfloat16).astype(jnp.float32)
        d_signal_ref[:, lane] = (d_drive_low * spread_lanes(step_ref[pair])).astype(jnp.bfloat16)
        stats_ref[pair] = jnp.concatenate(
            [head_rows(d_mixed * mixed_ref[:, lane] - drive * d_drive), head_rows(d_drive_low * signal_ref[:, lane])], 0
        )

    over_pairs(one, False)

def mix_back(d_mixed, mixed, drive, signal, step_rows, cumul_rows, enter_rows, tail_rows, gram_t, bias_t, writer, state, d_state):
    count = drive.shape[0]
    rows = pair_block(count)
    return pl.pallas_call(
        mix_back_kernel,
        grid=(PAIRS // PER,),
        in_specs=[lanes(count), lanes(count), lanes(count), lanes(count), rows, rows, rows, rows, fixed(count, count), fixed(count, count),
                  fixed(count, STATE), lanes(STATE), lanes(STATE)],
        out_specs=[lanes(count), fixed(count, count), fixed(count, STATE), fixed(count, STATE),
                   pl.BlockSpec((PER, 4, count), lambda p: (p, 0, 0)), pl.BlockSpec((PER, 2, TILE), lambda p: (p, 0, 0))],
        out_shape=[jax.ShapeDtypeStruct((count, INNER), jnp.bfloat16), jax.ShapeDtypeStruct((count, count), jnp.float32),
                   jax.ShapeDtypeStruct((count, STATE), jnp.float32), jax.ShapeDtypeStruct((count, STATE), jnp.float32),
                   jax.ShapeDtypeStruct((PAIRS, 4, count), jnp.float32), jax.ShapeDtypeStruct((PAIRS, 2, TILE), jnp.float32)],
        compiler_params=pltpu.CompilerParams(vmem_limit_bytes=48 * 2**20),
        name="mix_back",
    )(d_mixed, mixed, drive, signal, step_rows, cumul_rows, enter_rows, tail_rows, gram_t, bias_t, writer, state, d_state)


def body(
    tokens,
    cotangent,
    doc_start,
    query_weight,
    key_weight,
    value_weight,
    inner_weight,
    select_weight,
    step_weight,
    mamba_out,
    mixer_out,
    gate_weight,
    up_weight,
    down_weight,
    attention_gain,
    attention_scale,
    mamba_scale,
    feed_gain,
    decay_rate,
):
    count = tokens.shape[0]
    core = lax.axis_index("core")
    begin = lax.axis_index(("zz", "core", "shard")) * count
    place = begin + jnp.arange(count, dtype=jnp.int32)
    blocks = (WINDOW + count - 1) // count
    rows = query_weight.shape[0]
    pair_weight = jnp.concatenate(
        [key_weight.reshape(rows, KV_HEADS, HEAD_DIM), value_weight.reshape(rows, KV_HEADS, HEAD_DIM)], 2
    ).reshape(rows, PAIR_WIDTH)
    wide = query_weight.shape[1]
    lead = 2 * STATE + MAMBA_HEADS
    front_weight = jnp.concatenate(
        [inner_weight, jnp.pad(jnp.concatenate([select_weight, step_weight], 1), ((0, 0), (0, 128 - lead)))], 1
    )
    spare = -(wide + PAIR_WIDTH) % 256
    query_pair_full = gathered(
        jnp.pad(jnp.concatenate([query_weight, pair_weight], 1), ((0, 0), (0, spare))), core
    )
    inputs = tokens.astype(jnp.float32)
    scale_one = inverse_rms(inputs)
    unit_one = inputs * scale_one
    normed = (unit_one * attention_gain).astype(jnp.bfloat16)
    normed_both = jnp.concatenate([normed, swapped(normed)], 0)
    query_pair = project(normed, query_pair_full).astype(jnp.bfloat16)
    front_full = gathered(after(front_weight, query_pair), core)
    query = query_pair[:, :wide]
    pair = query_pair[:, wide : wide + PAIR_WIDTH]
    window = jnp.concatenate([moved(pair, "shard", d) for d in range(blocks, 0, -1)] + [pair], 0)
    low = jnp.maximum(jnp.arange(1, count + 1, dtype=jnp.int32), doc_start - begin + blocks * count)[None]
    attended, logsum = attend(low, query, window)
    mamba_full = gathered(after(mamba_out, front_full, attended), core)
    front = project(normed, front_full)
    switch = front[:, INNER : 2 * INNER]
    select = front[:, 2 * INNER : 2 * INNER + 2 * STATE]
    step_raw = front[:, 2 * INNER + 2 * STATE : 2 * INNER + lead]
    writer = select[:, :STATE].astype(jnp.bfloat16)
    reader = select[:, STATE:].astype(jnp.bfloat16)
    step = jax.nn.softplus(step_raw)
    cumul = jnp.cumsum(-step * decay_rate[None, :], axis=0)
    valid = (place[None, :] <= place[:, None]) & (place[None, :] >= doc_start[:, None])
    bias = jnp.where(valid, 0.0, -1e30)
    gram = right_product(reader, writer)
    enter = jnp.exp(cumul) * (doc_start < begin)[:, None]
    tail = jnp.exp(cumul[-1][None, :] - cumul) * (place >= doc_start[-1])[:, None]
    carry = jnp.exp(cumul[-1]) * (doc_start[-1] < begin)
    carry_lanes = head_lanes(carry)
    step_rows, cumul_rows, enter_rows, tail_rows = (pair_rows(v) for v in (step, cumul, enter, tail))
    drive, local = make_drive(front, step_rows, tail_rows, writer.T)
    state_in = state_from(local, carry_lanes, 1)
    mixed_flat = mix(drive, cumul_rows, enter_rows, gram, bias, reader, state_in)
    mixer_full = gathered(after(mixer_out, mamba_full, state_in), core)
    gated = (mixed_flat * jax.nn.silu(switch)).astype(jnp.bfloat16)
    mamba_y = project(gated, mamba_full)
    scale_att = inverse_rms(attended)
    unit_att = attended * scale_att
    scale_mam = inverse_rms(mamba_y)
    unit_mam = mamba_y * scale_mam
    blend = (0.5 * (attention_scale * unit_att + mamba_scale * unit_mam)).astype(jnp.bfloat16)
    middle = inputs + project(blend, mixer_full)
    scale_two = inverse_rms(middle)
    unit_two = middle * scale_two
    feed_in = (unit_two * feed_gain).astype(jnp.bfloat16)
    feed_all = lax.all_gather(feed_in, "shard", axis=0, tiled=True)
    cotangent_all = lax.all_gather(after(cotangent, feed_in), "shard", axis=0, tiled=True)
    gate = project(feed_all, gate_weight)
    up = project(feed_all, up_weight)
    active = lax.optimization_barrier((jax.nn.silu(gate) * up).astype(jnp.bfloat16))
    output_part = project(active, down_weight).astype(jnp.bfloat16)
    upstream = cotangent.astype(jnp.float32)
    d_active = right_product(cotangent_all, down_weight)
    d_gate = (d_active * up * silu_slope(gate)).astype(jnp.bfloat16)
    d_up = (d_active * jax.nn.silu(gate)).astype(jnp.bfloat16)
    feed_back = scattered(right_product(d_gate, gate_weight) + right_product(d_up, up_weight)).astype(
        jnp.float32
    )
    gate_part = left_product(feed_all, d_gate).astype(jnp.bfloat16)
    up_part = left_product(feed_all, d_up).astype(jnp.bfloat16)
    down_part = left_product(cotangent_all, active).astype(jnp.bfloat16)
    feed_sums = [ChipSum(core_half(part, core)) for part in (gate_part, up_part, down_part)]
    feed_back = after(feed_back, *(s.part for s in feed_sums))
    gate_sum, up_sum, down_sum = feed_sums
    feed_gain_part = jnp.sum(feed_back * unit_two, axis=0)
    d_middle = upstream + rms_back(feed_back * feed_gain, unit_two, scale_two)
    d_branch = d_middle.astype(jnp.bfloat16)
    d_blend = right_product(d_branch, mixer_full)
    attention_scale_part = jnp.sum(0.5 * d_blend * unit_att, axis=0)
    mamba_scale_part = jnp.sum(0.5 * d_blend * unit_mam, axis=0)
    d_attended = rms_back(0.5 * d_blend * attention_scale, unit_att, scale_att).astype(jnp.bfloat16)
    d_mamba = rms_back(0.5 * d_blend * mamba_scale, unit_mam, scale_mam).astype(jnp.bfloat16)
    d_gated = right_product(d_mamba, mamba_full)
    d_mixed = (d_gated * jax.nn.silu(switch)).astype(jnp.bfloat16)
    d_switch = (d_gated * mixed_flat * silu_slope(switch)).astype(jnp.bfloat16)
    blend_both = jnp.concatenate([blend, swapped(blend)], 0)
    mixer_part = left_product(blend_both, both_cores(d_branch, core)).astype(jnp.bfloat16)
    gated_both = jnp.concatenate([gated, swapped(gated)], 0)
    mamba_part = left_product(gated_both, both_cores(d_mamba, core)).astype(jnp.bfloat16)
    mixer_half = scattered(mixer_part)
    mamba_half = scattered(mamba_part)
    d_mixed, d_switch = advance((d_mixed, d_switch, mixer_part, mamba_part), [gate_sum], [up_sum, down_sum])[:2]
    switch_half = scattered(left_product(normed_both, both_cores(d_switch, core)))
    state_grad = leave_back(d_mixed, enter_rows, reader.T)
    d_state = state_from(state_grad, carry_lanes, -1)
    d_signal, d_gram_t, d_reader_state, d_writer_state, stats, sums = mix_back(
        d_mixed, mixed_flat, drive, front, step_rows, cumul_rows, enter_rows, tail_rows, gram.T, bias.T, writer,
        state_in, d_state,
    )
    d_signal = advance((d_signal, mixer_half), [gate_sum, up_sum], [down_sum])[0]
    signal_part = left_product(normed_both, both_cores(d_signal, core)).astype(jnp.bfloat16)
    signal_half = scattered(signal_part)
    d_attended = after(d_attended, signal_part)
    output_half = scattered(after(output_part, signal_part))
    head_stats = stats.reshape(PAIRS, 2, 2, count).transpose(1, 3, 0, 2).reshape(2, count, MAMBA_HEADS)
    head_totals = jnp.sum(sums.reshape(PAIRS, 2, 2, MAMBA_DIM), axis=3).transpose(1, 0, 2).reshape(2, MAMBA_HEADS)
    d_cumul = head_stats[0].at[-1].add(head_totals[1] + head_totals[0] * carry)
    d_rate = jnp.flip(jnp.cumsum(jnp.flip(d_cumul, 0), axis=0), 0)
    decay_rate_part = -jnp.sum(d_rate * step, axis=0)
    d_step = -d_rate * decay_rate[None, :] + head_stats[1]
    d_step_raw = (d_step * jax.nn.sigmoid(step_raw)).astype(jnp.bfloat16)
    d_gram_t = d_gram_t.astype(jnp.bfloat16)
    d_reader = (left_product(d_gram_t, writer) + d_reader_state).astype(jnp.bfloat16)
    d_writer = (project(d_gram_t, reader) + d_writer_state).astype(jnp.bfloat16)
    d_query, d_window = attend_back(low, query, window, attended, logsum, d_attended)
    d_window = advance((d_window, mamba_half, switch_half), [gate_sum, up_sum, down_sum])[0]
    mamba_sum, mixer_sum = ChipSum(mamba_half), ChipSum(mixer_half)
    own_grads = d_window[blocks * count :]
    for distance in range(1, blocks + 1):
        away = d_window[(blocks - distance) * count : (blocks - distance + 1) * count]
        own_grads = own_grads + moved(away.astype(jnp.bfloat16), "shard", -distance).astype(jnp.float32)
    own_grads = after(own_grads, output_half)
    d_small = jnp.pad(jnp.concatenate([d_writer, d_reader, d_step_raw], 1), ((0, 0), (0, 128 - lead)))
    d_pair = own_grads.astype(jnp.bfloat16)
    d_last = jnp.concatenate([d_query, d_pair, d_small], 1)
    unused = -d_last.shape[1] % 256
    last_part = left_product(normed_both, both_cores(jnp.pad(d_last, ((0, 0), (0, unused))), core)).astype(jnp.bfloat16)
    last_half = scattered(last_part)
    d_front = jnp.concatenate([d_signal, d_switch, d_small], 1)
    d_query_pair = jnp.pad(jnp.concatenate([d_query, d_pair], 1), ((0, 0), (0, spare)))
    d_normed = right_product(d_front, front_full) + right_product(d_query_pair, query_pair_full)
    d_normed = advance((d_normed, signal_half), [up_sum, down_sum, mamba_sum, mixer_sum])[0]
    switch_sum, signal_sum = lax.psum((switch_half, signal_half), "zz")
    attention_gain_part = jnp.sum(d_normed * unit_one, axis=0)
    token_gradient = (d_middle + rms_back(d_normed * attention_gain, unit_one, scale_one)).astype(
        jnp.bfloat16
    )
    small = jnp.concatenate(
        [attention_gain_part, attention_scale_part, mamba_scale_part, feed_gain_part, decay_rate_part]
    )
    length = small.shape[0]
    small = jnp.pad(small, (0, -length % 1024)).reshape(-1, 1024)
    small = sum_over_axis(sum_over_axis(small, "core"), "shard")
    output = (middle + output_half.astype(jnp.float32)).astype(jnp.bfloat16)
    small = sum_over_axis(small, "zz").reshape(-1)
    token_gradient, switch_sum, signal_sum = advance(
        (token_gradient, switch_sum, signal_sum), [down_sum, mamba_sum, mixer_sum]
    )
    last_sum = lax.psum(after(last_half, switch_sum, signal_sum), "zz")
    token_gradient = advance(token_gradient, [mamba_sum, mixer_sum])
    last_gradient = both_halves(last_sum, core, 1)
    pair_gradient = last_gradient[:, wide : wide + PAIR_WIDTH].reshape(rows, KV_HEADS, 2, HEAD_DIM)
    base = wide + PAIR_WIDTH
    ends = [0]
    for part in (attention_gain_part, attention_scale_part, mamba_scale_part, feed_gain_part, decay_rate_part):
        ends.append(ends[-1] + part.shape[0])
    return (
        output,
        token_gradient,
        last_gradient[:, :wide],
        pair_gradient[:, :, 0].reshape(rows, KV_HEADS * HEAD_DIM),
        pair_gradient[:, :, 1].reshape(rows, KV_HEADS * HEAD_DIM),
        jnp.concatenate([both_halves(signal_sum, core, 1), both_halves(switch_sum, core, 1)], 1),
        last_gradient[:, base : base + 2 * STATE],
        last_gradient[:, base + 2 * STATE : base + lead],
        both_halves(mamba_sum.part, core, 1),
        both_halves(mixer_sum.part, core, 1),
        both_halves(gate_sum.part, core, 0),
        both_halves(up_sum.part, core, 0),
        both_halves(down_sum.part, core, 0).T,
        *(small[ends[i] : ends[i + 1]] for i in range(5)),
    )


def solution(mesh):
    rep, shard = mesh.shape["rep"], mesh.shape["shard"]
    mesh = jax.sharding.Mesh(mesh.devices.reshape(rep // 2, 2, shard), ("zz", "core", "shard"))
    placed = (
        P(("zz", "core", "shard"), None),
        P(("zz", "core", "shard"), None),
        P(("zz", "core", "shard")),
        P("shard", None),
        P("shard", None),
        P("shard", None),
        P("shard", None),
        P("shard", None),
        P("shard", None),
        P("shard", None),
        P("shard", None),
        P(None, "shard"),
        P(None, "shard"),
        P("shard", None),
        P(),
        P(),
        P(),
        P(),
        P(),
    )
    return jax.shard_map(
        body,
        mesh=mesh,
        in_specs=placed,
        out_specs=(
            P(("zz", "core", "shard"), None),
            P(("zz", "core", "shard"), None),
            P("shard", None),
            P("shard", None),
            P("shard", None),
            P("shard", None),
            P("shard", None),
            P("shard", None),
            P("shard", None),
            P("shard", None),
            P(None, "shard"),
            P(None, "shard"),
            P("shard", None),
            P(),
            P(),
            P(),
            P(),
            P(),
        ),
        check_vma=False,
    )
```

time: 1740 us -> 1460 us (0.84)
  matrix products: 571 us -> 310 us
  Pallas kernels: 0 us -> 179 us
  waiting for transfers between devices: 619 us -> 510 us
  blocking collectives: 74.9 us -> 0 us
  other arithmetic: 253 us -> 184 us
  local copies, waits for them, and re-layouts: 107 us -> 172 us
    dot_general x16 -> x0, matrix products: 284 us -> none  [the longest x1 56.8 us: body(): jnp.einsum('tkgd,skd->kgts', d_heads, all_values, preferred_element_type=...]
    ppermute x21 -> x20, waiting for transfers between devices: 346 us -> 140 us  [the longest x5 104 us: sum_over_axis(): lax.ppermute(values, axis, [(i, i ^ distance) for i in range(size)])]
    pallas_call x0 -> x6, Pallas kernels: none -> 179 us  [the longest x1 51.2 us: attend_back(): pl.pallas_call(attend_back_kernel, grid=(count // rows,), in_specs=[pl.Bl...]
    psum x1 -> x0, blocking collectives: 74.9 us -> none  [body(): lax.psum((attention_gain_part, attention_scale_part, mamba_scale_part, fe...]
    convert_element_type x18 -> x13, other arithmetic: 99 us -> 40.1 us  [the longest x10 34.9 us: add_low(): (first.astype(jnp.float32) + second.astype(jnp.float32)).astype(jnp.bfloa...]
    psum x0 -> x2, waiting for transfers between devices: none -> 39.3 us  [the longest x1 39.2 us: body(): last_sum = lax.psum(after(last_half, switch_sum, signal_sum), 'zz')]
    all_gather x4, waiting for transfers between devices: 43.2 us -> 80.7 us  [gathered(): return lax.all_gather(half, ('shard', 'core'), axis=0, tiled=True)]
    reduce_scatter x4 -> x3, waiting for transfers between devices: 63.2 us -> 28.3 us  [scattered(): lax.psum_scatter(part.astype(jnp.bfloat16), 'shard', scatter_dimension=ax...]
  transfers between devices with their start and end apart: 64 -> 68, of which waited for: 22 -> 17; matrix products, arithmetic and copies ran while one was open for 49% -> 37% of each run, Pallas kernels for 0% -> 12%
where the time goes in v2:
time: 1460 us; the launch traced here: 1450 us
  waiting for transfers between devices  510 us (35%)
  matrix products  310 us (21%)
  other arithmetic  184 us (13%)
  Pallas kernels  179 us (12%)
  local copies, waits for them, and re-layouts  172 us (12%)
  starting transfers between devices  78.6 us (5%)
  between operations  17.2 us (1%)
    dot_general x8, matrix products, right_product(): lax.dot_general(left, right, (((1,), (1,)), ((), ())), preferred_element_...  111 us
    ppermute x5, waiting for transfers between devices, sum_over_axis(): lax.ppermute(values, axis, [(i, i ^ distance) for i in range(size)])  104 us
    dot_general x8, matrix products, project(): return jnp.dot(left, right, preferred_element_type=jnp.float32)  102 us
    dot_general x9, matrix products, left_product(): lax.dot_general(left, right, (((0,), (0,)), ((), ())), preferred_element_...  97 us
    all_gather x4, waiting for transfers between devices, gathered(): return lax.all_gather(half, ('shard', 'core'), axis=0, tiled=True)  80.7 us
    all_gather x1, waiting for transfers between devices, body(): feed_all = lax.all_gather(feed_in, 'shard', axis=0, tiled=True)  77.6 us
    ppermute x14, waiting for transfers between devices, moved(): return lax.ppermute(block, axis, route)  70.4 us
    unnamed x199, local copies, waits for them, and re-layouts  59.3 us
  transfers between devices with their start and end apart: 68, of which 17 were waited for; matrix products, arithmetic and copies ran while one was open for 37% of the time, Pallas kernels for 12%

profile of v2, /device:TPU:1, one launch (start us, length us, event | category | flops | bytes accessed | tf_op | source)
XLA Modules:
  0.0 1449.9 jit_solution(3168456528773118385)
XLA Ops:
  24.4 5.6 fusion.12
  30.0 38.3 %all-gather.7.cloned.1.call-done = bf16[1600,2304]{1,0:T(8,128)(2,1)} async-done(((bf16[200,2304]{1,0:T(8,128)(2,1)}), bf16[1600,2304]{1,0:T(8,128)(2,1)}) %all-gather.7.cloned.1.call-update) | async-done | bytes 7372816 | tf_op jit(solution)/shard_map/all_gather | solution.py:102
  68.3 9.6 convolution_convert_fusion.8
  92.0 29.9 %collective-permute-done = bf16[512,640]{1,0:T(8,128)(2,1)} collective-permute-done((bf16[512,640]{1,0:T(8,128)(2,1)S(1)}, bf16[512,640]{1,0:T(8,128)(2,1)}, u32[]{:S(2)}, u32[]{:S(2)}) %collective-permute-start) | collective-permute-done | bytes 655392 | tf_op jit(solution)/shard_map/ppermute | solution.py:29
  124.7 49.6 %attend.1 = (f32[512,1600]{1,0:T(8,128)}, f32[25,1,512]{2,1,0:T(1,128)}) custom-call(s32[1,512]{1,0:T(1,128)} %bitcast.90, bf16[512,1600]{1,0:T(8,128)(2,1)} %slice.195.query_ref, bf16[1536,640]{1,0:T(8,128)(2,1)} %pad_maximum_fusion.1.pair_ref), custom_call_target="tpu_custom_call" | custom-call | tf_op jit(solution)/shard_map/attend/pallas_call | solution.py:215
  174.3 33.8 %all-gather.9.cloned.1.call-done = bf16[1600,6528]{1,0:T(8,128)(2,1)} async-done(((bf16[200,6528]{1,0:T(8,128)(2,1)}), bf16[1600,6528]{1,0:T(8,128)(2,1)}) %all-gather.9.cloned.1.call-update) | async-done | bytes 20889616 | tf_op jit(solution)/shard_map/all_gather | solution.py:102
  211.5 21.0 %fusion.95 = (bf16[512,6528]{1,0:T(8,128)(2,1)}, f32[512,6528]{1,0:T(8,128)}) fusion(bf16[512,1600]{1,0:T(8,128)(2,1)} %fusion.22, bf16[1600,6528]{1,0:T(8,128)(2,1)} %all-gather.9.cloned.1.call-done), kind=kOutput, calls=%fused_computation.236 | convolution fusion | flops 10698817536 | bytes 42582016 | tf_op jit(solution)/shard_map/dot_general | solution.py:128
  239.8 9.2 make_drive.1
  258.5 12.2 collective-permute-done.3
  270.9 8.6 all-gather.11.cloned.1.call-done
  286.5 21.1 %mix.1.mixed_ref = f32[512,3200]{1,0:T(8,128)S(1)} custom-call(bf16[512,3200]{1,0:T(8,128)(2,1)S(1)} %copy-done.3, f32[25,2,512]{2,1,0:T(2,128)S(1)} %reduce_window_sum.33.cumul_ref, f32[25,2,512]{2,1,0:T(2,128)S(1)} %get-tuple-element.315.enter_ref, f32[512,512]{1,0:T(8,128)S(1)} %fusion.84.gram_ref, f32[512,512]{1,0:T(8,128)S(1)} %get-tuple-element.322.bias_ref, ...), custom_call_target="tpu_custom_call" | custom-call | tf_op jit(solution)/shard_map/mix/pallas_call | solution.py:412
  314.6 12.8 multiply_reduce_fusion.8
  327.5 4.7 copy.222
  332.2 5.0 multiply_convert_fusion.9
  337.2 7.1 multiply_reduce_fusion.6
  348.3 77.6 %all-gather.15.cloned.1.call-done = bf16[2048,1600]{1,0:T(8,128)(2,1)} async-done(((bf16[512,1600]{1,0:T(8,128)(2,1)}), bf16[2048,1600]{1,0:T(8,128)(2,1)}) %all-gather.15.cloned.1.call-update) | async-done | bytes 6553616 | tf_op jit(solution)/shard_map/all_gather | solution.py:593
  425.9 16.8 %fusion.96 = f32[2048,1376]{0,1:T(8,128)} fusion(bf16[2048,1600]{1,0:T(8,128)(2,1)} %all-gather.15.cloned.1.call-done, bf16[1600,1376]{1,0:T(8,128)(2,1)} %param.32), kind=kOutput, calls=%fused_computation.237 | convolution fusion | flops 9017753600 | bytes 22228992 | tf_op jit(solution)/shard_map/dot_general | solution.py:128
  442.7 15.7 %fusion.97 = f32[2048,1376]{0,1:T(8,128)} fusion(bf16[2048,1600]{1,0:T(8,128)(2,1)S(1)} %copy-done.84, bf16[1600,1376]{1,0:T(8,128)(2,1)} %param.33), kind=kOutput, calls=%fused_computation.238 | convolution fusion | flops 9017753600 | bytes 22228992 | tf_op jit(solution)/shard_map/dot_general | solution.py:128
  458.3 41.5 %all-gather.17.cloned.1.call-done = bf16[2048,1600]{0,1:T(8,128)(2,1)} async-done(((bf16[512,1600]{0,1:T(8,128)(2,1)}), bf16[2048,1600]{0,1:T(8,128)(2,1)}) %all-gather.17.cloned.1.call-update) | async-done | bytes 6553616 | tf_op jit(solution)/shard_map/all_gather | solution.py:594
  499.8 24.0 %multiply_convert_fusion = (bf16[2048,1376]{0,1:T(8,128)(2,1)}, bf16[2048,1376]{0,1:T(8,128)(2,1)}, bf16[2048,1376]{0,1:T(8,128)(2,1)}) fusion(f32[2048,1376]{0,1:T(8,128)} %fusion.96, f32[2048,1376]{0,1:T(8,128)} %fusion.97, bf16[2048,1600]{0,1:T(8,128)(2,1)} %all-gather.17.cloned.1.call-done, bf16[1376,1600]{0,1:T(8,128)(2,1)} %param.34), kind=kOutput, calls=%fused_computation | convolution fusion | flops 9060024320 | bytes 50409472 | tf_op jit(solution)/shard_map/dot_general | solution.py:138
  523.8 14.0 fusion.98
  537.9 15.8 %convolution_add_fusion = bf16[2048,1600]{0,1:T(8,128)(2,1)} fusion(f32[2048,1600]{0,1:T(8,128)S(1)} %fusion.98, bf16[1600,1376]{1,0:T(8,128)(2,1)} %param.33, bf16[2048,1376]{0,1:T(8,128)(2,1)} %get-tuple-element.264), kind=kOutput, calls=%fused_computation.8 | convolution fusion | flops 9024307200 | bytes 29700096 | tf_op jit(solution)/shard_map/dot_general | solution.py:138
  553.7 9.5 copy.228
  567.9 15.2 %convolution_convert_fusion.3 = bf16[1600,1376]{1,0:T(8,128)(2,1)S(1)} fusion(bf16[2048,1600]{0,1:T(8,128)(2,1)} %all-gather.17.cloned.1.call-done, bf16[2048,1376]{0,1:T(8,128)(2,1)} %get-tuple-element.266), kind=kOutput, calls=%fused_computation.12 | convolution fusion | flops 9019955200 | bytes 16592896 | tf_op jit(solution)/shard_map/dot_general | solution.py:132
  584.7 17.9 %convolution_convert_fusion.6 = bf16[1600,1376]{1,0:T(8,128)(2,1)S(1)} fusion(bf16[2048,1600]{1,0:T(8,128)(2,1)} %all-gather.15.cloned.1.call-done, bf16[2048,1376]{0,1:T(8,128)(2,1)} %get-tuple-element.265), kind=kOutput, calls=%fused_computation.15 | convolution fusion | flops 9019955200 | bytes 16592896 | tf_op jit(solution)/shard_map/dot_general | solution.py:132
  604.4 11.9 convolution_convert_fusion.5
  627.8 4.5 add_convert_fusion.8
  632.3 4.5 collective-permute-start.15
  636.8 4.5 add_convert_fusion.6
  653.6 7.6 multiply_reduce_fusion.1
  671.9 15.7 %multiply_convert_fusion.3 = (bf16[512,3200]{1,0:T(8,128)(2,1)}, bf16[512,3200]{1,0:T(8,128)(2,1)}) fusion(f32[512,3200]{1,0:T(8,128)} %copy-done.2, f32[512,6528]{1,0:T(8,128)} %get-tuple-element.324.signal_ref, bf16[512,1600]{1,0:T(8,128)(2,1)} %copy-done.39, bf16[3200,1600]{1,0:T(8,128)(2,1)} %all-gather.11.cloned.1.call-done), kind=kOutput, calls=%fused_computation.26 | convolution fusion | flops 5264179200 | bytes 31539200 | tf_op jit(solution)/shard_map/dot_general | solution.py:138
  691.8 7.2 convolution_convert_fusion.9
  698.9 11.1 convolution_convert_fusion.7
  710.2 8.7 copy.281
  723.3 4.4 broadcast_select_fusion.10
  738.8 11.5 convolution_convert_fusion.1
  750.4 4.3 add_convert_fusion.5
  762.9 6.0 leave_back.1
  775.5 7.4 collective-permute-done.16
  785.7 7.4 collective-permute-done.20
  794.4 41.4 %mix_back.1 = (bf16[512,3200]{1,0:T(8,128)(2,1)}, f32[512,512]{1,0:T(8,128)S(1)}, f32[512,16]{1,0:T(8,128)S(1)}, f32[512,16]{1,0:T(8,128)S(1)}, f32[25,4,512]{2,1,0:T(4,128)S(1)}, /*index=5*/f32[25,2,128]{2,1,0:T(2,128)S(1)}) custom-call(bf16[512,3200]{1,0:T(8,128)(2,1)} %get-tuple-element.101.d_mixed_ref, f32[512,3200]{1,0:T(8,128)} %copy-done.2, ...), custom_call_target="tpu_custom_call" | custom-call | tf_op jit(solution)/shard_map/mix_back/pallas_call | solution.py:495
  846.8 17.6 %convolution_convert_fusion.4 = bf16[2048,1600]{1,0:T(8,128)(2,1)} fusion(bf16[2048,1376]{0,1:T(8,128)(2,1)} %get-tuple-element.266, bf16[1376,1600]{0,1:T(8,128)(2,1)} %param.34), kind=kOutput, calls=%fused_computation.13 | convolution fusion | flops 9021030400 | bytes 16592896 | tf_op jit(solution)/shard_map/dot_general | solution.py:128
  868.5 11.1 convolution_convert_fusion.2
  885.9 4.8 add_convert_fusion.4
  892.1 6.7 collective-permute-start.27
  908.0 51.2 %attend_back.1 = (bf16[512,1600]{1,0:T(8,128)(2,1)}, f32[1536,640]{1,0:T(8,128)}) custom-call(s32[1,512]{1,0:T(1,128)} %bitcast.91, bf16[512,1600]{1,0:T(8,128)(2,1)} %slice.195.query_ref, bf16[1536,640]{1,0:T(8,128)(2,1)} %pad_maximum_fusion.1.pair_ref, f32[512,1600]{1,0:T(8,128)} %get-tuple-element.93.out_ref, ...), custom_call_target="tpu_custom_call" | custom-call | tf_op jit(solution)/shard_map/attend_back/pallas_call | solution.py:300
  977.3 4.3 add_convert_fusion.1
  985.8 10.7 collective-permute-done.28
  1006.3 28.3 %reduce-scatter.16.cloned.1.call-done = bf16[512,1600]{1,0:T(8,128)(2,1)} async-done(((bf16[2048,1600]{1,0:T(8,128)(2,1)}), bf16[512,1600]{1,0:T(8,128)(2,1)}) %reduce-scatter.16.cloned.1.call-update) | async-done | bytes 1638416 | tf_op jit(solution)/shard_map/reduce_scatter | solution.py:124
  1034.6 10.2 fusion.43
  1044.8 22.1 %fusion.19 = f32[512,1600]{1,0:T(8,128)} fusion(f32[512,1600]{1,0:T(8,128)} %fusion.43, bf16[1600,6528]{1,0:T(8,128)(2,1)} %all-gather.9.cloned.1.call-done, bf16[512,128]{1,0:T(8,128)(2,1)S(1)} %fusion.71, bf16[512,3200]{1,0:T(8,128)(2,1)S(1)} %copy-done.44, bf16[512,3200]{1,0:T(8,128)(2,1)} %get-tuple-element.107), kind=kOutput, calls=%fused_computation.54 | convolution fusion | flops 10716348416 | bytes 34127872 | tf_op jit(solution)/shard_map/dot_general | solution.py:138
  1070.8 31.1 %reduce-scatter.24.cloned.1.call-done = bf16[400,1600]{1,0:T(8,128)(2,1)} async-done(((bf16[1600,1600]{1,0:T(8,128)(2,1)}), bf16[400,1600]{1,0:T(8,128)(2,1)}) %reduce-scatter.24.cloned.1.call-update) | async-done | bytes 1280016
  1106.3 4.9 maximum_convert_fusion
  1118.1 9.2 convolution_convert_fusion
  1138.4 4.6 add_convert_fusion
  1144.4 6.0 collective-permute-start.51
  1150.4 103.5 %collective-permute-done.51 = f32[7,1024]{1,0:T(8,128)S(1)} collective-permute-done((f32[7,1024]{1,0:T(8,128)S(1)}, f32[7,1024]{1,0:T(8,128)S(1)}, u32[]{:S(2)}, u32[]{:S(2)}) %collective-permute-start.51) | collective-permute-done | bytes 28704 | tf_op jit(solution)/shard_map/ppermute | solution.py:160
  1283.9 36.2 %collective-permute-done.38 = bf16[400,800]{1,0:T(8,128)(2,1)S(1)} collective-permute-done((bf16[400,800]{1,0:T(8,128)(2,1)}, bf16[400,800]{1,0:T(8,128)(2,1)S(1)}, u32[]{:S(2)}, u32[]{:S(2)}) %collective-permute-start.38) | collective-permute-done | bytes 640032 | tf_op jit(solution)/shard_map/ppermute | solution.py:69
  1334.5 8.9 concatenate.101
  1343.4 7.1 concatenate.102
  1362.4 4.4 copy.270
  1371.0 39.2 %all-reduce.14.cloned.1.call-done = bf16[400,1280]{1,0:T(8,128)(2,1)} async-done(((bf16[400,1280]{1,0:T(8,128)(2,1)}), bf16[400,1280]{1,0:T(8,128)(2,1)}) %all-reduce.14.cloned.1.call-update) | async-done | bytes 1024016 | tf_op jit(solution)/shard_map/psum | solution.py:686
  1410.7 5.8 convert_bitcast_fusion
  1421.4 6.6 copy.269
  (498 shorter events, 323.9 us)
Async XLA Ops:
  7.2 61.1 %all-gather.7.cloned.1.call-start = ((), (), s32[]{:S(2)}) async-start(), calls=%async_computation.6 | async-start | bytes 8294400 | tf_op jit(solution)/shard_map/all_gather | solution.py:102
  15.6 192.6 %all-gather.9.cloned.1.call-start = ((), (), s32[]{:S(2)}) async-start(), calls=%async_computation.7 | async-start | bytes 23500800 | tf_op jit(solution)/shard_map/all_gather | solution.py:102
  79.6 199.9 %all-gather.11.cloned.1.call-start = ((), (), s32[]{:S(2)}) async-start(), calls=%async_computation.8 | async-start | bytes 11980800 | tf_op jit(solution)/shard_map/all_gather | solution.py:102
  81.1 40.8 %collective-permute-start = (bf16[512,640]{1,0:T(8,128)(2,1)S(1)}, bf16[512,640]{1,0:T(8,128)(2,1)}, u32[]{:S(2)}, u32[]{:S(2)}) collective-permute-start(bf16[512,640]{1,0:T(8,128)(2,1)S(1)} %slice.196), channel_id=1, source_target_pairs={{0,2},{1,3},{4,6},{5,7},{8,10},{9,11},{12,14},{13,15},{16,18},{17,... | collective-permute-start | bytes 1966088 | tf_op jit(solution)/shard_map/ppermute | solution.py:29
  84.8 37.1 %collective-permute-start.1 = (bf16[512,640]{1,0:T(8,128)(2,1)S(1)}, bf16[512,640]{1,0:T(8,128)(2,1)}, u32[]{:S(2)}, u32[]{:S(2)}) collective-permute-start(bf16[512,640]{1,0:T(8,128)(2,1)S(1)} %slice.196), channel_id=1, source_target_pairs={{0,1},{1,2},{2,3},{4,5},{5,6},{6,7},{8,9},{9,10},{10,11},{12,13},{... | collective-permute-start | bytes 1966088 | tf_op jit(solution)/shard_map/ppermute | solution.py:29
  209.3 127.9 %all-gather.13.cloned.1.call-start = ((), (), s32[]{:S(2)}) async-start(), calls=%async_computation.9 | async-start | bytes 5990400 | tf_op jit(solution)/shard_map/all_gather | solution.py:102
  249.0 21.7 %collective-permute-start.2 = (f32[16,3200]{1,0:T(8,128)}, f32[16,3200]{1,0:T(8,128)S(1)}, u32[]{:S(2)}, u32[]{:S(2)}) collective-permute-start(f32[16,3200]{1,0:T(8,128)} %get-tuple-element.96), channel_id=1, source_target_pairs={{0,1},{1,2},{2,3},{4,5},{5,6},{6,7},{8,9},{9,10},{10,11},{12,13},{... | collective-permute-start | bytes 614408 | tf_op jit(solution)/shard_map/ppermute | solution.py:29
  252.2 18.6 %collective-permute-start.4 = (f32[16,3200]{1,0:T(8,128)}, f32[16,3200]{1,0:T(8,128)S(1)}, u32[]{:S(2)}, u32[]{:S(2)}) collective-permute-start(f32[16,3200]{1,0:T(8,128)} %get-tuple-element.96), channel_id=1, source_target_pairs={{0,2},{1,3},{4,6},{5,7},{8,10},{9,11},{12,14},{13,15},{16,18},{17,... | collective-permute-start | bytes 614408 | tf_op jit(solution)/shard_map/ppermute | solution.py:29
  254.5 16.4 %collective-permute-start.6 = (f32[16,3200]{1,0:T(8,128)}, f32[16,3200]{1,0:T(8,128)S(1)}, u32[]{:S(2)}, u32[]{:S(2)}) collective-permute-start(f32[16,3200]{1,0:T(8,128)} %get-tuple-element.96), channel_id=1, source_target_pairs={{0,3},{4,7},{8,11},{12,15},{16,19},{20,23},{24,27},{28,31}} | collective-permute-start | bytes 614408 | tf_op jit(solution)/shard_map/ppermute | solution.py:29
  255.9 14.8 %collective-permute-start.3 = (f32[1,3200]{1,0:T(1,128)S(1)}, f32[1,3200]{1,0:T(1,128)S(1)}, u32[]{:S(2)}, u32[]{:S(2)}) collective-permute-start(f32[1,3200]{1,0:T(1,128)S(1)} %broadcast_in_dim_reshape.3), channel_id=1, source_target_pairs={{0,1},{1,2},{2,3},{4,5},{5,6},{6,7},{8,9},{9,10},{10,11},{12,13},{... | collective-permute-start | bytes 38408 | tf_op jit(solution)/shard_map/ppermute | solution.py:29
  257.2 13.5 collective-permute-start.5
  281.5 144.4 %all-gather.15.cloned.1.call-start = ((), (), s32[]{:S(2)}) async-start(), calls=%async_computation.10 | async-start | bytes 8519680 | tf_op jit(solution)/shard_map/all_gather | solution.py:593
  347.7 152.1 %all-gather.17.cloned.1.call-start = ((), (), s32[]{:S(2)}) async-start(), calls=%async_computation.11 | async-start | bytes 8192000 | tf_op jit(solution)/shard_map/all_gather | solution.py:594
  348.3 296.5 %reduce-scatter.14.cloned.1.call-start = ((), (), s32[]{:S(2)}) async-start(), calls=%async_computation.12 | async-start | bytes 8519680 | tf_op jit(solution)/shard_map/reduce_scatter | solution.py:124
  563.2 274.3 %all-reduce.16.cloned.1.call-start = ((), (), s32[]{:S(2)}) async-start(), calls=%async_computation.17 | async-start | bytes 5324800
  567.2 56.9 %collective-permute-start.11 = (bf16[512,1600]{0,1:T(8,128)(2,1)}, bf16[512,1600]{0,1:T(8,128)(2,1)}, u32[]{:S(2)}, u32[]{:S(2)}) collective-permute-start(bf16[512,1600]{0,1:T(8,128)(2,1)} %copy.230), channel_id=1, source_target_pairs={{0,4},{4,0},{1,5},{5,1},{2,6},{6,2},{3,7},{7,3},{8,12},{12,8},{9,1... | collective-permute-start | bytes 4915208 | tf_op jit(solution)/shard_map/ppermute | solution.py:33
  584.7 52.0 %collective-permute-start.10 = (bf16[800,1376]{1,0:T(8,128)(2,1)}, bf16[800,1376]{1,0:T(8,128)(2,1)}, u32[]{:S(2)}, u32[]{:S(2)}) collective-permute-start(bf16[800,1376]{1,0:T(8,128)(2,1)} %constant_dynamic-slice_fusion), channel_id=1, source_target_pairs={{0,4},{4,0},{1,5},{5,1},{2,6},{6,2},{3,7},{7,3},{8,12},{12,8},{9,1... | collective-permute-start | bytes 6604808 | tf_op jit(solution)/shard_map/ppermute | solution.py:33
  604.3 23.5 %collective-permute-start.8 = (bf16[800,1376]{1,0:T(8,128)(2,1)}, bf16[800,1376]{1,0:T(8,128)(2,1)}, u32[]{:S(2)}, u32[]{:S(2)}) collective-permute-start(bf16[800,1376]{1,0:T(8,128)(2,1)} %constant_dynamic-slice_fusion.2), channel_id=1, source_target_pairs={{0,4},{4,0},{1,5},{5,1},{2,6},{6,2},{3,7},{7,3},{8,12},{12,8},{9,1... | collective-permute-start | bytes 6604808 | tf_op jit(solution)/shard_map/ppermute | solution.py:33
  620.0 21.2 %collective-permute-start.9 = (bf16[800,1376]{1,0:T(8,128)(2,1)}, bf16[800,1376]{1,0:T(8,128)(2,1)}, u32[]{:S(2)}, u32[]{:S(2)}) collective-permute-start(bf16[800,1376]{1,0:T(8,128)(2,1)} %constant_dynamic-slice_fusion.1), channel_id=1, source_target_pairs={{0,4},{4,0},{1,5},{5,1},{2,6},{6,2},{3,7},{7,3},{8,12},{12,8},{9,1... | collective-permute-start | bytes 6604808 | tf_op jit(solution)/shard_map/ppermute | solution.py:33
  624.0 74.9 %collective-permute-start.13 = (bf16[512,3200]{1,0:T(8,128)(2,1)}, bf16[512,3200]{1,0:T(8,128)(2,1)}, u32[]{:S(2)}, u32[]{:S(2)}) collective-permute-start(bf16[512,3200]{1,0:T(8,128)(2,1)} %copy-done.45), channel_id=1, source_target_pairs={{0,4},{4,0},{1,5},{5,1},{2,6},{6,2},{3,7},{7,3},{8,12},{12,8},{9,1... | collective-permute-start | bytes 9830408 | tf_op jit(solution)/shard_map/ppermute | solution.py:33
  632.3 77.8 %collective-permute-start.15 = (bf16[800,1376]{1,0:T(8,128)(2,1)}, bf16[800,1376]{1,0:T(8,128)(2,1)}, u32[]{:S(2)}, u32[]{:S(2)}) collective-permute-start(bf16[800,1376]{1,0:T(8,128)(2,1)} %add_convert_fusion.8), channel_id=1, source_target_pairs={{0,8},{24,16},{1,9},{25,17},{2,10},{26,18},{3,11},{27,19},{4,12},{... | collective-permute-start | bytes 6604808 | tf_op jit(solution)/shard_map/ppermute | solution.py:69
  666.9 20.6 %collective-permute-start.14 = (bf16[512,800]{0,1:T(8,128)(2,1)S(1)}, bf16[512,800]{0,1:T(8,128)(2,1)}, u32[]{:S(2)}, u32[]{:S(2)}) collective-permute-start(bf16[512,800]{0,1:T(8,128)(2,1)S(1)} %copy.234), channel_id=1, source_target_pairs={{0,4},{4,0},{1,5},{5,1},{2,6},{6,2},{3,7},{7,3},{8,12},{12,8},{9,1... | collective-permute-start | bytes 2457608 | tf_op jit(solution)/shard_map/ppermute | solution.py:33
  671.9 17.3 %collective-permute-start.12 = (bf16[512,800]{0,1:T(8,128)(2,1)}, bf16[512,800]{0,1:T(8,128)(2,1)}, u32[]{:S(2)}, u32[]{:S(2)}) collective-permute-start(bf16[512,800]{0,1:T(8,128)(2,1)} %copy.232), channel_id=1, source_target_pairs={{0,4},{4,0},{1,5},{5,1},{2,6},{6,2},{3,7},{7,3},{8,12},{12,8},{9,1... | collective-permute-start | bytes 2457608 | tf_op jit(solution)/shard_map/ppermute | solution.py:33
  710.1 249.0 %reduce-scatter.20.cloned.1.call-start = ((), (), s32[]{:S(2)}) async-start(), calls=%async_computation.16 | async-start | bytes 7168000
  718.9 243.9 %reduce-scatter.22.cloned.1.call-start = ((), (), s32[]{:S(2)}) async-start(), calls=%async_computation.18 | async-start | bytes 6656000
  722.7 8.7 collective-permute-start.7
  750.4 284.3 %reduce-scatter.16.cloned.1.call-start = ((), (), s32[]{:S(2)}) async-start(), calls=%async_computation.13 | async-start | bytes 8519680 | tf_op jit(solution)/shard_map/reduce_scatter | solution.py:124
  754.7 84.3 %collective-permute-start.21 = (bf16[800,1376]{1,0:T(8,128)(2,1)}, bf16[800,1376]{1,0:T(8,128)(2,1)}, u32[]{:S(2)}, u32[]{:S(2)}) collective-permute-start(bf16[800,1376]{1,0:T(8,128)(2,1)} %add_convert_fusion.5), channel_id=1, source_target_pairs={{8,16},{16,8},{9,17},{17,9},{10,18},{18,10},{11,19},{19,11},{12,20... | collective-permute-start | bytes 6604808 | tf_op jit(solution)/shard_map/ppermute | solution.py:69
  756.9 82.2 %collective-permute-start.22 = (bf16[800,1376]{1,0:T(8,128)(2,1)}, bf16[800,1376]{1,0:T(8,128)(2,1)}, u32[]{:S(2)}, u32[]{:S(2)}) collective-permute-start(bf16[800,1376]{1,0:T(8,128)(2,1)} %add_convert_fusion.7), channel_id=1, source_target_pairs={{0,8},{24,16},{1,9},{25,17},{2,10},{26,18},{3,11},{27,19},{4,12},{... | collective-permute-start | bytes 6604808 | tf_op jit(solution)/shard_map/ppermute | solution.py:69
  759.6 10.6 collective-permute-start.17
  760.9 10.6 collective-permute-start.19
  768.9 13.9 collective-permute-start.16
  770.2 15.4 %collective-permute-start.18 = (f32[16,3200]{1,0:T(8,128)}, f32[16,3200]{1,0:T(8,128)S(1)}, u32[]{:S(2)}, u32[]{:S(2)}) collective-permute-start(f32[16,3200]{1,0:T(8,128)} %leave_back.1), channel_id=1, source_target_pairs={{2,0},{3,1},{6,4},{7,5},{10,8},{11,9},{14,12},{15,13},{18,16},{19,... | collective-permute-start | bytes 614408 | tf_op jit(solution)/shard_map/ppermute | solution.py:29
  771.5 21.5 %collective-permute-start.20 = (f32[16,3200]{1,0:T(8,128)}, f32[16,3200]{1,0:T(8,128)S(1)}, u32[]{:S(2)}, u32[]{:S(2)}) collective-permute-start(f32[16,3200]{1,0:T(8,128)} %leave_back.1), channel_id=1, source_target_pairs={{3,0},{7,4},{11,8},{15,12},{19,16},{23,20},{27,24},{31,28}} | collective-permute-start | bytes 614408 | tf_op jit(solution)/shard_map/ppermute | solution.py:29
  845.2 19.2 %collective-permute-start.23 = (bf16[512,1600]{0,1:T(8,128)(2,1)}, bf16[512,1600]{0,1:T(8,128)(2,1)}, u32[]{:S(2)}, u32[]{:S(2)}) collective-permute-start(bf16[512,1600]{0,1:T(8,128)(2,1)} %copy.238), channel_id=1, source_target_pairs={{0,4},{4,0},{1,5},{5,1},{2,6},{6,2},{3,7},{7,3},{8,12},{12,8},{9,1... | collective-permute-start | bytes 4915208 | tf_op jit(solution)/shard_map/ppermute | solution.py:33
  879.5 222.4 %reduce-scatter.24.cloned.1.call-start = ((), (), s32[]{:S(2)}) async-start(), calls=%async_computation.19 | async-start | bytes 6656000
  883.8 78.9 %collective-permute-start.26 = (bf16[800,1376]{1,0:T(8,128)(2,1)}, bf16[800,1376]{1,0:T(8,128)(2,1)}, u32[]{:S(2)}, u32[]{:S(2)}) collective-permute-start(bf16[800,1376]{1,0:T(8,128)(2,1)} %add_convert_fusion.3), channel_id=1, source_target_pairs={{8,16},{16,8},{9,17},{17,9},{10,18},{18,10},{11,19},{19,11},{12,20... | collective-permute-start | bytes 6604808 | tf_op jit(solution)/shard_map/ppermute | solution.py:69
  885.9 381.0 %all-reduce.18.cloned.1.call-start = ((), (), s32[]{:S(2)}) async-start(), calls=%async_computation.20 | async-start | bytes 5324800 | tf_op jit(solution)/shard_map/psum | solution.py:670
  890.7 72.0 %collective-permute-start.25 = (bf16[800,1376]{1,0:T(8,128)(2,1)}, bf16[800,1376]{1,0:T(8,128)(2,1)}, u32[]{:S(2)}, u32[]{:S(2)}) collective-permute-start(bf16[800,1376]{1,0:T(8,128)(2,1)} %add_convert_fusion.4), channel_id=1, source_target_pairs={{8,0},{16,24},{9,1},{17,25},{10,2},{18,26},{11,3},{19,27},{12,4},{... | collective-permute-start | bytes 6604808 | tf_op jit(solution)/shard_map/ppermute | solution.py:69
  892.1 70.6 %collective-permute-start.27 = (bf16[800,1376]{1,0:T(8,128)(2,1)}, bf16[800,1376]{1,0:T(8,128)(2,1)}, u32[]{:S(2)}, u32[]{:S(2)}) collective-permute-start(bf16[800,1376]{1,0:T(8,128)(2,1)} %add_convert_fusion.6), channel_id=1, source_target_pairs={{0,8},{24,16},{1,9},{25,17},{2,10},{26,18},{3,11},{27,19},{4,12},{... | collective-permute-start | bytes 6604808 | tf_op jit(solution)/shard_map/ppermute | solution.py:69
  964.7 37.5 %collective-permute-start.45 = (bf16[800,1376]{1,0:T(8,128)(2,1)S(1)}, bf16[800,1376]{1,0:T(8,128)(2,1)}, u32[]{:S(2)}, u32[]{:S(2)}) collective-permute-start(bf16[800,1376]{1,0:T(8,128)(2,1)S(1)} %broadcast_select_fusion.2), channel_id=1, source_target_pairs={{0,4},{4,0},{1,5},{5,1},{2,6},{6,2},{3,7},{7,3},{8,12},{12,8},{9,1... | collective-permute-start | bytes 6604808 | tf_op jit(solution)/shard_map/ppermute | solution.py:33
  967.7 103.1 %collective-permute-start.33 = (bf16[400,800]{1,0:T(8,128)(2,1)}, bf16[400,800]{1,0:T(8,128)(2,1)}, u32[]{:S(2)}, u32[]{:S(2)}) collective-permute-start(bf16[400,800]{1,0:T(8,128)(2,1)} %copy.252), channel_id=1, source_target_pairs={{0,8},{24,16},{1,9},{25,17},{2,10},{26,18},{3,11},{27,19},{4,12},{... | collective-permute-start | bytes 1920008 | tf_op jit(solution)/shard_map/ppermute | solution.py:69
  969.8 101.0 %collective-permute-start.32 = (bf16[800,800]{0,1:T(8,128)(2,1)}, bf16[800,800]{0,1:T(8,128)(2,1)}, u32[]{:S(2)}, u32[]{:S(2)}) collective-permute-start(bf16[800,800]{0,1:T(8,128)(2,1)} %copy.282), channel_id=1, source_target_pairs={{0,8},{24,16},{1,9},{25,17},{2,10},{26,18},{3,11},{27,19},{4,12},{... | collective-permute-start | bytes 3840008 | tf_op jit(solution)/shard_map/ppermute | solution.py:69
  974.7 21.8 %collective-permute-start.28 = (bf16[512,640]{1,0:T(8,128)(2,1)S(1)}, bf16[512,640]{1,0:T(8,128)(2,1)S(1)}, u32[]{:S(2)}, u32[]{:S(2)}) collective-permute-start(bf16[512,640]{1,0:T(8,128)(2,1)S(1)} %get-tuple-element.301), channel_id=1, source_target_pairs={{1,0},{2,1},{3,2},{5,4},{6,5},{7,6},{9,8},{10,9},{11,10},{13,12},{... | collective-permute-start | bytes 1966088 | tf_op jit(solution)/shard_map/ppermute | solution.py:29
  976.0 22.5 %collective-permute-start.29 = (bf16[512,640]{1,0:T(8,128)(2,1)S(1)}, bf16[512,640]{1,0:T(8,128)(2,1)S(1)}, u32[]{:S(2)}, u32[]{:S(2)}) collective-permute-start(bf16[512,640]{1,0:T(8,128)(2,1)S(1)} %get-tuple-element.302), channel_id=1, source_target_pairs={{2,0},{3,1},{6,4},{7,5},{10,8},{11,9},{14,12},{15,13},{18,16},{19,... | collective-permute-start | bytes 1966088 | tf_op jit(solution)/shard_map/ppermute | solution.py:29
  996.5 74.3 %collective-permute-start.31 = (bf16[800,1376]{1,0:T(8,128)(2,1)}, bf16[800,1376]{1,0:T(8,128)(2,1)}, u32[]{:S(2)}, u32[]{:S(2)}) collective-permute-start(bf16[800,1376]{1,0:T(8,128)(2,1)} %add_convert_fusion.1), channel_id=1, source_target_pairs={{8,16},{16,8},{9,17},{17,9},{10,18},{18,10},{11,19},{19,11},{12,20... | collective-permute-start | bytes 6604808 | tf_op jit(solution)/shard_map/ppermute | solution.py:69
  998.5 72.3 %collective-permute-start.30 = (bf16[800,1376]{1,0:T(8,128)(2,1)}, bf16[800,1376]{1,0:T(8,128)(2,1)}, u32[]{:S(2)}, u32[]{:S(2)}) collective-permute-start(bf16[800,1376]{1,0:T(8,128)(2,1)} %add_convert_fusion.2), channel_id=1, source_target_pairs={{8,0},{16,24},{9,1},{17,25},{10,2},{18,26},{11,3},{19,27},{12,4},{... | collective-permute-start | bytes 6604808 | tf_op jit(solution)/shard_map/ppermute | solution.py:69
  1102.0 256.9 %reduce-scatter.18.cloned.1.call-start = ((), (), s32[]{:S(2)}) async-start(), calls=%async_computation.14 | async-start | bytes 5120000 | tf_op jit(solution)/shard_map/reduce_scatter | solution.py:124
  1105.6 12.5 collective-permute-start.39
  1112.4 20.0 %collective-permute-start.48 = (f32[7,1024]{1,0:T(8,128)S(1)}, f32[7,1024]{1,0:T(8,128)S(1)}, u32[]{:S(2)}, u32[]{:S(2)}) collective-permute-start(f32[7,1024]{1,0:T(8,128)S(1)} %reshape.230), channel_id=1, source_target_pairs={{0,4},{4,0},{1,5},{5,1},{2,6},{6,2},{3,7},{7,3},{8,12},{12,8},{9,1... | collective-permute-start | bytes 86024 | tf_op jit(solution)/shard_map/ppermute | solution.py:160
  1117.4 149.5 %collective-permute-start.36 = (bf16[400,800]{1,0:T(8,128)(2,1)}, bf16[400,800]{1,0:T(8,128)(2,1)S(1)}, u32[]{:S(2)}, u32[]{:S(2)}) collective-permute-start(bf16[400,800]{1,0:T(8,128)(2,1)} %copy.254), channel_id=1, source_target_pairs={{8,16},{16,8},{9,17},{17,9},{10,18},{18,10},{11,19},{19,11},{12,20... | collective-permute-start | bytes 1920008 | tf_op jit(solution)/shard_map/ppermute | solution.py:69
  1127.3 282.9 %all-reduce.14.cloned.1.call-start = ((), (), s32[]{:S(2)}) async-start(), calls=%async_computation.15 | async-start | bytes 2048000 | tf_op jit(solution)/shard_map/psum | solution.py:686
  1130.6 136.3 %collective-permute-start.35 = (bf16[800,800]{0,1:T(8,128)(2,1)}, bf16[800,800]{0,1:T(8,128)(2,1)}, u32[]{:S(2)}, u32[]{:S(2)}) collective-permute-start(bf16[800,800]{0,1:T(8,128)(2,1)} %add_convert_fusion.11), channel_id=1, source_target_pairs={{8,16},{16,8},{9,17},{17,9},{10,18},{18,10},{11,19},{19,11},{12,20... | collective-permute-start | bytes 3840008 | tf_op jit(solution)/shard_map/ppermute | solution.py:69
  1137.0 125.7 %collective-permute-start.46 = (bf16[800,1376]{1,0:T(8,128)(2,1)}, bf16[800,1376]{1,0:T(8,128)(2,1)}, u32[]{:S(2)}, u32[]{:S(2)}) collective-permute-start(bf16[800,1376]{1,0:T(8,128)(2,1)} %broadcast_select_fusion.1), channel_id=1, source_target_pairs={{0,4},{4,0},{1,5},{5,1},{2,6},{6,2},{3,7},{7,3},{8,12},{12,8},{9,1... | collective-permute-start | bytes 6604808 | tf_op jit(solution)/shard_map/ppermute | solution.py:33
  1143.1 123.8 %collective-permute-start.34 = (bf16[800,1376]{1,0:T(8,128)(2,1)}, bf16[800,1376]{1,0:T(8,128)(2,1)}, u32[]{:S(2)}, u32[]{:S(2)}) collective-permute-start(bf16[800,1376]{1,0:T(8,128)(2,1)} %add_convert_fusion), channel_id=1, source_target_pairs={{8,0},{16,24},{9,1},{17,25},{10,2},{18,26},{11,3},{19,27},{12,4},{... | collective-permute-start | bytes 6604808 | tf_op jit(solution)/shard_map/ppermute | solution.py:69
  1144.4 109.5 %collective-permute-start.51 = (f32[7,1024]{1,0:T(8,128)S(1)}, f32[7,1024]{1,0:T(8,128)S(1)}, u32[]{:S(2)}, u32[]{:S(2)}) collective-permute-start(f32[7,1024]{1,0:T(8,128)S(1)} %add.307), channel_id=1, source_target_pairs={{0,8},{8,0},{16,24},{24,16},{1,9},{9,1},{17,25},{25,17},{2,10},{10... | collective-permute-start | bytes 86024 | tf_op jit(solution)/shard_map/ppermute | solution.py:160
  1270.6 49.5 %collective-permute-start.37 = (bf16[800,800]{0,1:T(8,128)(2,1)}, bf16[800,800]{0,1:T(8,128)(2,1)}, u32[]{:S(2)}, u32[]{:S(2)}) collective-permute-start(bf16[800,800]{0,1:T(8,128)(2,1)} %add_convert_fusion.10), channel_id=1, source_target_pairs={{8,0},{16,24},{9,1},{17,25},{10,2},{18,26},{11,3},{19,27},{12,4},{... | collective-permute-start | bytes 3840008 | tf_op jit(solution)/shard_map/ppermute | solution.py:69
  1279.1 41.0 %collective-permute-start.38 = (bf16[400,800]{1,0:T(8,128)(2,1)}, bf16[400,800]{1,0:T(8,128)(2,1)S(1)}, u32[]{:S(2)}, u32[]{:S(2)}) collective-permute-start(bf16[400,800]{1,0:T(8,128)(2,1)} %copy.256), channel_id=1, source_target_pairs={{8,0},{16,24},{9,1},{17,25},{10,2},{18,26},{11,3},{19,27},{12,4},{... | collective-permute-start | bytes 1920008 | tf_op jit(solution)/shard_map/ppermute | solution.py:69
  1280.4 47.8 %collective-permute-start.42 = (bf16[400,1600]{1,0:T(8,128)(2,1)}, bf16[400,1600]{1,0:T(8,128)(2,1)}, u32[]{:S(2)}, u32[]{:S(2)}) collective-permute-start(bf16[400,1600]{1,0:T(8,128)(2,1)} %get-tuple-element.143), channel_id=1, source_target_pairs={{0,4},{4,0},{1,5},{5,1},{2,6},{6,2},{3,7},{7,3},{8,12},{12,8},{9,1... | collective-permute-start | bytes 3840008 | tf_op jit(solution)/shard_map/ppermute | solution.py:33
  1281.4 50.0 %collective-permute-start.41 = (bf16[400,1600]{1,0:T(8,128)(2,1)}, bf16[400,1600]{1,0:T(8,128)(2,1)}, u32[]{:S(2)}, u32[]{:S(2)}) collective-permute-start(bf16[400,1600]{1,0:T(8,128)(2,1)} %get-tuple-element.144), channel_id=1, source_target_pairs={{0,4},{4,0},{1,5},{5,1},{2,6},{6,2},{3,7},{7,3},{8,12},{12,8},{9,1... | collective-permute-start | bytes 3840008 | tf_op jit(solution)/shard_map/ppermute | solution.py:33
  1283.4 83.4 %collective-permute-start.47 = (bf16[800,1376]{1,0:T(8,128)(2,1)S(1)}, bf16[800,1376]{1,0:T(8,128)(2,1)}, u32[]{:S(2)}, u32[]{:S(2)}) collective-permute-start(bf16[800,1376]{1,0:T(8,128)(2,1)S(1)} %broadcast_select_fusion), channel_id=1, source_target_pairs={{0,4},{4,0},{1,5},{5,1},{2,6},{6,2},{3,7},{7,3},{8,12},{12,8},{9,1... | collective-permute-start | bytes 6604808 | tf_op jit(solution)/shard_map/ppermute | solution.py:33
  1323.7 30.4 %collective-permute-start.44 = (bf16[400,800]{1,0:T(8,128)(2,1)}, bf16[400,800]{1,0:T(8,128)(2,1)}, u32[]{:S(2)}, u32[]{:S(2)}) collective-permute-start(bf16[400,800]{1,0:T(8,128)(2,1)} %copy.259), channel_id=1, source_target_pairs={{0,4},{4,0},{1,5},{5,1},{2,6},{6,2},{3,7},{7,3},{8,12},{12,8},{9,1... | collective-permute-start | bytes 1920008 | tf_op jit(solution)/shard_map/ppermute | solution.py:33
  1328.1 88.4 %collective-permute-start.43 = (bf16[800,800]{0,1:T(8,128)(2,1)}, bf16[800,800]{0,1:T(8,128)(2,1)}, u32[]{:S(2)}, u32[]{:S(2)}) collective-permute-start(bf16[800,800]{0,1:T(8,128)(2,1)} %broadcast_select_fusion.13), channel_id=1, source_target_pairs={{0,4},{4,0},{1,5},{5,1},{2,6},{6,2},{3,7},{7,3},{8,12},{12,8},{9,1... | collective-permute-start | bytes 3840008 | tf_op jit(solution)/shard_map/ppermute | solution.py:33
  1410.2 17.8 %collective-permute-start.40 = (bf16[400,1280]{1,0:T(8,128)(2,1)}, bf16[400,1280]{1,0:T(8,128)(2,1)}, u32[]{:S(2)}, u32[]{:S(2)}) collective-permute-start(bf16[400,1280]{1,0:T(8,128)(2,1)} %all-reduce.14.cloned.1.call-done), channel_id=1, source_target_pairs={{0,4},{4,0},{1,5},{5,1},{2,6},{6,2},{3,7},{7,3},{8,12},{12,8},{9,1... | collective-permute-start | bytes 3072008 | tf_op jit(solution)/shard_map/ppermute | solution.py:33
  (96 other events, 2166.2 us)
Sparse Core Ops, SparseCore 0:
  15.7 52.5 all-gather.6
  79.7 128.3 all-gather.8
  210.6 68.8 all-gather.10
  281.8 45.6 all-gather.12
  347.8 78.0 all-gather.14
  427.6 72.1 all-gather.16
  563.3 74.5 reduce-scatter.13
  710.2 86.9 all-reduce.15
  800.9 65.5 reduce-scatter.19
  869.9 63.8 reduce-scatter.21
  937.3 97.2 reduce-scatter.15
  1038.1 63.8 reduce-scatter.23
  1104.4 142.2 all-reduce.17
  1250.5 51.6 reduce-scatter.17
  1359.0 51.1 all-reduce.13

commit v3 on v2

--- a/solution.py
+++ b/solution.py
@@ -577,8 +577,8 @@
     step_rows, cumul_rows, enter_rows, tail_rows = (pair_rows(v) for v in (step, cumul, enter, tail))
     drive, local = make_drive(front, step_rows, tail_rows, writer.T)
     state_in = state_from(local, carry_lanes, 1)
+    mixer_full = gathered(after(mixer_out, mamba_full, state_in), core)
     mixed_flat = mix(drive, cumul_rows, enter_rows, gram, bias, reader, state_in)
-    mixer_full = gathered(after(mixer_out, mamba_full, state_in), core)
     gated = (mixed_flat * jax.nn.silu(switch)).astype(jnp.bfloat16)
     mamba_y = project(gated, mamba_full)
     scale_att = inverse_rms(attended)
@@ -597,7 +597,7 @@
     active = lax.optimization_barrier((jax.nn.silu(gate) * up).astype(jnp.bfloat16))
     output_part = project(active, down_weight).astype(jnp.bfloat16)
     upstream = cotangent.astype(jnp.float32)
-    d_active = right_product(cotangent_all, down_weight)
+    d_active = right_product(after(cotangent_all, output_part), down_weight)
     d_gate = (d_active * up * silu_slope(gate)).astype(jnp.bfloat16)
     d_up = (d_active * jax.nn.silu(gate)).astype(jnp.bfloat16)
     feed_back = scattered(right_product(d_gate, gate_weight) + right_product(d_up, up_weight)).astype(
@@ -621,20 +621,21 @@
     d_mixed = (d_gated * jax.nn.silu(switch)).astype(jnp.bfloat16)
     d_switch = (d_gated * mixed_flat * silu_slope(switch)).astype(jnp.bfloat16)
     blend_both = jnp.concatenate([blend, swapped(blend)], 0)
-    mixer_part = left_product(blend_both, both_cores(d_branch, core)).astype(jnp.bfloat16)
+    mixer_half = scattered(left_product(blend_both, both_cores(d_branch, core)))
     gated_both = jnp.concatenate([gated, swapped(gated)], 0)
-    mamba_part = left_product(gated_both, both_cores(d_mamba, core)).astype(jnp.bfloat16)
-    mixer_half = scattered(mixer_part)
-    mamba_half = scattered(mamba_part)
-    d_mixed, d_switch = advance((d_mixed, d_switch, mixer_part, mamba_part), [gate_sum], [up_sum, down_sum])[:2]
-    switch_half = scattered(left_product(normed_both, both_cores(d_switch, core)))
+    mamba_half = scattered(left_product(gated_both, both_cores(d_mamba, core)))
+    d_mixed, d_switch = advance((d_mixed, d_switch), [gate_sum], [up_sum, down_sum])
     state_grad = leave_back(d_mixed, enter_rows, reader.T)
     d_state = state_from(state_grad, carry_lanes, -1)
+    d_switch = after(d_switch, state_grad)
+    switch_half = scattered(left_product(normed_both, both_cores(d_switch, core)))
+    d_state = advance(d_state, [gate_sum, up_sum], [down_sum])
     d_signal, d_gram_t, d_reader_state, d_writer_state, stats, sums = mix_back(
         d_mixed, mixed_flat, drive, front, step_rows, cumul_rows, enter_rows, tail_rows, gram.T, bias.T, writer,
         state_in, d_state,
     )
-    d_signal = advance((d_signal, mixer_half), [gate_sum, up_sum], [down_sum])[0]
+    d_signal = advance((d_signal, mixer_half), [gate_sum, up_sum, down_sum])[0]
+    mamba_sum, mixer_sum, switch_sum = ChipSum(mamba_half), ChipSum(mixer_half), ChipSum(switch_half)
     signal_part = left_product(normed_both, both_cores(d_signal, core)).astype(jnp.bfloat16)
     signal_half = scattered(signal_part)
     d_attended = after(d_attended, signal_part)
@@ -650,13 +651,12 @@
     d_reader = (left_product(d_gram_t, writer) + d_reader_state).astype(jnp.bfloat16)
     d_writer = (project(d_gram_t, reader) + d_writer_state).astype(jnp.bfloat16)
     d_query, d_window = attend_back(low, query, window, attended, logsum, d_attended)
-    d_window = advance((d_window, mamba_half, switch_half), [gate_sum, up_sum, down_sum])[0]
-    mamba_sum, mixer_sum = ChipSum(mamba_half), ChipSum(mixer_half)
+    d_window = advance(d_window, [up_sum, down_sum, mamba_sum, mixer_sum], [switch_sum])
     own_grads = d_window[blocks * count :]
     for distance in range(1, blocks + 1):
         away = d_window[(blocks - distance) * count : (blocks - distance + 1) * count]
         own_grads = own_grads + moved(away.astype(jnp.bfloat16), "shard", -distance).astype(jnp.float32)
-    own_grads = after(own_grads, output_half)
+    own_grads = advance((own_grads, output_half), [down_sum, mamba_sum, mixer_sum, switch_sum])[0]
     d_small = jnp.pad(jnp.concatenate([d_writer, d_reader, d_step_raw], 1), ((0, 0), (0, 128 - lead)))
     d_pair = own_grads.astype(jnp.bfloat16)
     d_last = jnp.concatenate([d_query, d_pair, d_small], 1)
@@ -666,8 +666,7 @@
     d_front = jnp.concatenate([d_signal, d_switch, d_small], 1)
     d_query_pair = jnp.pad(jnp.concatenate([d_query, d_pair], 1), ((0, 0), (0, spare)))
     d_normed = right_product(d_front, front_full) + right_product(d_query_pair, query_pair_full)
-    d_normed = advance((d_normed, signal_half), [up_sum, down_sum, mamba_sum, mixer_sum])[0]
-    switch_sum, signal_sum = lax.psum((switch_half, signal_half), "zz")
+    d_normed = advance((d_normed, signal_half), [mamba_sum, mixer_sum, switch_sum])[0]
     attention_gain_part = jnp.sum(d_normed * unit_one, axis=0)
     token_gradient = (d_middle + rms_back(d_normed * attention_gain, unit_one, scale_one)).astype(
         jnp.bfloat16
@@ -679,12 +678,10 @@
     small = jnp.pad(small, (0, -length % 1024)).reshape(-1, 1024)
     small = sum_over_axis(sum_over_axis(small, "core"), "shard")
     output = (middle + output_half.astype(jnp.float32)).astype(jnp.bfloat16)
-    small = sum_over_axis(small, "zz").reshape(-1)
-    token_gradient, switch_sum, signal_sum = advance(
-        (token_gradient, switch_sum, signal_sum), [down_sum, mamba_sum, mixer_sum]
-    )
-    last_sum = lax.psum(after(last_half, switch_sum, signal_sum), "zz")
-    token_gradient = advance(token_gradient, [mamba_sum, mixer_sum])
+    signal_half, last_half = lax.optimization_barrier((signal_half, last_half))
+    signal_sum, last_sum = lax.psum((signal_half, last_half), "zz")
+    small = sum_over_axis(after(small, last_sum), "zz").reshape(-1)
+    token_gradient = advance(token_gradient, [switch_sum])
     last_gradient = both_halves(last_sum, core, 1)
     pair_gradient = last_gradient[:, wide : wide + PAIR_WIDTH].reshape(rows, KV_HEADS, 2, HEAD_DIM)
     base = wide + PAIR_WIDTH
@@ -697,7 +694,7 @@
         last_gradient[:, :wide],
         pair_gradient[:, :, 0].reshape(rows, KV_HEADS * HEAD_DIM),
         pair_gradient[:, :, 1].reshape(rows, KV_HEADS * HEAD_DIM),
-        jnp.concatenate([both_halves(signal_sum, core, 1), both_halves(switch_sum, core, 1)], 1),
+        jnp.concatenate([both_halves(signal_sum, core, 1), both_halves(switch_sum.part, core, 1)], 1),
         last_gradient[:, base : base + 2 * STATE],
         last_gradient[:, base + 2 * STATE : base + lead],
         both_halves(mamba_sum.part, core, 1),

time: 1460 us -> 1350 us (0.925)
  waiting for transfers between devices: 510 us -> 435 us
  local copies, waits for them, and re-layouts: 172 us -> 130 us
    ppermute x5, waiting for transfers between devices: 104 us -> 1.83 us  [sum_over_axis(): lax.ppermute(values, axis, [(i, i ^ distance) for i in range(size)])]
    ppermute x15 -> x18, waiting for transfers between devices: 36.2 us -> 103 us  [send(): return lax.ppermute(self.part, 'zz', self.routes[self.step])]
    unnamed x19 -> x14, waiting for transfers between devices: 31.9 us -> 0.74 us
    reduce_scatter x3 -> x4, waiting for transfers between devices: 28.3 us -> 4.24 us  [scattered(): lax.psum_scatter(part.astype(jnp.bfloat16), 'shard', scatter_dimension=ax...]
    all_gather x1, waiting for transfers between devices: 41.5 us -> 20 us  [body(): lax.all_gather(after(cotangent, feed_in), 'shard', axis=0, tiled=True)]
    unnamed x199 -> x233, local copies, waits for them, and re-layouts: 59.3 us -> 40.1 us
    psum x2 -> x1, waiting for transfers between devices: 39.3 us -> 58.2 us  [body(): signal_sum, last_sum = lax.psum((signal_half, last_half), 'zz')]
    ppermute x15 -> x18, starting transfers between devices: 33.9 us -> 46.1 us  [send(): return lax.ppermute(self.part, 'zz', self.routes[self.step])]
  transfers between devices with their start and end apart: 68 -> 70, of which waited for: 17 -> 23; matrix products, arithmetic and copies ran while one was open for 37% -> 35% of each run, Pallas kernels for 12% -> 13%
where the time goes in v3:
time: 1350 us; the launch traced here: 1340 us
  waiting for transfers between devices  435 us (32%)
  matrix products  313 us (23%)
  Pallas kernels  179 us (13%)
  other arithmetic  174 us (13%)
  local copies, waits for them, and re-layouts  130 us (10%)
  starting transfers between devices  92.8 us (7%)
  between operations  16.7 us (1%)
    dot_general x8, matrix products, right_product(): lax.dot_general(left, right, (((1,), (1,)), ((), ())), preferred_element_...  114 us
    dot_general x8, matrix products, project(): return jnp.dot(left, right, preferred_element_type=jnp.float32)  106 us
    ppermute x18, waiting for transfers between devices, send(): return lax.ppermute(self.part, 'zz', self.routes[self.step])  103 us
    dot_general x9, matrix products, left_product(): lax.dot_general(left, right, (((0,), (0,)), ((), ())), preferred_element_...  93.3 us
    ppermute x14, waiting for transfers between devices, moved(): return lax.ppermute(block, axis, route)  83.4 us
    all_gather x4, waiting for transfers between devices, gathered(): return lax.all_gather(half, ('shard', 'core'), axis=0, tiled=True)  80.7 us
    all_gather x1, waiting for transfers between devices, body(): feed_all = lax.all_gather(feed_in, 'shard', axis=0, tiled=True)  77.6 us
    psum x1, waiting for transfers between devices, body(): signal_sum, last_sum = lax.psum((signal_half, last_half), 'zz')  58.2 us
  transfers between devices with their start and end apart: 70, of which 23 were waited for; matrix products, arithmetic and copies ran while one was open for 35% of the time, Pallas kernels for 13%

profile of v3, /device:TPU:1, one launch (start us, length us, event | category | flops | bytes accessed | tf_op | source)
XLA Modules:
  0.0 1340.8 jit_solution(4319161268904440824)
XLA Ops:
  24.4 5.6 fusion.12
  30.0 38.3 %all-gather.7.cloned.1.call-done = bf16[1600,2304]{1,0:T(8,128)(2,1)} async-done(((bf16[200,2304]{1,0:T(8,128)(2,1)}), bf16[1600,2304]{1,0:T(8,128)(2,1)}) %all-gather.7.cloned.1.call-update) | async-done | bytes 7372816 | tf_op jit(solution)/shard_map/all_gather | solution.py:102
  68.3 9.6 convolution_convert_fusion.8
  92.3 29.6 %collective-permute-done = bf16[512,640]{1,0:T(8,128)(2,1)} collective-permute-done((bf16[512,640]{1,0:T(8,128)(2,1)S(1)}, bf16[512,640]{1,0:T(8,128)(2,1)}, u32[]{:S(2)}, u32[]{:S(2)}) %collective-permute-start) | collective-permute-done | bytes 655392 | tf_op jit(solution)/shard_map/ppermute | solution.py:29
  124.6 49.7 %attend.1 = (f32[512,1600]{1,0:T(8,128)}, f32[25,1,512]{2,1,0:T(1,128)}) custom-call(s32[1,512]{1,0:T(1,128)} %bitcast.87, bf16[512,1600]{1,0:T(8,128)(2,1)} %slice.195.query_ref, bf16[1536,640]{1,0:T(8,128)(2,1)} %pad_maximum_fusion.1.pair_ref), custom_call_target="tpu_custom_call" | custom-call | tf_op jit(solution)/shard_map/attend/pallas_call | solution.py:215
  174.3 33.8 %all-gather.9.cloned.1.call-done = bf16[1600,6528]{1,0:T(8,128)(2,1)} async-done(((bf16[200,6528]{1,0:T(8,128)(2,1)}), bf16[1600,6528]{1,0:T(8,128)(2,1)}) %all-gather.9.cloned.1.call-update) | async-done | bytes 20889616 | tf_op jit(solution)/shard_map/all_gather | solution.py:102
  211.4 21.1 %fusion.95 = (bf16[512,6528]{1,0:T(8,128)(2,1)}, f32[512,6528]{1,0:T(8,128)}) fusion(bf16[512,1600]{1,0:T(8,128)(2,1)} %fusion.22, bf16[1600,6528]{1,0:T(8,128)(2,1)} %all-gather.9.cloned.1.call-done), kind=kOutput, calls=%fused_computation.238 | convolution fusion | flops 10698817536 | bytes 42582016 | tf_op jit(solution)/shard_map/dot_general | solution.py:128
  239.8 9.2 make_drive.1
  258.5 12.2 collective-permute-done.3
  270.9 8.6 all-gather.11.cloned.1.call-done
  286.5 20.5 %mix.1.mixed_ref = f32[512,3200]{1,0:T(8,128)S(1)} custom-call(bf16[512,3200]{1,0:T(8,128)(2,1)S(1)} %copy-done.3, f32[25,2,512]{2,1,0:T(2,128)S(1)} %reduce_window_sum.33.cumul_ref, f32[25,2,512]{2,1,0:T(2,128)S(1)} %get-tuple-element.332.enter_ref, f32[512,512]{1,0:T(8,128)S(1)} %fusion.84.gram_ref, f32[512,512]{1,0:T(8,128)S(1)} %get-tuple-element.339.bias_ref, ...), custom_call_target="tpu_custom_call" | custom-call | tf_op jit(solution)/shard_map/mix/pallas_call | solution.py:412
  314.1 12.7 multiply_reduce_fusion.8
  326.8 4.6 copy.205
  331.5 5.0 multiply_convert_fusion.9
  336.5 7.1 multiply_reduce_fusion.6
  347.6 77.6 %all-gather.15.cloned.1.call-done = bf16[2048,1600]{1,0:T(8,128)(2,1)} async-done(((bf16[512,1600]{1,0:T(8,128)(2,1)}), bf16[2048,1600]{1,0:T(8,128)(2,1)}) %all-gather.15.cloned.1.call-update) | async-done | bytes 6553616 | tf_op jit(solution)/shard_map/all_gather | solution.py:593
  425.2 16.6 %fusion.96 = f32[2048,1376]{0,1:T(8,128)} fusion(bf16[2048,1600]{1,0:T(8,128)(2,1)} %all-gather.15.cloned.1.call-done, bf16[1600,1376]{1,0:T(8,128)(2,1)} %param.32), kind=kOutput, calls=%fused_computation.239 | convolution fusion | flops 9017753600 | bytes 22228992 | tf_op jit(solution)/shard_map/dot_general | solution.py:128
  441.8 20.4 %multiply_convert_fusion.2 = (bf16[2048,1376]{0,1:T(8,128)(2,1)}, f32[2048,1376]{0,1:T(8,128)}) fusion(f32[2048,1376]{0,1:T(8,128)} %fusion.96, bf16[2048,1600]{1,0:T(8,128)(2,1)} %all-gather.15.cloned.1.call-done, bf16[1600,1376]{1,0:T(8,128)(2,1)} %param.33), kind=kOutput, calls=%fused_computation.2 | convolution fusion | flops 9034661888 | bytes 39137280 | tf_op jit(solution)/shard_map/dot_general | solution.py:128
  462.1 17.0 %convolution_convert_fusion.4 = bf16[2048,1600]{1,0:T(8,128)(2,1)} fusion(bf16[2048,1376]{0,1:T(8,128)(2,1)} %get-tuple-element.346, bf16[1376,1600]{0,1:T(8,128)(2,1)} %param.34), kind=kOutput, calls=%fused_computation.13 | convolution fusion | flops 9021030400 | bytes 16592896 | tf_op jit(solution)/shard_map/dot_general | solution.py:128
  479.1 20.0 %all-gather.17.cloned.1.call-done = bf16[2048,1600]{0,1:T(8,128)(2,1)} async-done(((bf16[512,1600]{0,1:T(8,128)(2,1)}), bf16[2048,1600]{0,1:T(8,128)(2,1)}) %all-gather.17.cloned.1.call-update) | async-done | bytes 6553616 | tf_op jit(solution)/shard_map/all_gather | solution.py:594
  499.1 25.7 %multiply_convert_fusion = (bf16[2048,1376]{0,1:T(8,128)(2,1)}, bf16[2048,1376]{0,1:T(8,128)(2,1)}) fusion(f32[2048,1376]{0,1:T(8,128)} %fusion.96, f32[2048,1376]{0,1:T(8,128)} %get-tuple-element.347, bf16[2048,1600]{0,1:T(8,128)(2,1)} %all-gather.17.cloned.1.call-done, bf16[1376,1600]{0,1:T(8,128)(2,1)} %param.34), kind=kOutput, calls=%fused_computation | convolution fusion | flops 9054388224 | bytes 44773376 | tf_op jit(solution)/shard_map/dot_general | solution.py:138
  524.8 14.0 %fusion.97 = f32[2048,1600]{0,1:T(8,128)S(1)} fusion(bf16[1600,1376]{1,0:T(8,128)(2,1)} %param.32, bf16[2048,1376]{0,1:T(8,128)(2,1)} %get-tuple-element.283), kind=kOutput, calls=%fused_computation.240 | convolution fusion | flops 9017753600 | bytes 23146496 | tf_op jit(solution)/shard_map/dot_general | solution.py:138
  538.9 16.0 %convolution_add_fusion = bf16[2048,1600]{0,1:T(8,128)(2,1)} fusion(f32[2048,1600]{0,1:T(8,128)S(1)} %fusion.97, bf16[1600,1376]{1,0:T(8,128)(2,1)} %param.33, bf16[2048,1376]{0,1:T(8,128)(2,1)} %get-tuple-element.282), kind=kOutput, calls=%fused_computation.8 | convolution fusion | flops 9024307200 | bytes 29700096 | tf_op jit(solution)/shard_map/dot_general | solution.py:138
  554.8 9.5 copy.211
  564.4 14.3 %convolution_convert_fusion.3 = bf16[1600,1376]{1,0:T(8,128)(2,1)S(1)} fusion(bf16[2048,1600]{0,1:T(8,128)(2,1)} %all-gather.17.cloned.1.call-done, bf16[2048,1376]{0,1:T(8,128)(2,1)} %get-tuple-element.346), kind=kOutput, calls=%fused_computation.12 | convolution fusion | flops 9019955200 | bytes 16592896 | tf_op jit(solution)/shard_map/dot_general | solution.py:132
  581.0 17.4 %convolution_convert_fusion.5 = bf16[1600,1376]{1,0:T(8,128)(2,1)S(1)} fusion(bf16[2048,1600]{1,0:T(8,128)(2,1)} %all-gather.15.cloned.1.call-done, bf16[2048,1376]{0,1:T(8,128)(2,1)} %get-tuple-element.282), kind=kOutput, calls=%fused_computation.14 | convolution fusion | flops 9019955200 | bytes 16592896 | tf_op jit(solution)/shard_map/dot_general | solution.py:132
  600.6 11.9 convolution_convert_fusion.6
  623.2 4.6 add_convert_fusion.6
  634.9 4.2 reduce-scatter.14.cloned.1.call-done
  654.5 7.3 convolution_convert_fusion.9
  662.1 9.9 multiply_reduce_fusion.1
  681.9 11.4 convolution_convert_fusion.7
  693.3 4.7 collective-permute-start.11
  702.9 15.8 %multiply_convert_fusion.3 = (bf16[512,3200]{1,0:T(8,128)(2,1)}, bf16[512,3200]{1,0:T(8,128)(2,1)}) fusion(f32[512,3200]{1,0:T(8,128)} %copy-done.2, f32[512,6528]{1,0:T(8,128)} %get-tuple-element.341.signal_ref, bf16[512,1600]{1,0:T(8,128)(2,1)} %copy-done.36, bf16[3200,1600]{1,0:T(8,128)(2,1)} %all-gather.11.cloned.1.call-done), kind=kOutput, calls=%fused_computation.26 | convolution fusion | flops 5264179200 | bytes 31539200 | tf_op jit(solution)/shard_map/dot_general | solution.py:138
  718.7 26.2 %collective-permute-done.11 = bf16[800,1376]{1,0:T(8,128)(2,1)} collective-permute-done((bf16[800,1376]{1,0:T(8,128)(2,1)}, bf16[800,1376]{1,0:T(8,128)(2,1)}, u32[]{:S(2)}, u32[]{:S(2)}) %collective-permute-start.11) | collective-permute-done | bytes 2201632 | tf_op jit(solution)/shard_map/ppermute | solution.py:69
  744.9 6.1 leave_back.1
  751.0 4.8 broadcast_select_fusion.10
  767.5 11.7 convolution_convert_fusion.1
  783.1 6.6 collective-permute-start.18
  798.2 7.8 collective-permute-done.12
  808.6 7.9 collective-permute-done.16
  816.6 20.8 %collective-permute-done.18 = bf16[800,1376]{1,0:T(8,128)(2,1)S(1)} collective-permute-done((bf16[800,1376]{1,0:T(8,128)(2,1)S(1)}, bf16[800,1376]{1,0:T(8,128)(2,1)S(1)}, u32[]{:S(2)}, u32[]{:S(2)}) %collective-permute-start.18) | collective-permute-done | bytes 2201632 | tf_op jit(solution)/shard_map/ppermute | solution.py:69
  844.7 7.3 collective-permute-start.23
  855.5 42.2 %mix_back.1 = (bf16[512,3200]{1,0:T(8,128)(2,1)}, f32[512,512]{1,0:T(8,128)S(1)}, f32[512,16]{1,0:T(8,128)S(1)}, f32[512,16]{1,0:T(8,128)S(1)}, f32[25,4,512]{2,1,0:T(4,128)S(1)}, /*index=5*/f32[25,2,128]{2,1,0:T(2,128)S(1)}) custom-call(bf16[512,3200]{1,0:T(8,128)(2,1)} %get-tuple-element.111.d_mixed_ref, f32[512,3200]{1,0:T(8,128)} %copy-done.2, ...), custom_call_target="tpu_custom_call" | custom-call | tf_op jit(solution)/shard_map/mix_back/pallas_call | solution.py:495
  899.4 4.4 broadcast_select_fusion.12
  916.4 11.1 convolution_convert_fusion.2
  933.8 4.4 add_convert_fusion.1
  940.4 4.7 add_convert_fusion.2
  950.6 6.5 collective-permute-start.29
  961.1 51.0 %attend_back.1 = (bf16[512,1600]{1,0:T(8,128)(2,1)}, f32[1536,640]{1,0:T(8,128)}) custom-call(s32[1,512]{1,0:T(1,128)} %bitcast.88, bf16[512,1600]{1,0:T(8,128)(2,1)} %slice.195.query_ref, bf16[1536,640]{1,0:T(8,128)(2,1)} %pad_maximum_fusion.1.pair_ref, f32[512,1600]{1,0:T(8,128)} %get-tuple-element.102.out_ref, ...), custom_call_target="tpu_custom_call" | custom-call | tf_op jit(solution)/shard_map/attend_back/pallas_call | solution.py:300
  1012.1 4.3 broadcast_select_fusion.8
  1027.9 4.3 maximum_convert_fusion
  1034.9 21.3 %collective-permute-done.32 = bf16[512,640]{1,0:T(8,128)(2,1)S(1)} collective-permute-done((bf16[512,640]{1,0:T(8,128)(2,1)S(1)}, bf16[512,640]{1,0:T(8,128)(2,1)S(1)}, u32[]{:S(2)}, u32[]{:S(2)}) %collective-permute-start.32) | collective-permute-done | bytes 655392 | tf_op jit(solution)/shard_map/ppermute | solution.py:29
  1064.9 22.2 %collective-permute-done.37 = bf16[400,1600]{1,0:T(8,128)(2,1)S(1)} collective-permute-done((bf16[400,1600]{1,0:T(8,128)(2,1)S(1)}, bf16[400,1600]{1,0:T(8,128)(2,1)S(1)}, u32[]{:S(2)}, u32[]{:S(2)}) %collective-permute-start.37) | collective-permute-done | bytes 1280032 | tf_op jit(solution)/shard_map/ppermute | solution.py:69
  1095.5 4.2 maximum_convert_fusion.1
  1108.2 7.0 convolution_convert_fusion
  1120.9 9.7 fusion.43
  1130.6 21.4 %fusion.19 = f32[512,1600]{1,0:T(8,128)} fusion(f32[512,1600]{1,0:T(8,128)} %fusion.43, bf16[1600,6528]{1,0:T(8,128)(2,1)} %all-gather.9.cloned.1.call-done, bf16[512,128]{1,0:T(8,128)(2,1)S(1)} %copy-done.71, bf16[512,3200]{1,0:T(8,128)(2,1)S(1)} %copy-done.51, bf16[512,3200]{1,0:T(8,128)(2,1)S(1)} %copy-done.52), kind=kOutput, calls=%fused_computation.55 | convolution fusion | flops 10716348416 | bytes 34127872 | tf_op jit(solution)/shard_map/dot_general | solution.py:138
  1175.6 5.3 fusion.27
  1189.3 30.3 %collective-permute-done.41 = bf16[400,1600]{1,0:T(8,128)(2,1)} collective-permute-done((bf16[400,1600]{1,0:T(8,128)(2,1)}, bf16[400,1600]{1,0:T(8,128)(2,1)}, u32[]{:S(2)}, u32[]{:S(2)}) %collective-permute-start.41) | collective-permute-done | bytes 1280032 | tf_op jit(solution)/shard_map/ppermute | solution.py:69
  1231.5 58.2 %all-reduce.12.cloned.1.call-done = (bf16[400,1280]{1,0:T(8,128)(2,1)}, bf16[400,1600]{1,0:T(8,128)(2,1)}) async-done(((bf16[400,1280]{1,0:T(8,128)(2,1)}, bf16[400,1600]{1,0:T(8,128)(2,1)}), (bf16[400,1280]{1,0:T(8,128)(2,1)}, bf16[400,1600]{1,0:T(8,128)(2,1)})) %all-reduce.12.cloned.1.call-update) | async-done | bytes 2304016 | tf_op jit(solution)/shard_map/psum | solution.py:682
  1290.3 5.0 maximum_convert_fusion.2
  1318.4 8.4 concatenate.101
  1326.7 7.3 concatenate.102
  (528 shorter events, 306.0 us)
Async XLA Ops:
  7.2 61.1 %all-gather.7.cloned.1.call-start = ((), (), s32[]{:S(2)}) async-start(), calls=%async_computation.7 | async-start | bytes 8294400 | tf_op jit(solution)/shard_map/all_gather | solution.py:102
  15.6 192.6 %all-gather.9.cloned.1.call-start = ((), (), s32[]{:S(2)}) async-start(), calls=%async_computation.8 | async-start | bytes 23500800 | tf_op jit(solution)/shard_map/all_gather | solution.py:102
  79.6 199.8 %all-gather.11.cloned.1.call-start = ((), (), s32[]{:S(2)}) async-start(), calls=%async_computation.9 | async-start | bytes 11980800 | tf_op jit(solution)/shard_map/all_gather | solution.py:102
  81.1 40.8 %collective-permute-start = (bf16[512,640]{1,0:T(8,128)(2,1)S(1)}, bf16[512,640]{1,0:T(8,128)(2,1)}, u32[]{:S(2)}, u32[]{:S(2)}) collective-permute-start(bf16[512,640]{1,0:T(8,128)(2,1)S(1)} %slice.196), channel_id=1, source_target_pairs={{0,2},{1,3},{4,6},{5,7},{8,10},{9,11},{12,14},{13,15},{16,18},{17,... | collective-permute-start | bytes 1966088 | tf_op jit(solution)/shard_map/ppermute | solution.py:29
  84.8 37.2 %collective-permute-start.1 = (bf16[512,640]{1,0:T(8,128)(2,1)S(1)}, bf16[512,640]{1,0:T(8,128)(2,1)}, u32[]{:S(2)}, u32[]{:S(2)}) collective-permute-start(bf16[512,640]{1,0:T(8,128)(2,1)S(1)} %slice.196), channel_id=1, source_target_pairs={{0,1},{1,2},{2,3},{4,5},{5,6},{6,7},{8,9},{9,10},{10,11},{12,13},{... | collective-permute-start | bytes 1966088 | tf_op jit(solution)/shard_map/ppermute | solution.py:29
  209.3 127.3 %all-gather.13.cloned.1.call-start = ((), (), s32[]{:S(2)}) async-start(), calls=%async_computation.10 | async-start | bytes 5990400 | tf_op jit(solution)/shard_map/all_gather | solution.py:102
  249.0 21.7 %collective-permute-start.2 = (f32[16,3200]{1,0:T(8,128)}, f32[16,3200]{1,0:T(8,128)S(1)}, u32[]{:S(2)}, u32[]{:S(2)}) collective-permute-start(f32[16,3200]{1,0:T(8,128)} %get-tuple-element.105), channel_id=1, source_target_pairs={{0,1},{1,2},{2,3},{4,5},{5,6},{6,7},{8,9},{9,10},{10,11},{12,13},{... | collective-permute-start | bytes 614408 | tf_op jit(solution)/shard_map/ppermute | solution.py:29
  252.2 18.6 %collective-permute-start.4 = (f32[16,3200]{1,0:T(8,128)}, f32[16,3200]{1,0:T(8,128)S(1)}, u32[]{:S(2)}, u32[]{:S(2)}) collective-permute-start(f32[16,3200]{1,0:T(8,128)} %get-tuple-element.105), channel_id=1, source_target_pairs={{0,2},{1,3},{4,6},{5,7},{8,10},{9,11},{12,14},{13,15},{16,18},{17,... | collective-permute-start | bytes 614408 | tf_op jit(solution)/shard_map/ppermute | solution.py:29
  254.4 16.4 %collective-permute-start.6 = (f32[16,3200]{1,0:T(8,128)}, f32[16,3200]{1,0:T(8,128)S(1)}, u32[]{:S(2)}, u32[]{:S(2)}) collective-permute-start(f32[16,3200]{1,0:T(8,128)} %get-tuple-element.105), channel_id=1, source_target_pairs={{0,3},{4,7},{8,11},{12,15},{16,19},{20,23},{24,27},{28,31}} | collective-permute-start | bytes 614408 | tf_op jit(solution)/shard_map/ppermute | solution.py:29
  255.9 14.8 %collective-permute-start.3 = (f32[1,3200]{1,0:T(1,128)S(1)}, f32[1,3200]{1,0:T(1,128)S(1)}, u32[]{:S(2)}, u32[]{:S(2)}) collective-permute-start(f32[1,3200]{1,0:T(1,128)S(1)} %broadcast_in_dim_reshape.3), channel_id=1, source_target_pairs={{0,1},{1,2},{2,3},{4,5},{5,6},{6,7},{8,9},{9,10},{10,11},{12,13},{... | collective-permute-start | bytes 38408 | tf_op jit(solution)/shard_map/ppermute | solution.py:29
  257.2 13.5 %collective-permute-start.5 = (f32[1,3200]{1,0:T(1,128)S(1)}, f32[1,3200]{1,0:T(1,128)S(1)}, u32[]{:S(2)}, u32[]{:S(2)}) collective-permute-start(f32[1,3200]{1,0:T(1,128)S(1)} %broadcast_in_dim_reshape.3), channel_id=1, source_target_pairs={{0,2},{1,3},{4,6},{5,7},{8,10},{9,11},{12,14},{13,15},{16,18},{17,... | collective-permute-start | bytes 38408 | tf_op jit(solution)/shard_map/ppermute | solution.py:29
  281.4 143.7 %all-gather.15.cloned.1.call-start = ((), (), s32[]{:S(2)}) async-start(), calls=%async_computation.11 | async-start | bytes 8519680 | tf_op jit(solution)/shard_map/all_gather | solution.py:593
  347.0 152.1 %all-gather.17.cloned.1.call-start = ((), (), s32[]{:S(2)}) async-start(), calls=%async_computation.12 | async-start | bytes 8192000 | tf_op jit(solution)/shard_map/all_gather | solution.py:594
  347.6 291.6 %reduce-scatter.14.cloned.1.call-start = ((), (), s32[]{:S(2)}) async-start(), calls=%async_computation.13 | async-start | bytes 8519680 | tf_op jit(solution)/shard_map/reduce_scatter | solution.py:124
  564.4 335.0 %reduce-scatter.22.cloned.1.call-start = ((), (), s32[]{:S(2)}) async-start(), calls=%async_computation.17 | async-start | bytes 3584000
  580.3 42.8 %collective-permute-start.10 = (bf16[800,1376]{1,0:T(8,128)(2,1)}, bf16[800,1376]{1,0:T(8,128)(2,1)}, u32[]{:S(2)}, u32[]{:S(2)}) collective-permute-start(bf16[800,1376]{1,0:T(8,128)(2,1)} %constant_dynamic-slice_fusion), channel_id=1, source_target_pairs={{0,4},{4,0},{1,5},{5,1},{2,6},{6,2},{3,7},{7,3},{8,12},{12,8},{9,1... | collective-permute-start | bytes 6604808 | tf_op jit(solution)/shard_map/ppermute | solution.py:33
  600.1 27.6 %collective-permute-start.9 = (bf16[800,1376]{1,0:T(8,128)(2,1)}, bf16[800,1376]{1,0:T(8,128)(2,1)}, u32[]{:S(2)}, u32[]{:S(2)}) collective-permute-start(bf16[800,1376]{1,0:T(8,128)(2,1)} %constant_dynamic-slice_fusion.1), channel_id=1, source_target_pairs={{0,4},{4,0},{1,5},{5,1},{2,6},{6,2},{3,7},{7,3},{8,12},{12,8},{9,1... | collective-permute-start | bytes 6604808 | tf_op jit(solution)/shard_map/ppermute | solution.py:33
  615.4 15.9 %collective-permute-start.8 = (bf16[800,1376]{1,0:T(8,128)(2,1)}, bf16[800,1376]{1,0:T(8,128)(2,1)}, u32[]{:S(2)}, u32[]{:S(2)}) collective-permute-start(bf16[800,1376]{1,0:T(8,128)(2,1)} %constant_dynamic-slice_fusion.2), channel_id=1, source_target_pairs={{0,4},{4,0},{1,5},{5,1},{2,6},{6,2},{3,7},{7,3},{8,12},{12,8},{9,1... | collective-permute-start | bytes 6604808 | tf_op jit(solution)/shard_map/ppermute | solution.py:33
  622.7 26.3 %collective-permute-start.19 = (bf16[512,1600]{0,1:T(8,128)(2,1)}, bf16[512,1600]{0,1:T(8,128)(2,1)}, u32[]{:S(2)}, u32[]{:S(2)}) collective-permute-start(bf16[512,1600]{0,1:T(8,128)(2,1)} %copy.215), channel_id=1, source_target_pairs={{0,4},{4,0},{1,5},{5,1},{2,6},{6,2},{3,7},{7,3},{8,12},{12,8},{9,1... | collective-permute-start | bytes 4915208 | tf_op jit(solution)/shard_map/ppermute | solution.py:33
  661.9 288.7 %reduce-scatter.18.cloned.1.call-start = ((), (), s32[]{:S(2)}) async-start(), calls=%async_computation.15 | async-start | bytes 7168000 | tf_op jit(solution)/shard_map/reduce_scatter | solution.py:124
  662.0 19.9 %collective-permute-start.27 = (bf16[512,3200]{1,0:T(8,128)(2,1)}, bf16[512,3200]{1,0:T(8,128)(2,1)}, u32[]{:S(2)}, u32[]{:S(2)}) collective-permute-start(bf16[512,3200]{1,0:T(8,128)(2,1)} %copy-done.53), channel_id=1, source_target_pairs={{0,4},{4,0},{1,5},{5,1},{2,6},{6,2},{3,7},{7,3},{8,12},{12,8},{9,1... | collective-permute-start | bytes 9830408 | tf_op jit(solution)/shard_map/ppermute | solution.py:33
  693.3 324.0 %reduce-scatter.24.cloned.1.call-start = ((), (), s32[]{:S(2)}) async-start(), calls=%async_computation.18 | async-start | bytes 6656000
  693.3 51.6 %collective-permute-start.11 = (bf16[800,1376]{1,0:T(8,128)(2,1)}, bf16[800,1376]{1,0:T(8,128)(2,1)}, u32[]{:S(2)}, u32[]{:S(2)}) collective-permute-start(bf16[800,1376]{1,0:T(8,128)(2,1)} %add_convert_fusion.8), channel_id=1, source_target_pairs={{0,8},{24,16},{1,9},{25,17},{2,10},{26,18},{3,11},{27,19},{4,12},{... | collective-permute-start | bytes 6604808 | tf_op jit(solution)/shard_map/ppermute | solution.py:69
  701.6 58.5 %collective-permute-start.7 = (bf16[512,1600]{0,1:T(8,128)(2,1)}, bf16[512,1600]{0,1:T(8,128)(2,1)}, u32[]{:S(2)}, u32[]{:S(2)}) collective-permute-start(bf16[512,1600]{0,1:T(8,128)(2,1)} %copy.208), channel_id=1, source_target_pairs={{0,4},{4,0},{1,5},{5,1},{2,6},{6,2},{3,7},{7,3},{8,12},{12,8},{9,1... | collective-permute-start | bytes 4915208 | tf_op jit(solution)/shard_map/ppermute | solution.py:33
  779.2 309.0 %reduce-scatter.16.cloned.1.call-start = ((), (), s32[]{:S(2)}) async-start(), calls=%async_computation.14 | async-start | bytes 8519680 | tf_op jit(solution)/shard_map/reduce_scatter | solution.py:124
  782.3 34.3 %collective-permute-start.17 = (bf16[800,1376]{1,0:T(8,128)(2,1)S(1)}, bf16[800,1376]{1,0:T(8,128)(2,1)S(1)}, u32[]{:S(2)}, u32[]{:S(2)}) collective-permute-start(bf16[800,1376]{1,0:T(8,128)(2,1)S(1)} %add_convert_fusion.5), channel_id=1, source_target_pairs={{8,16},{16,8},{9,17},{17,9},{10,18},{18,10},{11,19},{19,11},{12,20... | collective-permute-start | bytes 6604808 | tf_op jit(solution)/shard_map/ppermute | solution.py:69
  783.1 54.3 %collective-permute-start.18 = (bf16[800,1376]{1,0:T(8,128)(2,1)S(1)}, bf16[800,1376]{1,0:T(8,128)(2,1)S(1)}, u32[]{:S(2)}, u32[]{:S(2)}) collective-permute-start(bf16[800,1376]{1,0:T(8,128)(2,1)S(1)} %copy-done.33), channel_id=1, source_target_pairs={{0,8},{24,16},{1,9},{25,17},{2,10},{26,18},{3,11},{27,19},{4,12},{... | collective-permute-start | bytes 6604808 | tf_op jit(solution)/shard_map/ppermute | solution.py:69
  791.0 5.8 collective-permute-start.15
  792.4 13.7 %collective-permute-start.12 = (f32[16,3200]{1,0:T(8,128)S(1)}, f32[16,3200]{1,0:T(8,128)S(1)}, u32[]{:S(2)}, u32[]{:S(2)}) collective-permute-start(f32[16,3200]{1,0:T(8,128)S(1)} %copy-done.74), channel_id=1, source_target_pairs={{1,0},{2,1},{3,2},{5,4},{6,5},{7,6},{9,8},{10,9},{11,10},{13,12},{... | collective-permute-start | bytes 614408 | tf_op jit(solution)/shard_map/ppermute | solution.py:29
  794.8 13.8 %collective-permute-start.14 = (f32[16,3200]{1,0:T(8,128)S(1)}, f32[16,3200]{1,0:T(8,128)S(1)}, u32[]{:S(2)}, u32[]{:S(2)}) collective-permute-start(f32[16,3200]{1,0:T(8,128)S(1)} %copy-done.74), channel_id=1, source_target_pairs={{2,0},{3,1},{6,4},{7,5},{10,8},{11,9},{14,12},{15,13},{18,16},{19,... | collective-permute-start | bytes 614408 | tf_op jit(solution)/shard_map/ppermute | solution.py:29
  796.9 19.6 %collective-permute-start.16 = (f32[16,3200]{1,0:T(8,128)S(1)}, f32[16,3200]{1,0:T(8,128)S(1)}, u32[]{:S(2)}, u32[]{:S(2)}) collective-permute-start(f32[16,3200]{1,0:T(8,128)S(1)} %copy-done.74), channel_id=1, source_target_pairs={{3,0},{7,4},{11,8},{15,12},{19,16},{23,20},{27,24},{31,28}} | collective-permute-start | bytes 614408 | tf_op jit(solution)/shard_map/ppermute | solution.py:29
  839.4 60.0 %collective-permute-start.22 = (bf16[800,1376]{1,0:T(8,128)(2,1)}, bf16[800,1376]{1,0:T(8,128)(2,1)}, u32[]{:S(2)}, u32[]{:S(2)}) collective-permute-start(bf16[800,1376]{1,0:T(8,128)(2,1)} %add_convert_fusion.3), channel_id=1, source_target_pairs={{8,16},{16,8},{9,17},{17,9},{10,18},{18,10},{11,19},{19,11},{12,20... | collective-permute-start | bytes 6604808 | tf_op jit(solution)/shard_map/ppermute | solution.py:69
  843.4 55.9 %collective-permute-start.21 = (bf16[800,1376]{1,0:T(8,128)(2,1)}, bf16[800,1376]{1,0:T(8,128)(2,1)}, u32[]{:S(2)}, u32[]{:S(2)}) collective-permute-start(bf16[800,1376]{1,0:T(8,128)(2,1)} %add_convert_fusion.4), channel_id=1, source_target_pairs={{8,0},{16,24},{9,1},{17,25},{10,2},{18,26},{11,3},{19,27},{12,4},{... | collective-permute-start | bytes 6604808 | tf_op jit(solution)/shard_map/ppermute | solution.py:69
  844.7 54.6 %collective-permute-start.23 = (bf16[800,1376]{1,0:T(8,128)(2,1)}, bf16[800,1376]{1,0:T(8,128)(2,1)}, u32[]{:S(2)}, u32[]{:S(2)}) collective-permute-start(bf16[800,1376]{1,0:T(8,128)(2,1)} %add_convert_fusion.6), channel_id=1, source_target_pairs={{0,8},{24,16},{1,9},{25,17},{2,10},{26,18},{3,11},{27,19},{4,12},{... | collective-permute-start | bytes 6604808 | tf_op jit(solution)/shard_map/ppermute | solution.py:69
  907.6 5.3 collective-permute-start.24
  927.5 224.6 %reduce-scatter.26.cloned.1.call-start = ((), (), s32[]{:S(2)}) async-start(), calls=%async_computation.19 | async-start | bytes 6656000
  933.5 78.7 %collective-permute-start.48 = (bf16[800,1376]{1,0:T(8,128)(2,1)}, bf16[800,1376]{1,0:T(8,128)(2,1)}, u32[]{:S(2)}, u32[]{:S(2)}) collective-permute-start(bf16[800,1376]{1,0:T(8,128)(2,1)} %broadcast_select_fusion.2), channel_id=1, source_target_pairs={{0,4},{4,0},{1,5},{5,1},{2,6},{6,2},{3,7},{7,3},{8,12},{12,8},{9,1... | collective-permute-start | bytes 6604808 | tf_op jit(solution)/shard_map/ppermute | solution.py:33
  938.2 79.1 %collective-permute-start.26 = (bf16[800,1376]{1,0:T(8,128)(2,1)}, bf16[800,1376]{1,0:T(8,128)(2,1)}, u32[]{:S(2)}, u32[]{:S(2)}) collective-permute-start(bf16[800,1376]{1,0:T(8,128)(2,1)} %add_convert_fusion.1), channel_id=1, source_target_pairs={{8,16},{16,8},{9,17},{17,9},{10,18},{18,10},{11,19},{19,11},{12,20... | collective-permute-start | bytes 6604808 | tf_op jit(solution)/shard_map/ppermute | solution.py:69
  940.3 246.2 %reduce-scatter.20.cloned.1.call-start = ((), (), s32[]{:S(2)}) async-start(), calls=%async_computation.16 | async-start | bytes 5120000 | tf_op jit(solution)/shard_map/reduce_scatter | solution.py:124
  945.0 72.3 %collective-permute-start.25 = (bf16[800,1376]{1,0:T(8,128)(2,1)}, bf16[800,1376]{1,0:T(8,128)(2,1)}, u32[]{:S(2)}, u32[]{:S(2)}) collective-permute-start(bf16[800,1376]{1,0:T(8,128)(2,1)} %add_convert_fusion.2), channel_id=1, source_target_pairs={{8,0},{16,24},{9,1},{17,25},{10,2},{18,26},{11,3},{19,27},{12,4},{... | collective-permute-start | bytes 6604808 | tf_op jit(solution)/shard_map/ppermute | solution.py:69
  950.6 66.7 %collective-permute-start.29 = (bf16[800,800]{1,0:T(8,128)(2,1)}, bf16[800,800]{1,0:T(8,128)(2,1)}, u32[]{:S(2)}, u32[]{:S(2)}) collective-permute-start(bf16[800,800]{1,0:T(8,128)(2,1)} %reduce-scatter.18.cloned.1.call-done), channel_id=1, source_target_pairs={{0,8},{24,16},{1,9},{25,17},{2,10},{26,18},{3,11},{27,19},{4,12},{... | collective-permute-start | bytes 3840008 | tf_op jit(solution)/shard_map/ppermute | solution.py:69
  959.8 56.7 %collective-permute-start.30 = (bf16[400,800]{1,0:T(8,128)(2,1)S(1)}, bf16[400,800]{1,0:T(8,128)(2,1)S(1)}, u32[]{:S(2)}, u32[]{:S(2)}) collective-permute-start(bf16[400,800]{1,0:T(8,128)(2,1)S(1)} %copy-done.64), channel_id=1, source_target_pairs={{0,8},{24,16},{1,9},{25,17},{2,10},{26,18},{3,11},{27,19},{4,12},{... | collective-permute-start | bytes 1920008 | tf_op jit(solution)/shard_map/ppermute | solution.py:69
  1019.2 42.0 %collective-permute-start.49 = (bf16[800,1376]{1,0:T(8,128)(2,1)S(1)}, bf16[800,1376]{1,0:T(8,128)(2,1)S(1)}, u32[]{:S(2)}, u32[]{:S(2)}) collective-permute-start(bf16[800,1376]{1,0:T(8,128)(2,1)S(1)} %broadcast_select_fusion.1), channel_id=1, source_target_pairs={{0,4},{4,0},{1,5},{5,1},{2,6},{6,2},{3,7},{7,3},{8,12},{12,8},{9,1... | collective-permute-start | bytes 6604808 | tf_op jit(solution)/shard_map/ppermute | solution.py:33
  1023.4 64.8 %collective-permute-start.34 = (bf16[800,1376]{1,0:T(8,128)(2,1)S(1)}, bf16[800,1376]{1,0:T(8,128)(2,1)}, u32[]{:S(2)}, u32[]{:S(2)}) collective-permute-start(bf16[800,1376]{1,0:T(8,128)(2,1)S(1)} %add_convert_fusion), channel_id=1, source_target_pairs={{8,0},{16,24},{9,1},{17,25},{10,2},{18,26},{11,3},{19,27},{12,4},{... | collective-permute-start | bytes 6604808 | tf_op jit(solution)/shard_map/ppermute | solution.py:69
  1025.3 30.9 %collective-permute-start.32 = (bf16[512,640]{1,0:T(8,128)(2,1)S(1)}, bf16[512,640]{1,0:T(8,128)(2,1)S(1)}, u32[]{:S(2)}, u32[]{:S(2)}) collective-permute-start(bf16[512,640]{1,0:T(8,128)(2,1)S(1)} %get-tuple-element.318), channel_id=1, source_target_pairs={{1,0},{2,1},{3,2},{5,4},{6,5},{7,6},{9,8},{10,9},{11,10},{13,12},{... | collective-permute-start | bytes 1966088 | tf_op jit(solution)/shard_map/ppermute | solution.py:29
  1026.6 32.8 %collective-permute-start.33 = (bf16[512,640]{1,0:T(8,128)(2,1)S(1)}, bf16[512,640]{1,0:T(8,128)(2,1)S(1)}, u32[]{:S(2)}, u32[]{:S(2)}) collective-permute-start(bf16[512,640]{1,0:T(8,128)(2,1)S(1)} %get-tuple-element.319), channel_id=1, source_target_pairs={{2,0},{3,1},{6,4},{7,5},{10,8},{11,9},{14,12},{15,13},{18,16},{19,... | collective-permute-start | bytes 1966088 | tf_op jit(solution)/shard_map/ppermute | solution.py:29
  1034.1 29.7 %collective-permute-start.35 = (bf16[800,800]{1,0:T(8,128)(2,1)S(1)}, bf16[800,800]{1,0:T(8,128)(2,1)S(1)}, u32[]{:S(2)}, u32[]{:S(2)}) collective-permute-start(bf16[800,800]{1,0:T(8,128)(2,1)S(1)} %add_convert_fusion.11), channel_id=1, source_target_pairs={{8,16},{16,8},{9,17},{17,9},{10,18},{18,10},{11,19},{19,11},{12,20... | collective-permute-start | bytes 3840008 | tf_op jit(solution)/shard_map/ppermute | solution.py:69
  1056.2 30.9 %collective-permute-start.37 = (bf16[400,1600]{1,0:T(8,128)(2,1)S(1)}, bf16[400,1600]{1,0:T(8,128)(2,1)S(1)}, u32[]{:S(2)}, u32[]{:S(2)}) collective-permute-start(bf16[400,1600]{1,0:T(8,128)(2,1)S(1)} %copy-done.60), channel_id=1, source_target_pairs={{0,8},{24,16},{1,9},{25,17},{2,10},{26,18},{3,11},{27,19},{4,12},{... | collective-permute-start | bytes 3840008 | tf_op jit(solution)/shard_map/ppermute | solution.py:69
  1094.1 14.0 %collective-permute-start.42 = (bf16[512,1280]{1,0:T(8,128)(2,1)S(1)}, bf16[512,1280]{1,0:T(8,128)(2,1)S(1)}, u32[]{:S(2)}, u32[]{:S(2)}) collective-permute-start(bf16[512,1280]{1,0:T(8,128)(2,1)S(1)} %get-tuple-element.301), channel_id=1, source_target_pairs={{0,4},{4,0},{1,5},{5,1},{2,6},{6,2},{3,7},{7,3},{8,12},{12,8},{9,1... | collective-permute-start | bytes 3932168 | tf_op jit(solution)/shard_map/ppermute | solution.py:33
  1101.2 50.9 %collective-permute-start.40 = (bf16[400,1600]{1,0:T(8,128)(2,1)}, bf16[400,1600]{1,0:T(8,128)(2,1)}, u32[]{:S(2)}, u32[]{:S(2)}) collective-permute-start(bf16[400,1600]{1,0:T(8,128)(2,1)} %add_convert_fusion.13), channel_id=1, source_target_pairs={{8,16},{16,8},{9,17},{17,9},{10,18},{18,10},{11,19},{19,11},{12,20... | collective-permute-start | bytes 3840008 | tf_op jit(solution)/shard_map/ppermute | solution.py:69
  1104.1 48.0 %collective-permute-start.39 = (bf16[400,800]{1,0:T(8,128)(2,1)}, bf16[400,800]{1,0:T(8,128)(2,1)}, u32[]{:S(2)}, u32[]{:S(2)}) collective-permute-start(bf16[400,800]{1,0:T(8,128)(2,1)} %add_convert_fusion.14), channel_id=1, source_target_pairs={{8,0},{16,24},{9,1},{17,25},{10,2},{18,26},{11,3},{19,27},{12,4},{... | collective-permute-start | bytes 1920008 | tf_op jit(solution)/shard_map/ppermute | solution.py:69
  1106.9 48.6 %collective-permute-start.38 = (bf16[800,800]{1,0:T(8,128)(2,1)}, bf16[800,800]{1,0:T(8,128)(2,1)}, u32[]{:S(2)}, u32[]{:S(2)}) collective-permute-start(bf16[800,800]{1,0:T(8,128)(2,1)} %add_convert_fusion.10), channel_id=1, source_target_pairs={{8,0},{16,24},{9,1},{17,25},{10,2},{18,26},{11,3},{19,27},{12,4},{... | collective-permute-start | bytes 3840008 | tf_op jit(solution)/shard_map/ppermute | solution.py:69
  1115.2 174.4 %all-reduce.12.cloned.1.call-start = ((), (), s32[]{:S(2)}) async-start(), calls=%async_computation.20 | async-start | bytes 4710400 | tf_op jit(solution)/shard_map/psum | solution.py:682
  1120.2 66.4 %collective-permute-start.50 = (bf16[800,1376]{1,0:T(8,128)(2,1)}, bf16[800,1376]{1,0:T(8,128)(2,1)}, u32[]{:S(2)}, u32[]{:S(2)}) collective-permute-start(bf16[800,1376]{1,0:T(8,128)(2,1)} %broadcast_select_fusion), channel_id=1, source_target_pairs={{0,4},{4,0},{1,5},{5,1},{2,6},{6,2},{3,7},{7,3},{8,12},{12,8},{9,1... | collective-permute-start | bytes 6604808 | tf_op jit(solution)/shard_map/ppermute | solution.py:33
  1158.5 11.5 collective-permute-start.51
  1161.9 22.6 %collective-permute-start.47 = (bf16[400,800]{1,0:T(8,128)(2,1)S(1)}, bf16[400,800]{1,0:T(8,128)(2,1)S(1)}, u32[]{:S(2)}, u32[]{:S(2)}) collective-permute-start(bf16[400,800]{1,0:T(8,128)(2,1)S(1)} %broadcast_select_fusion.29), channel_id=1, source_target_pairs={{0,4},{4,0},{1,5},{5,1},{2,6},{6,2},{3,7},{7,3},{8,12},{12,8},{9,1... | collective-permute-start | bytes 1920008 | tf_op jit(solution)/shard_map/ppermute | solution.py:33
  1164.8 63.0 %collective-permute-start.46 = (bf16[800,800]{1,0:T(8,128)(2,1)}, bf16[800,800]{1,0:T(8,128)(2,1)}, u32[]{:S(2)}, u32[]{:S(2)}) collective-permute-start(bf16[800,800]{1,0:T(8,128)(2,1)} %broadcast_select_fusion.13), channel_id=1, source_target_pairs={{0,4},{4,0},{1,5},{5,1},{2,6},{6,2},{3,7},{7,3},{8,12},{12,8},{9,1... | collective-permute-start | bytes 3840008 | tf_op jit(solution)/shard_map/ppermute | solution.py:33
  1168.5 51.1 %collective-permute-start.41 = (bf16[400,1600]{1,0:T(8,128)(2,1)}, bf16[400,1600]{1,0:T(8,128)(2,1)}, u32[]{:S(2)}, u32[]{:S(2)}) collective-permute-start(bf16[400,1600]{1,0:T(8,128)(2,1)} %add_convert_fusion.12), channel_id=1, source_target_pairs={{8,0},{16,24},{9,1},{17,25},{10,2},{18,26},{11,3},{19,27},{12,4},{... | collective-permute-start | bytes 3840008 | tf_op jit(solution)/shard_map/ppermute | solution.py:69
  1174.9 9.6 collective-permute-start.53
  1222.1 76.7 %collective-permute-start.45 = (bf16[400,1600]{1,0:T(8,128)(2,1)}, bf16[400,1600]{1,0:T(8,128)(2,1)}, u32[]{:S(2)}, u32[]{:S(2)}) collective-permute-start(bf16[400,1600]{1,0:T(8,128)(2,1)} %broadcast_select_fusion.16), channel_id=1, source_target_pairs={{0,4},{4,0},{1,5},{5,1},{2,6},{6,2},{3,7},{7,3},{8,12},{12,8},{9,1... | collective-permute-start | bytes 3840008 | tf_op jit(solution)/shard_map/ppermute | solution.py:33
  1289.6 14.5 %collective-permute-start.43 = (bf16[400,1280]{1,0:T(8,128)(2,1)}, bf16[400,1280]{1,0:T(8,128)(2,1)}, u32[]{:S(2)}, u32[]{:S(2)}) collective-permute-start(bf16[400,1280]{1,0:T(8,128)(2,1)} %get-tuple-element.280), channel_id=1, source_target_pairs={{0,4},{4,0},{1,5},{5,1},{2,6},{6,2},{3,7},{7,3},{8,12},{12,8},{9,1... | collective-permute-start | bytes 3072008 | tf_op jit(solution)/shard_map/ppermute | solution.py:33
  1290.3 7.3 collective-permute-start.54
  1297.6 5.3 collective-permute-start.55
  1302.3 12.4 collective-permute-start.44
  (117 other events, 1527.7 us)
Sparse Core Ops, SparseCore 0:
  15.7 52.5 all-gather.6
  79.7 128.3 all-gather.8
  210.6 68.8 all-gather.10
  281.7 45.6 all-gather.12
  347.1 78.0 all-gather.14
  426.9 72.1 all-gather.16
  564.5 74.5 reduce-scatter.13
  662.0 41.9 reduce-scatter.21
  707.9 65.5 reduce-scatter.17
  779.3 72.6 reduce-scatter.23
  927.6 73.3 reduce-scatter.15
  1004.7 88.7 reduce-scatter.25
  1115.3 57.1 reduce-scatter.19
  1186.7 102.8 all-reduce.11

commit v4 on v3

--- a/solution.py
+++ b/solution.py
@@ -638,8 +638,8 @@
     mamba_sum, mixer_sum, switch_sum = ChipSum(mamba_half), ChipSum(mixer_half), ChipSum(switch_half)
     signal_part = left_product(normed_both, both_cores(d_signal, core)).astype(jnp.bfloat16)
     signal_half = scattered(signal_part)
-    d_attended = after(d_attended, signal_part)
-    output_half = scattered(after(output_part, signal_part))
+    output_half = scattered(after(output_part, d_mixed))
+    d_attended = after(d_attended, signal_part, output_half)
     head_stats = stats.reshape(PAIRS, 2, 2, count).transpose(1, 3, 0, 2).reshape(2, count, MAMBA_HEADS)
     head_totals = jnp.sum(sums.reshape(PAIRS, 2, 2, MAMBA_DIM), axis=3).transpose(1, 0, 2).reshape(2, MAMBA_HEADS)
     d_cumul = head_stats[0].at[-1].add(head_totals[1] + head_totals[0] * carry)
@@ -656,7 +656,7 @@
     for distance in range(1, blocks + 1):
         away = d_window[(blocks - distance) * count : (blocks - distance + 1) * count]
         own_grads = own_grads + moved(away.astype(jnp.bfloat16), "shard", -distance).astype(jnp.float32)
-    own_grads = advance((own_grads, output_half), [down_sum, mamba_sum, mixer_sum, switch_sum])[0]
+    own_grads = advance(own_grads, [down_sum, mamba_sum, mixer_sum, switch_sum])
     d_small = jnp.pad(jnp.concatenate([d_writer, d_reader, d_step_raw], 1), ((0, 0), (0, 128 - lead)))
     d_pair = own_grads.astype(jnp.bfloat16)
     d_last = jnp.concatenate([d_query, d_pair, d_small], 1)

time: 1350 us -> 1350 us (level)
    ppermute x18, waiting for transfers between devices: 103 us -> 126 us  [send(): return lax.ppermute(self.part, 'zz', self.routes[self.step])]
    psum x1, waiting for transfers between devices: 58.2 us -> 42.1 us  [body(): signal_sum, last_sum = lax.psum((signal_half, last_half), 'zz')]
    unnamed x233 -> x191, local copies, waits for them, and re-layouts: 40.1 us -> 34.2 us
  transfers between devices with their start and end apart: 70 -> 70, of which waited for: 23 -> 25; matrix products, arithmetic and copies ran while one was open for 35% -> 36% of each run, Pallas kernels for 13% -> 13%
where the time goes in v4:
time: 1350 us; the launch traced here: 1340 us
  waiting for transfers between devices  433 us (32%)
  matrix products  314 us (23%)
  other arithmetic  178 us (13%)
  Pallas kernels  178 us (13%)
  local copies, waits for them, and re-layouts  123 us (9%)
  starting transfers between devices  94.9 us (7%)
  between operations  16.5 us (1%)
    ppermute x18, waiting for transfers between devices, send(): return lax.ppermute(self.part, 'zz', self.routes[self.step])  126 us
    dot_general x8, matrix products, right_product(): lax.dot_general(left, right, (((1,), (1,)), ((), ())), preferred_element_...  114 us
    dot_general x8, matrix products, project(): return jnp.dot(left, right, preferred_element_type=jnp.float32)  106 us
    dot_general x9, matrix products, left_product(): lax.dot_general(left, right, (((0,), (0,)), ((), ())), preferred_element_...  93.6 us
    all_gather x4, waiting for transfers between devices, gathered(): return lax.all_gather(half, ('shard', 'core'), axis=0, tiled=True)  80.7 us
    all_gather x1, waiting for transfers between devices, body(): feed_all = lax.all_gather(feed_in, 'shard', axis=0, tiled=True)  77.6 us
    ppermute x14, waiting for transfers between devices, moved(): return lax.ppermute(block, axis, route)  75.7 us
    pallas_call x1, Pallas kernels, attend_back(): pl.pallas_call(attend_back_kernel, grid=(count // rows,), in_specs=[pl.Bl...  51 us
  transfers between devices with their start and end apart: 70, of which 25 were waited for; matrix products, arithmetic and copies ran while one was open for 36% of the time, Pallas kernels for 13%

profile of v4, /device:TPU:1, one launch (start us, length us, event | category | flops | bytes accessed | tf_op | source)
XLA Modules:
  0.0 1338.0 jit_solution(8999124512474374410)
XLA Ops:
  24.4 5.6 fusion.12
  30.1 38.2 %all-gather.7.cloned.1.call-done = bf16[1600,2304]{1,0:T(8,128)(2,1)} async-done(((bf16[200,2304]{1,0:T(8,128)(2,1)}), bf16[1600,2304]{1,0:T(8,128)(2,1)}) %all-gather.7.cloned.1.call-update) | async-done | bytes 7372816 | tf_op jit(solution)/shard_map/all_gather | solution.py:102
  68.3 9.6 convolution_convert_fusion.8
  92.3 29.7 %collective-permute-done = bf16[512,640]{1,0:T(8,128)(2,1)} collective-permute-done((bf16[512,640]{1,0:T(8,128)(2,1)S(1)}, bf16[512,640]{1,0:T(8,128)(2,1)}, u32[]{:S(2)}, u32[]{:S(2)}) %collective-permute-start) | collective-permute-done | bytes 655392 | tf_op jit(solution)/shard_map/ppermute | solution.py:29
  124.7 49.7 %attend.1 = (f32[512,1600]{1,0:T(8,128)}, f32[25,1,512]{2,1,0:T(1,128)}) custom-call(s32[1,512]{1,0:T(1,128)} %bitcast.87, bf16[512,1600]{1,0:T(8,128)(2,1)} %slice.195.query_ref, bf16[1536,640]{1,0:T(8,128)(2,1)} %pad_maximum_fusion.1.pair_ref), custom_call_target="tpu_custom_call" | custom-call | tf_op jit(solution)/shard_map/attend/pallas_call | solution.py:215
  174.3 33.8 %all-gather.9.cloned.1.call-done = bf16[1600,6528]{1,0:T(8,128)(2,1)} async-done(((bf16[200,6528]{1,0:T(8,128)(2,1)}), bf16[1600,6528]{1,0:T(8,128)(2,1)}) %all-gather.9.cloned.1.call-update) | async-done | bytes 20889616 | tf_op jit(solution)/shard_map/all_gather | solution.py:102
  211.4 21.0 %fusion.95 = (bf16[512,6528]{1,0:T(8,128)(2,1)}, f32[512,6528]{1,0:T(8,128)}) fusion(bf16[512,1600]{1,0:T(8,128)(2,1)} %fusion.22, bf16[1600,6528]{1,0:T(8,128)(2,1)} %all-gather.9.cloned.1.call-done), kind=kOutput, calls=%fused_computation.238 | convolution fusion | flops 10698817536 | bytes 42582016 | tf_op jit(solution)/shard_map/dot_general | solution.py:128
  239.7 9.3 make_drive.1
  258.4 12.2 collective-permute-done.3
  270.8 8.6 all-gather.11.cloned.1.call-done
  286.5 20.5 %mix.1.mixed_ref = f32[512,3200]{1,0:T(8,128)S(1)} custom-call(bf16[512,3200]{1,0:T(8,128)(2,1)S(1)} %copy-done.3, f32[25,2,512]{2,1,0:T(2,128)S(1)} %reduce_window_sum.33.cumul_ref, f32[25,2,512]{2,1,0:T(2,128)S(1)} %get-tuple-element.332.enter_ref, f32[512,512]{1,0:T(8,128)S(1)} %fusion.84.gram_ref, f32[512,512]{1,0:T(8,128)S(1)} %get-tuple-element.339.bias_ref, ...), custom_call_target="tpu_custom_call" | custom-call | tf_op jit(solution)/shard_map/mix/pallas_call | solution.py:412
  314.1 12.7 multiply_reduce_fusion.8
  326.8 4.7 copy.205
  331.5 5.1 multiply_convert_fusion.9
  336.6 7.1 multiply_reduce_fusion.6
  347.7 77.6 %all-gather.15.cloned.1.call-done = bf16[2048,1600]{1,0:T(8,128)(2,1)} async-done(((bf16[512,1600]{1,0:T(8,128)(2,1)}), bf16[2048,1600]{1,0:T(8,128)(2,1)}) %all-gather.15.cloned.1.call-update) | async-done | bytes 6553616 | tf_op jit(solution)/shard_map/all_gather | solution.py:593
  425.3 16.6 %fusion.96 = f32[2048,1376]{0,1:T(8,128)} fusion(bf16[2048,1600]{1,0:T(8,128)(2,1)} %all-gather.15.cloned.1.call-done, bf16[1600,1376]{1,0:T(8,128)(2,1)} %param.32), kind=kOutput, calls=%fused_computation.239 | convolution fusion | flops 9017753600 | bytes 22228992 | tf_op jit(solution)/shard_map/dot_general | solution.py:128
  441.9 20.5 %multiply_convert_fusion.2 = (bf16[2048,1376]{0,1:T(8,128)(2,1)}, f32[2048,1376]{0,1:T(8,128)}) fusion(f32[2048,1376]{0,1:T(8,128)} %fusion.96, bf16[2048,1600]{1,0:T(8,128)(2,1)} %all-gather.15.cloned.1.call-done, bf16[1600,1376]{1,0:T(8,128)(2,1)} %param.33), kind=kOutput, calls=%fused_computation.2 | convolution fusion | flops 9034661888 | bytes 39137280 | tf_op jit(solution)/shard_map/dot_general | solution.py:128
  462.4 17.0 %convolution_convert_fusion.4 = bf16[2048,1600]{1,0:T(8,128)(2,1)} fusion(bf16[2048,1376]{0,1:T(8,128)(2,1)} %get-tuple-element.346, bf16[1376,1600]{0,1:T(8,128)(2,1)} %param.34), kind=kOutput, calls=%fused_computation.13 | convolution fusion | flops 9021030400 | bytes 16592896 | tf_op jit(solution)/shard_map/dot_general | solution.py:128
  479.3 19.9 %all-gather.17.cloned.1.call-done = bf16[2048,1600]{0,1:T(8,128)(2,1)} async-done(((bf16[512,1600]{0,1:T(8,128)(2,1)}), bf16[2048,1600]{0,1:T(8,128)(2,1)}) %all-gather.17.cloned.1.call-update) | async-done | bytes 6553616 | tf_op jit(solution)/shard_map/all_gather | solution.py:594
  499.2 25.8 %multiply_convert_fusion = (bf16[2048,1376]{0,1:T(8,128)(2,1)}, bf16[2048,1376]{0,1:T(8,128)(2,1)}) fusion(f32[2048,1376]{0,1:T(8,128)} %fusion.96, f32[2048,1376]{0,1:T(8,128)} %get-tuple-element.347, bf16[2048,1600]{0,1:T(8,128)(2,1)} %all-gather.17.cloned.1.call-done, bf16[1376,1600]{0,1:T(8,128)(2,1)} %param.34), kind=kOutput, calls=%fused_computation | convolution fusion | flops 9054388224 | bytes 44773376 | tf_op jit(solution)/shard_map/dot_general | solution.py:138
  525.0 14.0 %fusion.97 = f32[2048,1600]{0,1:T(8,128)S(1)} fusion(bf16[1600,1376]{1,0:T(8,128)(2,1)} %param.32, bf16[2048,1376]{0,1:T(8,128)(2,1)} %get-tuple-element.283), kind=kOutput, calls=%fused_computation.240 | convolution fusion | flops 9017753600 | bytes 23146496 | tf_op jit(solution)/shard_map/dot_general | solution.py:138
  539.0 16.0 %convolution_add_fusion = bf16[2048,1600]{0,1:T(8,128)(2,1)} fusion(f32[2048,1600]{0,1:T(8,128)S(1)} %fusion.97, bf16[1600,1376]{1,0:T(8,128)(2,1)} %param.33, bf16[2048,1376]{0,1:T(8,128)(2,1)} %get-tuple-element.282), kind=kOutput, calls=%fused_computation.8 | convolution fusion | flops 9024307200 | bytes 29700096 | tf_op jit(solution)/shard_map/dot_general | solution.py:138
  555.0 9.5 copy.209
  564.5 14.3 %convolution_convert_fusion.3 = bf16[1600,1376]{1,0:T(8,128)(2,1)S(1)} fusion(bf16[2048,1600]{0,1:T(8,128)(2,1)} %all-gather.17.cloned.1.call-done, bf16[2048,1376]{0,1:T(8,128)(2,1)} %get-tuple-element.346), kind=kOutput, calls=%fused_computation.12 | convolution fusion | flops 9019955200 | bytes 16592896 | tf_op jit(solution)/shard_map/dot_general | solution.py:132
  581.1 17.4 %convolution_convert_fusion.5 = bf16[1600,1376]{1,0:T(8,128)(2,1)S(1)} fusion(bf16[2048,1600]{1,0:T(8,128)(2,1)} %all-gather.15.cloned.1.call-done, bf16[2048,1376]{0,1:T(8,128)(2,1)} %get-tuple-element.282), kind=kOutput, calls=%fused_computation.14 | convolution fusion | flops 9019955200 | bytes 16592896 | tf_op jit(solution)/shard_map/dot_general | solution.py:132
  600.8 11.9 convolution_convert_fusion.6
  623.4 4.6 add_convert_fusion.6
  654.6 7.4 convolution_convert_fusion.9
  662.3 9.9 multiply_reduce_fusion.1
  682.0 11.4 convolution_convert_fusion.7
  693.5 4.5 collective-permute-start.10
  698.0 16.0 %multiply_convert_fusion.3 = (bf16[512,3200]{1,0:T(8,128)(2,1)}, bf16[512,3200]{1,0:T(8,128)(2,1)}) fusion(f32[512,3200]{1,0:T(8,128)} %copy-done.2, f32[512,6528]{1,0:T(8,128)} %get-tuple-element.341.signal_ref, bf16[512,1600]{1,0:T(8,128)(2,1)} %copy-done.30, bf16[3200,1600]{1,0:T(8,128)(2,1)} %all-gather.11.cloned.1.call-done), kind=kOutput, calls=%fused_computation.26 | convolution fusion | flops 5264179200 | bytes 31539200 | tf_op jit(solution)/shard_map/dot_general | solution.py:138
  714.0 31.0 %collective-permute-done.10 = bf16[800,1376]{1,0:T(8,128)(2,1)} collective-permute-done((bf16[800,1376]{1,0:T(8,128)(2,1)}, bf16[800,1376]{1,0:T(8,128)(2,1)}, u32[]{:S(2)}, u32[]{:S(2)}) %collective-permute-start.10) | collective-permute-done | bytes 2201632 | tf_op jit(solution)/shard_map/ppermute | solution.py:69
  750.7 6.2 leave_back.1
  756.9 4.4 broadcast_select_fusion.10
  772.4 11.7 convolution_convert_fusion.1
  788.5 6.2 collective-permute-start.17
  803.3 7.7 collective-permute-done.11
  813.5 8.0 collective-permute-done.15
  821.6 20.6 %collective-permute-done.17 = bf16[800,1376]{1,0:T(8,128)(2,1)S(1)} collective-permute-done((bf16[800,1376]{1,0:T(8,128)(2,1)S(1)}, bf16[800,1376]{1,0:T(8,128)(2,1)S(1)}, u32[]{:S(2)}, u32[]{:S(2)}) %collective-permute-start.17) | collective-permute-done | bytes 2201632 | tf_op jit(solution)/shard_map/ppermute | solution.py:69
  849.5 7.7 collective-permute-start.22
  860.7 41.8 %mix_back.1 = (bf16[512,3200]{1,0:T(8,128)(2,1)}, f32[512,512]{1,0:T(8,128)S(1)}, f32[512,16]{1,0:T(8,128)S(1)}, f32[512,16]{1,0:T(8,128)S(1)}, f32[25,4,512]{2,1,0:T(4,128)S(1)}, /*index=5*/f32[25,2,128]{2,1,0:T(2,128)S(1)}) custom-call(bf16[512,3200]{1,0:T(8,128)(2,1)} %get-tuple-element.111.d_mixed_ref, f32[512,3200]{1,0:T(8,128)} %copy-done.2, ...), custom_call_target="tpu_custom_call" | custom-call | tf_op jit(solution)/shard_map/mix_back/pallas_call | solution.py:495
  913.4 4.2 add_convert_fusion.1
  926.8 11.2 convolution_convert_fusion.2
  938.1 4.2 add_convert_fusion.2
  947.9 7.1 collective-permute-start.29
  964.1 51.0 %attend_back.1 = (bf16[512,1600]{1,0:T(8,128)(2,1)}, f32[1536,640]{1,0:T(8,128)}) custom-call(s32[1,512]{1,0:T(1,128)} %bitcast.88, bf16[512,1600]{1,0:T(8,128)(2,1)} %slice.195.query_ref, bf16[1536,640]{1,0:T(8,128)(2,1)} %pad_maximum_fusion.1.pair_ref, f32[512,1600]{1,0:T(8,128)} %get-tuple-element.102.out_ref, ...), custom_call_target="tpu_custom_call" | custom-call | tf_op jit(solution)/shard_map/attend_back/pallas_call | solution.py:300
  1021.4 4.2 maximum_convert_fusion
  1028.2 6.2 collective-permute-start.37
  1042.3 12.2 collective-permute-done.33
  1057.1 4.2 collective-permute-done.37
  1061.3 9.0 collective-permute-done.34
  1088.4 4.4 broadcast_select_fusion.6
  1092.9 7.0 convolution_convert_fusion
  1100.1 5.9 maximum_convert_fusion.1
  1106.0 9.5 fusion.43
  1115.5 21.7 %fusion.19 = f32[512,1600]{1,0:T(8,128)} fusion(f32[512,1600]{1,0:T(8,128)} %fusion.43, bf16[1600,6528]{1,0:T(8,128)(2,1)} %all-gather.9.cloned.1.call-done, bf16[512,128]{1,0:T(8,128)(2,1)S(1)} %fusion.71, bf16[512,3200]{1,0:T(8,128)(2,1)S(1)} %copy-done.42, bf16[512,3200]{1,0:T(8,128)(2,1)S(1)} %copy-done.43), kind=kOutput, calls=%fused_computation.55 | convolution fusion | flops 10716348416 | bytes 34127872 | tf_op jit(solution)/shard_map/dot_general | solution.py:138
  1163.4 7.2 fusion.27
  1174.2 60.7 %collective-permute-done.41 = bf16[400,1600]{1,0:T(8,128)(2,1)} collective-permute-done((bf16[400,1600]{1,0:T(8,128)(2,1)}, bf16[400,1600]{1,0:T(8,128)(2,1)}, u32[]{:S(2)}, u32[]{:S(2)}) %collective-permute-start.41) | collective-permute-done | bytes 1280032 | tf_op jit(solution)/shard_map/ppermute | solution.py:69
  1244.9 42.1 %all-reduce.12.cloned.1.call-done = (bf16[400,1280]{1,0:T(8,128)(2,1)}, bf16[400,1600]{1,0:T(8,128)(2,1)}) async-done(((bf16[400,1280]{1,0:T(8,128)(2,1)}, bf16[400,1600]{1,0:T(8,128)(2,1)}), (bf16[400,1280]{1,0:T(8,128)(2,1)}, bf16[400,1600]{1,0:T(8,128)(2,1)})) %all-reduce.12.cloned.1.call-update) | async-done | bytes 2304016 | tf_op jit(solution)/shard_map/psum | solution.py:682
  1287.7 5.0 maximum_convert_fusion.2
  1315.6 8.4 concatenate.101
  1324.0 7.3 concatenate.102
  (486 shorter events, 301.3 us)
Async XLA Ops:
  7.2 61.1 %all-gather.7.cloned.1.call-start = ((), (), s32[]{:S(2)}) async-start(), calls=%async_computation.7 | async-start | bytes 8294400 | tf_op jit(solution)/shard_map/all_gather | solution.py:102
  15.6 192.6 %all-gather.9.cloned.1.call-start = ((), (), s32[]{:S(2)}) async-start(), calls=%async_computation.8 | async-start | bytes 23500800 | tf_op jit(solution)/shard_map/all_gather | solution.py:102
  79.6 199.8 %all-gather.11.cloned.1.call-start = ((), (), s32[]{:S(2)}) async-start(), calls=%async_computation.9 | async-start | bytes 11980800 | tf_op jit(solution)/shard_map/all_gather | solution.py:102
  81.1 40.8 %collective-permute-start = (bf16[512,640]{1,0:T(8,128)(2,1)S(1)}, bf16[512,640]{1,0:T(8,128)(2,1)}, u32[]{:S(2)}, u32[]{:S(2)}) collective-permute-start(bf16[512,640]{1,0:T(8,128)(2,1)S(1)} %slice.196), channel_id=1, source_target_pairs={{0,2},{1,3},{4,6},{5,7},{8,10},{9,11},{12,14},{13,15},{16,18},{17,... | collective-permute-start | bytes 1966088 | tf_op jit(solution)/shard_map/ppermute | solution.py:29
  84.8 37.2 %collective-permute-start.1 = (bf16[512,640]{1,0:T(8,128)(2,1)S(1)}, bf16[512,640]{1,0:T(8,128)(2,1)}, u32[]{:S(2)}, u32[]{:S(2)}) collective-permute-start(bf16[512,640]{1,0:T(8,128)(2,1)S(1)} %slice.196), channel_id=1, source_target_pairs={{0,1},{1,2},{2,3},{4,5},{5,6},{6,7},{8,9},{9,10},{10,11},{12,13},{... | collective-permute-start | bytes 1966088 | tf_op jit(solution)/shard_map/ppermute | solution.py:29
  209.3 127.3 %all-gather.13.cloned.1.call-start = ((), (), s32[]{:S(2)}) async-start(), calls=%async_computation.10 | async-start | bytes 5990400 | tf_op jit(solution)/shard_map/all_gather | solution.py:102
  249.0 21.7 %collective-permute-start.2 = (f32[16,3200]{1,0:T(8,128)}, f32[16,3200]{1,0:T(8,128)S(1)}, u32[]{:S(2)}, u32[]{:S(2)}) collective-permute-start(f32[16,3200]{1,0:T(8,128)} %get-tuple-element.105), channel_id=1, source_target_pairs={{0,1},{1,2},{2,3},{4,5},{5,6},{6,7},{8,9},{9,10},{10,11},{12,13},{... | collective-permute-start | bytes 614408 | tf_op jit(solution)/shard_map/ppermute | solution.py:29
  252.1 18.6 %collective-permute-start.4 = (f32[16,3200]{1,0:T(8,128)}, f32[16,3200]{1,0:T(8,128)S(1)}, u32[]{:S(2)}, u32[]{:S(2)}) collective-permute-start(f32[16,3200]{1,0:T(8,128)} %get-tuple-element.105), channel_id=1, source_target_pairs={{0,2},{1,3},{4,6},{5,7},{8,10},{9,11},{12,14},{13,15},{16,18},{17,... | collective-permute-start | bytes 614408 | tf_op jit(solution)/shard_map/ppermute | solution.py:29
  254.4 16.4 %collective-permute-start.6 = (f32[16,3200]{1,0:T(8,128)}, f32[16,3200]{1,0:T(8,128)S(1)}, u32[]{:S(2)}, u32[]{:S(2)}) collective-permute-start(f32[16,3200]{1,0:T(8,128)} %get-tuple-element.105), channel_id=1, source_target_pairs={{0,3},{4,7},{8,11},{12,15},{16,19},{20,23},{24,27},{28,31}} | collective-permute-start | bytes 614408 | tf_op jit(solution)/shard_map/ppermute | solution.py:29
  255.8 14.8 %collective-permute-start.3 = (f32[1,3200]{1,0:T(1,128)S(1)}, f32[1,3200]{1,0:T(1,128)S(1)}, u32[]{:S(2)}, u32[]{:S(2)}) collective-permute-start(f32[1,3200]{1,0:T(1,128)S(1)} %broadcast_in_dim_reshape.3), channel_id=1, source_target_pairs={{0,1},{1,2},{2,3},{4,5},{5,6},{6,7},{8,9},{9,10},{10,11},{12,13},{... | collective-permute-start | bytes 38408 | tf_op jit(solution)/shard_map/ppermute | solution.py:29
  257.1 13.5 %collective-permute-start.5 = (f32[1,3200]{1,0:T(1,128)S(1)}, f32[1,3200]{1,0:T(1,128)S(1)}, u32[]{:S(2)}, u32[]{:S(2)}) collective-permute-start(f32[1,3200]{1,0:T(1,128)S(1)} %broadcast_in_dim_reshape.3), channel_id=1, source_target_pairs={{0,2},{1,3},{4,6},{5,7},{8,10},{9,11},{12,14},{13,15},{16,18},{17,... | collective-permute-start | bytes 38408 | tf_op jit(solution)/shard_map/ppermute | solution.py:29
  281.4 143.9 %all-gather.15.cloned.1.call-start = ((), (), s32[]{:S(2)}) async-start(), calls=%async_computation.11 | async-start | bytes 8519680 | tf_op jit(solution)/shard_map/all_gather | solution.py:593
  347.0 152.2 %all-gather.17.cloned.1.call-start = ((), (), s32[]{:S(2)}) async-start(), calls=%async_computation.12 | async-start | bytes 8192000 | tf_op jit(solution)/shard_map/all_gather | solution.py:594
  347.6 291.6 %reduce-scatter.14.cloned.1.call-start = ((), (), s32[]{:S(2)}) async-start(), calls=%async_computation.13 | async-start | bytes 8519680 | tf_op jit(solution)/shard_map/reduce_scatter | solution.py:124
  564.5 339.5 %reduce-scatter.22.cloned.1.call-start = ((), (), s32[]{:S(2)}) async-start(), calls=%async_computation.17 | async-start | bytes 3584000
  580.4 42.9 %collective-permute-start.9 = (bf16[800,1376]{1,0:T(8,128)(2,1)}, bf16[800,1376]{1,0:T(8,128)(2,1)}, u32[]{:S(2)}, u32[]{:S(2)}) collective-permute-start(bf16[800,1376]{1,0:T(8,128)(2,1)} %constant_dynamic-slice_fusion), channel_id=1, source_target_pairs={{0,4},{4,0},{1,5},{5,1},{2,6},{6,2},{3,7},{7,3},{8,12},{12,8},{9,1... | collective-permute-start | bytes 6604808 | tf_op jit(solution)/shard_map/ppermute | solution.py:33
  600.2 27.7 %collective-permute-start.8 = (bf16[800,1376]{1,0:T(8,128)(2,1)}, bf16[800,1376]{1,0:T(8,128)(2,1)}, u32[]{:S(2)}, u32[]{:S(2)}) collective-permute-start(bf16[800,1376]{1,0:T(8,128)(2,1)} %constant_dynamic-slice_fusion.1), channel_id=1, source_target_pairs={{0,4},{4,0},{1,5},{5,1},{2,6},{6,2},{3,7},{7,3},{8,12},{12,8},{9,1... | collective-permute-start | bytes 6604808 | tf_op jit(solution)/shard_map/ppermute | solution.py:33
  615.5 16.0 %collective-permute-start.7 = (bf16[800,1376]{1,0:T(8,128)(2,1)}, bf16[800,1376]{1,0:T(8,128)(2,1)}, u32[]{:S(2)}, u32[]{:S(2)}) collective-permute-start(bf16[800,1376]{1,0:T(8,128)(2,1)} %constant_dynamic-slice_fusion.2), channel_id=1, source_target_pairs={{0,4},{4,0},{1,5},{5,1},{2,6},{6,2},{3,7},{7,3},{8,12},{12,8},{9,1... | collective-permute-start | bytes 6604808 | tf_op jit(solution)/shard_map/ppermute | solution.py:33
  622.9 26.2 %collective-permute-start.18 = (bf16[512,1600]{0,1:T(8,128)(2,1)}, bf16[512,1600]{0,1:T(8,128)(2,1)}, u32[]{:S(2)}, u32[]{:S(2)}) collective-permute-start(bf16[512,1600]{0,1:T(8,128)(2,1)} %copy.213), channel_id=1, source_target_pairs={{0,4},{4,0},{1,5},{5,1},{2,6},{6,2},{3,7},{7,3},{8,12},{12,8},{9,1... | collective-permute-start | bytes 4915208 | tf_op jit(solution)/shard_map/ppermute | solution.py:33
  662.1 285.8 %reduce-scatter.18.cloned.1.call-start = ((), (), s32[]{:S(2)}) async-start(), calls=%async_computation.15 | async-start | bytes 7168000 | tf_op jit(solution)/shard_map/reduce_scatter | solution.py:124
  662.1 19.9 %collective-permute-start.27 = (bf16[512,3200]{1,0:T(8,128)(2,1)}, bf16[512,3200]{1,0:T(8,128)(2,1)}, u32[]{:S(2)}, u32[]{:S(2)}) collective-permute-start(bf16[512,3200]{1,0:T(8,128)(2,1)} %copy-done.44), channel_id=1, source_target_pairs={{0,4},{4,0},{1,5},{5,1},{2,6},{6,2},{3,7},{7,3},{8,12},{12,8},{9,1... | collective-permute-start | bytes 9830408 | tf_op jit(solution)/shard_map/ppermute | solution.py:33
  693.4 270.6 %reduce-scatter.16.cloned.1.call-start = ((), (), s32[]{:S(2)}) async-start(), calls=%async_computation.14 | async-start | bytes 8519680 | tf_op jit(solution)/shard_map/reduce_scatter | solution.py:124
  693.5 51.5 %collective-permute-start.10 = (bf16[800,1376]{1,0:T(8,128)(2,1)}, bf16[800,1376]{1,0:T(8,128)(2,1)}, u32[]{:S(2)}, u32[]{:S(2)}) collective-permute-start(bf16[800,1376]{1,0:T(8,128)(2,1)} %add_convert_fusion.8), channel_id=1, source_target_pairs={{0,8},{24,16},{1,9},{25,17},{2,10},{26,18},{3,11},{27,19},{4,12},{... | collective-permute-start | bytes 6604808 | tf_op jit(solution)/shard_map/ppermute | solution.py:69
  745.0 270.1 %reduce-scatter.24.cloned.1.call-start = ((), (), s32[]{:S(2)}) async-start(), calls=%async_computation.18 | async-start | bytes 6656000
  748.8 16.1 %collective-permute-start.23 = (bf16[512,1600]{0,1:T(8,128)(2,1)}, bf16[512,1600]{0,1:T(8,128)(2,1)}, u32[]{:S(2)}, u32[]{:S(2)}) collective-permute-start(bf16[512,1600]{0,1:T(8,128)(2,1)} %copy.225), channel_id=1, source_target_pairs={{0,4},{4,0},{1,5},{5,1},{2,6},{6,2},{3,7},{7,3},{8,12},{12,8},{9,1... | collective-permute-start | bytes 4915208 | tf_op jit(solution)/shard_map/ppermute | solution.py:33
  784.1 360.1 %reduce-scatter.26.cloned.1.call-start = ((), (), s32[]{:S(2)}) async-start(), calls=%async_computation.19 | async-start | bytes 6656000
  787.7 33.9 %collective-permute-start.16 = (bf16[800,1376]{1,0:T(8,128)(2,1)S(1)}, bf16[800,1376]{1,0:T(8,128)(2,1)S(1)}, u32[]{:S(2)}, u32[]{:S(2)}) collective-permute-start(bf16[800,1376]{1,0:T(8,128)(2,1)S(1)} %add_convert_fusion.5), channel_id=1, source_target_pairs={{8,16},{16,8},{9,17},{17,9},{10,18},{18,10},{11,19},{19,11},{12,20... | collective-permute-start | bytes 6604808 | tf_op jit(solution)/shard_map/ppermute | solution.py:69
  788.5 53.7 %collective-permute-start.17 = (bf16[800,1376]{1,0:T(8,128)(2,1)S(1)}, bf16[800,1376]{1,0:T(8,128)(2,1)S(1)}, u32[]{:S(2)}, u32[]{:S(2)}) collective-permute-start(bf16[800,1376]{1,0:T(8,128)(2,1)S(1)} %copy-done.26), channel_id=1, source_target_pairs={{0,8},{24,16},{1,9},{25,17},{2,10},{26,18},{3,11},{27,19},{4,12},{... | collective-permute-start | bytes 6604808 | tf_op jit(solution)/shard_map/ppermute | solution.py:69
  796.0 5.9 collective-permute-start.14
  797.3 13.6 %collective-permute-start.11 = (f32[16,3200]{1,0:T(8,128)S(1)}, f32[16,3200]{1,0:T(8,128)S(1)}, u32[]{:S(2)}, u32[]{:S(2)}) collective-permute-start(f32[16,3200]{1,0:T(8,128)S(1)} %copy-done.53), channel_id=1, source_target_pairs={{1,0},{2,1},{3,2},{5,4},{6,5},{7,6},{9,8},{10,9},{11,10},{13,12},{... | collective-permute-start | bytes 614408 | tf_op jit(solution)/shard_map/ppermute | solution.py:29
  799.8 13.7 %collective-permute-start.13 = (f32[16,3200]{1,0:T(8,128)S(1)}, f32[16,3200]{1,0:T(8,128)S(1)}, u32[]{:S(2)}, u32[]{:S(2)}) collective-permute-start(f32[16,3200]{1,0:T(8,128)S(1)} %copy-done.53), channel_id=1, source_target_pairs={{2,0},{3,1},{6,4},{7,5},{10,8},{11,9},{14,12},{15,13},{18,16},{19,... | collective-permute-start | bytes 614408 | tf_op jit(solution)/shard_map/ppermute | solution.py:29
  801.9 19.6 %collective-permute-start.15 = (f32[16,3200]{1,0:T(8,128)S(1)}, f32[16,3200]{1,0:T(8,128)S(1)}, u32[]{:S(2)}, u32[]{:S(2)}) collective-permute-start(f32[16,3200]{1,0:T(8,128)S(1)} %copy-done.53), channel_id=1, source_target_pairs={{3,0},{7,4},{11,8},{15,12},{19,16},{23,20},{27,24},{31,28}} | collective-permute-start | bytes 614408 | tf_op jit(solution)/shard_map/ppermute | solution.py:29
  844.2 59.8 %collective-permute-start.21 = (bf16[800,1376]{1,0:T(8,128)(2,1)}, bf16[800,1376]{1,0:T(8,128)(2,1)}, u32[]{:S(2)}, u32[]{:S(2)}) collective-permute-start(bf16[800,1376]{1,0:T(8,128)(2,1)} %add_convert_fusion.3), channel_id=1, source_target_pairs={{8,16},{16,8},{9,17},{17,9},{10,18},{18,10},{11,19},{19,11},{12,20... | collective-permute-start | bytes 6604808 | tf_op jit(solution)/shard_map/ppermute | solution.py:69
  848.2 55.8 %collective-permute-start.20 = (bf16[800,1376]{1,0:T(8,128)(2,1)}, bf16[800,1376]{1,0:T(8,128)(2,1)}, u32[]{:S(2)}, u32[]{:S(2)}) collective-permute-start(bf16[800,1376]{1,0:T(8,128)(2,1)} %add_convert_fusion.4), channel_id=1, source_target_pairs={{8,0},{16,24},{9,1},{17,25},{10,2},{18,26},{11,3},{19,27},{12,4},{... | collective-permute-start | bytes 6604808 | tf_op jit(solution)/shard_map/ppermute | solution.py:69
  849.5 54.5 %collective-permute-start.22 = (bf16[800,1376]{1,0:T(8,128)(2,1)}, bf16[800,1376]{1,0:T(8,128)(2,1)}, u32[]{:S(2)}, u32[]{:S(2)}) collective-permute-start(bf16[800,1376]{1,0:T(8,128)(2,1)} %add_convert_fusion.6), channel_id=1, source_target_pairs={{0,8},{24,16},{1,9},{25,17},{2,10},{26,18},{3,11},{27,19},{4,12},{... | collective-permute-start | bytes 6604808 | tf_op jit(solution)/shard_map/ppermute | solution.py:69
  910.2 13.0 collective-permute-start.24
  917.7 97.4 %collective-permute-start.26 = (bf16[800,1376]{1,0:T(8,128)(2,1)}, bf16[800,1376]{1,0:T(8,128)(2,1)}, u32[]{:S(2)}, u32[]{:S(2)}) collective-permute-start(bf16[800,1376]{1,0:T(8,128)(2,1)} %add_convert_fusion.1), channel_id=1, source_target_pairs={{8,16},{16,8},{9,17},{17,9},{10,18},{18,10},{11,19},{19,11},{12,20... | collective-permute-start | bytes 6604808 | tf_op jit(solution)/shard_map/ppermute | solution.py:69
  923.2 36.8 %collective-permute-start.48 = (bf16[800,1376]{1,0:T(8,128)(2,1)}, bf16[800,1376]{1,0:T(8,128)(2,1)}, u32[]{:S(2)}, u32[]{:S(2)}) collective-permute-start(bf16[800,1376]{1,0:T(8,128)(2,1)} %broadcast_select_fusion.2), channel_id=1, source_target_pairs={{0,4},{4,0},{1,5},{5,1},{2,6},{6,2},{3,7},{7,3},{8,12},{12,8},{9,1... | collective-permute-start | bytes 6604808 | tf_op jit(solution)/shard_map/ppermute | solution.py:33
  938.1 225.3 %reduce-scatter.20.cloned.1.call-start = ((), (), s32[]{:S(2)}) async-start(), calls=%async_computation.16 | async-start | bytes 5120000 | tf_op jit(solution)/shard_map/reduce_scatter | solution.py:124
  942.3 72.7 %collective-permute-start.25 = (bf16[800,1376]{1,0:T(8,128)(2,1)}, bf16[800,1376]{1,0:T(8,128)(2,1)}, u32[]{:S(2)}, u32[]{:S(2)}) collective-permute-start(bf16[800,1376]{1,0:T(8,128)(2,1)} %add_convert_fusion.2), channel_id=1, source_target_pairs={{8,0},{16,24},{9,1},{17,25},{10,2},{18,26},{11,3},{19,27},{12,4},{... | collective-permute-start | bytes 6604808 | tf_op jit(solution)/shard_map/ppermute | solution.py:69
  947.9 67.2 %collective-permute-start.29 = (bf16[800,800]{1,0:T(8,128)(2,1)}, bf16[800,800]{1,0:T(8,128)(2,1)}, u32[]{:S(2)}, u32[]{:S(2)}) collective-permute-start(bf16[800,800]{1,0:T(8,128)(2,1)} %reduce-scatter.18.cloned.1.call-done), channel_id=1, source_target_pairs={{0,8},{24,16},{1,9},{25,17},{2,10},{26,18},{3,11},{27,19},{4,12},{... | collective-permute-start | bytes 3840008 | tf_op jit(solution)/shard_map/ppermute | solution.py:69
  957.8 57.2 %collective-permute-start.30 = (bf16[400,800]{1,0:T(8,128)(2,1)S(1)}, bf16[400,800]{1,0:T(8,128)(2,1)}, u32[]{:S(2)}, u32[]{:S(2)}) collective-permute-start(bf16[400,800]{1,0:T(8,128)(2,1)S(1)} %copy-done.50), channel_id=1, source_target_pairs={{0,8},{24,16},{1,9},{25,17},{2,10},{26,18},{3,11},{27,19},{4,12},{... | collective-permute-start | bytes 1920008 | tf_op jit(solution)/shard_map/ppermute | solution.py:69
  1018.1 52.2 %collective-permute-start.34 = (bf16[800,1376]{1,0:T(8,128)(2,1)S(1)}, bf16[800,1376]{1,0:T(8,128)(2,1)S(1)}, u32[]{:S(2)}, u32[]{:S(2)}) collective-permute-start(bf16[800,1376]{1,0:T(8,128)(2,1)S(1)} %add_convert_fusion), channel_id=1, source_target_pairs={{8,0},{16,24},{9,1},{17,25},{10,2},{18,26},{11,3},{19,27},{12,4},{... | collective-permute-start | bytes 6604808 | tf_op jit(solution)/shard_map/ppermute | solution.py:69
  1020.1 17.7 %collective-permute-start.32 = (bf16[512,640]{1,0:T(8,128)(2,1)S(1)}, bf16[512,640]{1,0:T(8,128)(2,1)S(1)}, u32[]{:S(2)}, u32[]{:S(2)}) collective-permute-start(bf16[512,640]{1,0:T(8,128)(2,1)S(1)} %get-tuple-element.318), channel_id=1, source_target_pairs={{1,0},{2,1},{3,2},{5,4},{6,5},{7,6},{9,8},{10,9},{11,10},{13,12},{... | collective-permute-start | bytes 1966088 | tf_op jit(solution)/shard_map/ppermute | solution.py:29
  1027.4 29.7 %collective-permute-start.35 = (bf16[800,800]{1,0:T(8,128)(2,1)S(1)}, bf16[800,800]{1,0:T(8,128)(2,1)S(1)}, u32[]{:S(2)}, u32[]{:S(2)}) collective-permute-start(bf16[800,800]{1,0:T(8,128)(2,1)S(1)} %add_convert_fusion.11), channel_id=1, source_target_pairs={{8,16},{16,8},{9,17},{17,9},{10,18},{18,10},{11,19},{19,11},{12,20... | collective-permute-start | bytes 3840008 | tf_op jit(solution)/shard_map/ppermute | solution.py:69
  1028.2 33.1 %collective-permute-start.37 = (bf16[400,1600]{1,0:T(8,128)(2,1)S(1)}, bf16[400,1600]{1,0:T(8,128)(2,1)S(1)}, u32[]{:S(2)}, u32[]{:S(2)}) collective-permute-start(bf16[400,1600]{1,0:T(8,128)(2,1)S(1)} %copy-done.49), channel_id=1, source_target_pairs={{0,8},{24,16},{1,9},{25,17},{2,10},{26,18},{3,11},{27,19},{4,12},{... | collective-permute-start | bytes 3840008 | tf_op jit(solution)/shard_map/ppermute | solution.py:69
  1035.7 21.4 %collective-permute-start.36 = (bf16[400,800]{1,0:T(8,128)(2,1)S(1)}, bf16[400,800]{1,0:T(8,128)(2,1)S(1)}, u32[]{:S(2)}, u32[]{:S(2)}) collective-permute-start(bf16[400,800]{1,0:T(8,128)(2,1)S(1)} %add_convert_fusion.15), channel_id=1, source_target_pairs={{8,16},{16,8},{9,17},{17,9},{10,18},{18,10},{11,19},{19,11},{12,20... | collective-permute-start | bytes 1920008 | tf_op jit(solution)/shard_map/ppermute | solution.py:69
  1037.7 16.7 %collective-permute-start.33 = (bf16[512,640]{1,0:T(8,128)(2,1)S(1)}, bf16[512,640]{1,0:T(8,128)(2,1)S(1)}, u32[]{:S(2)}, u32[]{:S(2)}) collective-permute-start(bf16[512,640]{1,0:T(8,128)(2,1)S(1)} %get-tuple-element.319), channel_id=1, source_target_pairs={{2,0},{3,1},{6,4},{7,5},{10,8},{11,9},{14,12},{15,13},{18,16},{19,... | collective-permute-start | bytes 1966088 | tf_op jit(solution)/shard_map/ppermute | solution.py:29
  1054.5 33.3 %collective-permute-start.49 = (bf16[800,1376]{1,0:T(8,128)(2,1)}, bf16[800,1376]{1,0:T(8,128)(2,1)}, u32[]{:S(2)}, u32[]{:S(2)}) collective-permute-start(bf16[800,1376]{1,0:T(8,128)(2,1)} %broadcast_select_fusion.1), channel_id=1, source_target_pairs={{0,4},{4,0},{1,5},{5,1},{2,6},{6,2},{3,7},{7,3},{8,12},{12,8},{9,1... | collective-permute-start | bytes 6604808 | tf_op jit(solution)/shard_map/ppermute | solution.py:33
  1072.0 72.2 %collective-permute-start.40 = (bf16[400,1600]{1,0:T(8,128)(2,1)}, bf16[400,1600]{1,0:T(8,128)(2,1)}, u32[]{:S(2)}, u32[]{:S(2)}) collective-permute-start(bf16[400,1600]{1,0:T(8,128)(2,1)} %add_convert_fusion.13), channel_id=1, source_target_pairs={{8,16},{16,8},{9,17},{17,9},{10,18},{18,10},{11,19},{19,11},{12,20... | collective-permute-start | bytes 3840008 | tf_op jit(solution)/shard_map/ppermute | solution.py:69
  1074.8 69.4 %collective-permute-start.39 = (bf16[400,800]{1,0:T(8,128)(2,1)}, bf16[400,800]{1,0:T(8,128)(2,1)}, u32[]{:S(2)}, u32[]{:S(2)}) collective-permute-start(bf16[400,800]{1,0:T(8,128)(2,1)} %add_convert_fusion.14), channel_id=1, source_target_pairs={{8,0},{16,24},{9,1},{17,25},{10,2},{18,26},{11,3},{19,27},{12,4},{... | collective-permute-start | bytes 1920008 | tf_op jit(solution)/shard_map/ppermute | solution.py:69
  1077.6 66.6 %collective-permute-start.38 = (bf16[800,800]{1,0:T(8,128)(2,1)}, bf16[800,800]{1,0:T(8,128)(2,1)}, u32[]{:S(2)}, u32[]{:S(2)}) collective-permute-start(bf16[800,800]{1,0:T(8,128)(2,1)} %add_convert_fusion.10), channel_id=1, source_target_pairs={{8,0},{16,24},{9,1},{17,25},{10,2},{18,26},{11,3},{19,27},{12,4},{... | collective-permute-start | bytes 3840008 | tf_op jit(solution)/shard_map/ppermute | solution.py:69
  1084.6 8.2 collective-permute-start.42
  1087.8 49.5 %collective-permute-start.50 = (bf16[800,1376]{1,0:T(8,128)(2,1)}, bf16[800,1376]{1,0:T(8,128)(2,1)}, u32[]{:S(2)}, u32[]{:S(2)}) collective-permute-start(bf16[800,1376]{1,0:T(8,128)(2,1)} %broadcast_select_fusion), channel_id=1, source_target_pairs={{0,4},{4,0},{1,5},{5,1},{2,6},{6,2},{3,7},{7,3},{8,12},{12,8},{9,1... | collective-permute-start | bytes 6604808 | tf_op jit(solution)/shard_map/ppermute | solution.py:33
  1099.9 187.1 %all-reduce.12.cloned.1.call-start = ((), (), s32[]{:S(2)}) async-start(), calls=%async_computation.20 | async-start | bytes 4710400 | tf_op jit(solution)/shard_map/psum | solution.py:682
  1147.3 9.2 collective-permute-start.51
  1148.6 90.7 %collective-permute-start.47 = (bf16[400,800]{1,0:T(8,128)(2,1)S(1)}, bf16[400,800]{1,0:T(8,128)(2,1)S(1)}, u32[]{:S(2)}, u32[]{:S(2)}) collective-permute-start(bf16[400,800]{1,0:T(8,128)(2,1)S(1)} %broadcast_select_fusion.29), channel_id=1, source_target_pairs={{0,4},{4,0},{1,5},{5,1},{2,6},{6,2},{3,7},{7,3},{8,12},{12,8},{9,1... | collective-permute-start | bytes 1920008 | tf_op jit(solution)/shard_map/ppermute | solution.py:33
  1151.9 89.4 %collective-permute-start.46 = (bf16[800,800]{1,0:T(8,128)(2,1)}, bf16[800,800]{1,0:T(8,128)(2,1)}, u32[]{:S(2)}, u32[]{:S(2)}) collective-permute-start(bf16[800,800]{1,0:T(8,128)(2,1)} %broadcast_select_fusion.13), channel_id=1, source_target_pairs={{0,4},{4,0},{1,5},{5,1},{2,6},{6,2},{3,7},{7,3},{8,12},{12,8},{9,1... | collective-permute-start | bytes 3840008 | tf_op jit(solution)/shard_map/ppermute | solution.py:33
  1155.1 79.9 %collective-permute-start.41 = (bf16[400,1600]{1,0:T(8,128)(2,1)}, bf16[400,1600]{1,0:T(8,128)(2,1)}, u32[]{:S(2)}, u32[]{:S(2)}) collective-permute-start(bf16[400,1600]{1,0:T(8,128)(2,1)} %add_convert_fusion.12), channel_id=1, source_target_pairs={{8,0},{16,24},{9,1},{17,25},{10,2},{18,26},{11,3},{19,27},{12,4},{... | collective-permute-start | bytes 3840008 | tf_op jit(solution)/shard_map/ppermute | solution.py:69
  1160.5 13.7 %collective-permute-start.53 = (f32[7,1024]{1,0:T(8,128)S(1)}, f32[7,1024]{1,0:T(8,128)S(1)}, u32[]{:S(2)}, u32[]{:S(2)}) collective-permute-start(f32[7,1024]{1,0:T(8,128)S(1)} %add.312), channel_id=1, source_target_pairs={{0,2},{1,3},{2,0},{3,1},{4,6},{5,7},{6,4},{7,5},{8,10},{9,11},{10,... | collective-permute-start | bytes 86024 | tf_op jit(solution)/shard_map/ppermute | solution.py:160
  1237.5 58.7 %collective-permute-start.45 = (bf16[400,1600]{1,0:T(8,128)(2,1)}, bf16[400,1600]{1,0:T(8,128)(2,1)}, u32[]{:S(2)}, u32[]{:S(2)}) collective-permute-start(bf16[400,1600]{1,0:T(8,128)(2,1)} %broadcast_select_fusion.16), channel_id=1, source_target_pairs={{0,4},{4,0},{1,5},{5,1},{2,6},{6,2},{3,7},{7,3},{8,12},{12,8},{9,1... | collective-permute-start | bytes 3840008 | tf_op jit(solution)/shard_map/ppermute | solution.py:33
  1287.0 14.4 %collective-permute-start.43 = (bf16[400,1280]{1,0:T(8,128)(2,1)}, bf16[400,1280]{1,0:T(8,128)(2,1)}, u32[]{:S(2)}, u32[]{:S(2)}) collective-permute-start(bf16[400,1280]{1,0:T(8,128)(2,1)} %get-tuple-element.280), channel_id=1, source_target_pairs={{0,4},{4,0},{1,5},{5,1},{2,6},{6,2},{3,7},{7,3},{8,12},{12,8},{9,1... | collective-permute-start | bytes 3072008 | tf_op jit(solution)/shard_map/ppermute | solution.py:33
  1287.7 7.3 collective-permute-start.54
  1299.7 12.4 collective-permute-start.44
  (96 other events, 1085.7 us)
Sparse Core Ops, SparseCore 0:
  15.7 52.5 all-gather.6
  79.7 128.3 all-gather.8
  210.6 68.8 all-gather.10
  281.7 45.6 all-gather.12
  347.1 78.0 all-gather.14
  427.0 72.1 all-gather.16
  564.6 74.5 reduce-scatter.13
  662.2 42.0 reduce-scatter.21
  708.1 65.5 reduce-scatter.17
  777.3 83.7 reduce-scatter.15
  865.0 63.9 reduce-scatter.23
  938.2 63.6 reduce-scatter.25
  1100.0 63.3 reduce-scatter.19
  1165.8 121.1 all-reduce.11
